TPU v7x, 256 devices: a whole 4x4x8 slice. The times are simulated.
256 devices in a mesh: sub: 32 (over z, y), ifc: 8 (over x, core).
Axes of the slice: x: 4, y: 4, z: 8, core: 2. Of those that a mesh axis runs over, the one named last changes fastest.
Arguments:
- gap: float32 [32, 1024, 128], P('sub', 'ifc'), may hold values from -6 to 6
- flexibility: float32 [32, 2, 1024, 2048], P('sub', None, 'ifc'), may hold values from -1 to 4, as said below
- stiffness: float32 [32, 2, 1024, 2048], P('sub', None, 'ifc'), may hold values from -1 to 4, as said below
- modes: float32 [32, 6, 2, 1024], P('sub', None, None, 'ifc'), may hold values from -1 to 1
- mode_counts: int32 [32], P('sub'), may hold values from 3 to 6
Outputs:
- multipliers: float32 [32, 1024, 128], P('sub', 'ifc')
- residual: float32 [32, 1024, 128], P('sub', 'ifc')
Inputs may be any that keep to these rules, and one draw needn't show every extreme that they name: `flexibility`: each subdomain's block, as a matrix of order 2 * 1024, is symmetric positive definite. `stiffness`: each subdomain's block, as a matrix of order 2 * 1024, is symmetric positive definite.
All inputs are finite; a program needn't handle non-finite values.
Results may differ from a plain program's by a relative error of at most 0.0003.
Values sent between devices are 32-bit elements; how exact they have to be, the bound alone decides.
No kernel may reach another device: no remote copies, remote signals or barrier semaphores. Data moves between devices by JAX's collectives and lax.ppermute only.
A program may use at most 64 MiB of HBM per device.

v0:
```python
import functools

import jax
import jax.numpy as jnp
from jax import lax
from jax.sharding import Mesh
from jax.sharding import PartitionSpec as P

IFC = ("ifc_0", "ifc_1")
SUB = ("sub_0", "sub_1")
SUB_IFC = ("sub_0", "sub_1", "ifc_0", "ifc_1")


precise = lax.Precision.HIGHEST


def shifted_2(block, axis, distance):
    devices = range(lax.axis_size(axis))
    route = [(i - distance, i) for i in devices if i - distance in devices]
    return lax.ppermute(block, axis, route)


def laid_out(pieces, dim):
    pieces = jnp.moveaxis(pieces, 0, dim)
    shape = pieces.shape
    return pieces.reshape(*shape[:dim], shape[dim] * shape[dim + 1], *shape[dim + 2 :])


def from_everyone(value, axis):
    count = lax.axis_size(axis)
    return lax.all_to_all(
        jnp.broadcast_to(value[None], (count, *value.shape)), axis, 0, 0, tiled=True
    )


def gathered_copies(value, axis, dim):
    return laid_out(from_everyone(value, axis), dim)


def one_axis_at_a_time(value, axes):
    return functools.reduce(lax.psum, axes, value)


def all_blocks(value, axes, sequence):
    pieces = value
    for k in sequence:
        pieces = lax.all_gather(pieces, axes[k])
    done = sequence[::-1]
    back = [done.index(k) for k in range(len(axes))]
    pieces = pieces.transpose(*back, *range(len(axes), pieces.ndim))
    return pieces.reshape(-1, *value.shape)


def whole_of(value, axes, sequence, dim):
    return laid_out(all_blocks(value, axes, sequence), dim)


def taken_together(value, axis):
    return from_everyone(value, axis).sum(axis=0)


def assemble(own_blocks, next_blocks, off_blocks):
    subs_count = own_blocks.shape[0]
    mode_count = own_blocks.shape[1]
    shifted = jnp.concatenate(
        [jnp.zeros((1, mode_count, mode_count), jnp.float32), next_blocks[:-1]], 0
    )
    diag_blocks = own_blocks + shifted
    ident = jnp.eye(subs_count, dtype=jnp.float32)
    upper = jnp.eye(subs_count, k=1, dtype=jnp.float32)
    whole = jnp.einsum("st,sij->sitj", ident, diag_blocks, precision=precise)
    whole = whole + jnp.einsum("st,sij->sitj", upper, off_blocks, precision=precise)
    whole = whole + jnp.einsum("st,sij->tjsi", upper, off_blocks, precision=precise)
    return whole.reshape(subs_count * mode_count, subs_count * mode_count)


def coarse_solve(factor, rhs_matrix):
    forward = lax.linalg.triangular_solve(factor, rhs_matrix, left_side=True, lower=True)
    return lax.linalg.triangular_solve(
        factor, forward, left_side=True, lower=True, transpose_a=True
    )


def apply_jump(matrix, vector, edge_live):
    own_rows = vector.shape[0]
    face_len = own_rows * lax.axis_size(IFC)
    block_rows = matrix[0].reshape(2, own_rows, 2, face_len)
    before = shifted_2(vector, SUB, 1)
    traces = jnp.stack([-before, vector], 0)
    image = jnp.einsum(
        "aibj,bjk->aik", block_rows, gathered_copies(traces, IFC, 1), precision=precise
    )
    after = shifted_2(image[0], SUB, -1)
    return (image[1] - after) * edge_live


def inner(first_vec, second_vec):
    return one_axis_at_a_time(jnp.sum(first_vec * second_vec, axis=0), SUB_IFC)


def per_device(gap, flexibility, stiffness, modes, mode_counts):
    subs_count = lax.axis_size(SUB)
    lanes = lax.axis_size(IFC)
    sub_index = lax.axis_index(SUB)
    edge_live = (sub_index < subs_count - 1).astype(jnp.float32)
    first_lane = (lax.axis_index(IFC) == 0).astype(jnp.float32)
    mode_count = modes.shape[1]
    load_count = gap.shape[2]
    active = (jnp.arange(mode_count) < mode_counts[0]).astype(jnp.float32)
    mode_right = modes[0, :, 1] * active[:, None] * edge_live
    mode_next = shifted_2(modes[0, :, 0] * active[:, None], SUB, -1)
    own_blocks = jnp.dot(mode_right, mode_right.T, precision=precise)
    own_blocks = (
        own_blocks + jnp.eye(mode_count, dtype=jnp.float32) * (1.0 - active)[:, None] * first_lane
    )
    next_blocks = jnp.dot(mode_next, mode_next.T, precision=precise)
    off_blocks = -jnp.dot(mode_right, mode_next.T, precision=precise)
    partial_blocks = jnp.stack([own_blocks, next_blocks, off_blocks], 0)
    gathered = whole_of(partial_blocks[None], SUB_IFC, (1, 0, 2, 3), 0)
    gathered = gathered.reshape(subs_count, lanes, 3, mode_count, mode_count).sum(1)
    factor = jnp.linalg.cholesky(assemble(gathered[:, 0], gathered[:, 1], gathered[:, 2]))

    def project(vector):
        own_part = jnp.dot(mode_right, vector, precision=precise)
        next_part = -jnp.dot(mode_next, vector, precision=precise)
        partial_terms = jnp.stack([own_part, next_part], 0)
        summed = taken_together(partial_terms, IFC)
        all_partials = gathered_copies(summed[None], SUB, 0)
        coarse_rhs = all_partials[:, 0] + jnp.concatenate(
            [jnp.zeros((1, mode_count, load_count), jnp.float32), all_partials[:-1, 1]], 0
        )
        weights = coarse_solve(
            factor, coarse_rhs.reshape(subs_count * mode_count, load_count)
        ).reshape(subs_count, mode_count, load_count)
        weight_own = lax.dynamic_index_in_dim(weights, sub_index, 0, keepdims=False)
        weight_next = lax.dynamic_index_in_dim(
            weights, jnp.minimum(sub_index + 1, subs_count - 1), 0, keepdims=False
        )
        correction = jnp.dot(mode_right.T, weight_own, precision=precise) - jnp.dot(
            mode_next.T, weight_next, precision=precise
        )
        return vector - correction

    residual = project(gap[0] * edge_live)
    search = project(0.25 * apply_jump(stiffness, residual, edge_live))
    rz_now = inner(residual, search)
    image = project(apply_jump(flexibility, search, edge_live))
    step_size = rz_now / inner(search, image)
    multipliers = step_size * search
    residual = residual - step_size * image
    return (multipliers[None], residual[None])


def solution(mesh):
    finer = Mesh(mesh.devices.reshape(8, 4, 4, 2), ("sub_0", "sub_1", "ifc_0", "ifc_1"))
    return jax.shard_map(
        per_device,
        mesh=finer,
        in_specs=(
            P(SUB, IFC, None),
            P(SUB, None, IFC, None),
            P(SUB, None, IFC, None),
            P(SUB, None, None, IFC),
            P(SUB),
        ),
        out_specs=(P(SUB, IFC, None), P(SUB, IFC, None)),
        check_vma=False,
    )
```

profile of v0, /device:TPU:1, one launch (start us, length us, event | category | flops | bytes accessed | tf_op | source)
XLA Modules:
  0.0 330.0 jit_solution(696620062887227667)
XLA Ops:
  4.8 2.4 collective-permute-done
  7.5 11.4 %all-gather = f32[12,6,6]{2,1,0:T(8,128)S(1)} all-gather(f32[3,6,6]{2,1,0:T(8,128)S(1)} %pad_maximum_fusion.6), channel_id=2, replica_groups=mesh['sub_0'=8,'sub_1'=4,'ifc_0'=4,'ifc_1'=2] {'sub_1'}, dimensions={0}, use_global_device_ids=true | all-gather | bytes 2160 | tf_op jit(solution)/shard_map/all_gather | solution.py:47
  18.9 22.1 %all-gather.1 = f32[32,1,3,6,6]{4,1,3,2,0:T(1,128)S(1)} all-gather(f32[4,1,3,6,6]{4,1,3,2,0:T(1,128)S(1)} %copy.44), channel_id=3, replica_groups=mesh['sub_0'=8,'sub_1'=4,'ifc_0'=4,'ifc_1'=2] {'sub_0'}, dimensions={0}, use_global_device_ids=true | all-gather | bytes 15552 | tf_op jit(solution)/shard_map/all_gather | solution.py:47
  41.1 11.7 %all-gather.2 = f32[32,4,1,3,6,6]{5,1,4,3,2,0:T(4,128)S(1)} all-gather(f32[8,4,1,3,6,6]{5,1,4,3,2,0:T(4,128)S(1)} %copy.45), channel_id=4, replica_groups=mesh['sub_0'=8,'sub_1'=4,'ifc_0'=4,'ifc_1'=2] {'ifc_0'}, dimensions={0}, use_global_device_ids=true | all-gather | bytes 69120 | tf_op jit(solution)/shard_map/all_gather | solution.py:47
  54.8 16.3 %all-gather.3 = f32[8,8,4,1,3,6,6]{1,2,6,5,4,3,0:T(4,128)S(1)} all-gather(f32[4,8,4,1,3,6,6]{1,2,6,5,4,3,0:T(4,128)S(1)} %copy.46), channel_id=5, replica_groups=mesh['sub_0'=8,'sub_1'=4,'ifc_0'=4,'ifc_1'=2] {'ifc_1'}, dimensions={0}, use_global_device_ids=true | all-gather | bytes 165888 | tf_op jit(solution)/shard_map/all_gather | solution.py:47
  72.9 2.2 fusion
  75.1 9.6 %copy.51 = f32[32,6,32,6]{3,2,1,0:T(8,128)S(1)} copy(f32[32,6,32,6]{1,0,3,2:T(8,128)} %fusion) | data formatting | bytes 294912 | tf_op jit(solution)/shard_map/add | solution.py:72
  86.9 4.1 %reshape.143 = f32[192,192]{1,0:T(8,128)S(1)} reshape(f32[32,6,32,6]{3,2,1,0:T(8,128)} %fusion.1) | data formatting | bytes 294912 | tf_op jit(solution)/shard_map/reshape | solution.py:74
  91.1 11.7 %cholesky.51 = f32[128,128]{1,0:T(8,128)S(1)} custom-call(f32[128,128]{1,0:T(8,128)S(1)} %cholesky.124), custom_call_target="Cholesky" | custom-call | tf_op jit(solution)/shard_map/jit(cholesky)/cholesky | solution.py:121
  102.9 9.8 %custom-call.17 = f32[1,128,128]{1,2,0:T(8,128)S(1)} custom-call(f32[1,128,128]{2,1,0:T(8,128)S(1)} %get-tuple-element.79), custom_call_target="InvertDiagBlocksLowerTriangular" | custom-call | tf_op jit(solution)/shard_map/jit(cholesky)/cholesky | solution.py:121
  113.1 5.8 %cholesky.110 = f32[64,64]{1,0:T(8,128)S(1)} custom-call(f32[64,64]{1,0:T(8,128)S(1)} %convolution_subtract_fusion.9), custom_call_target="Cholesky" | custom-call | tf_op jit(solution)/shard_map/jit(cholesky)/cholesky | solution.py:121
  121.2 4.1 %all-to-all-start = ((f32[8,2,6,128]{3,1,2,0:T(2,128)}), f32[8,2,6,128]{3,1,2,0:T(2,128)S(1)}, u32[]{:S(2)}, u32[]{:S(2)}) async-start(f32[8,2,6,128]{3,1,2,0:T(2,128)} %broadcast_in_dim.22), calls=%async_computation | async-start | bytes 98304 | tf_op jit(solution)/shard_map/all_to_all | solution.py:31
  126.6 3.4 %all-to-all-done = f32[8,2,6,128]{3,1,2,0:T(2,128)S(1)} async-done(((f32[8,2,6,128]{3,1,2,0:T(2,128)}), f32[8,2,6,128]{3,1,2,0:T(2,128)S(1)}, u32[]{:S(2)}, u32[]{:S(2)}) %all-to-all-start) | async-done | bytes 49184 | tf_op jit(solution)/shard_map/all_to_all | solution.py:31
  130.8 7.5 %all-to-all-start.1 = ((f32[32,1,2,6,128]{4,2,3,1,0:T(2,128)}), f32[32,1,2,6,128]{4,2,3,1,0:T(2,128)S(1)}, u32[]{:S(2)}, u32[]{:S(2)}) async-start(f32[32,1,2,6,128]{4,2,3,1,0:T(2,128)} %broadcast_in_dim.23), calls=%async_computation.1 | async-start | bytes 393216 | tf_op jit(solution)/shard_map/all_to_all | solution.py:31
  138.4 19.7 %custom-call.23 = f32[2,128,128]{1,2,0:T(8,128)S(1)} custom-call(f32[2,128,128]{2,1,0:T(8,128)S(1)} %pad_maximum_fusion), custom_call_target="InvertDiagBlocksLowerTriangular" | custom-call | tf_op jit(solution)/shard_map/triangular_solve/custom-call.4 | solution.py:79
  160.4 3.1 collective-permute-start.1
  166.0 5.6 %all-to-all-start.2 = ((f32[8,2,128,128]{3,2,1,0:T(8,128)}), f32[8,2,128,128]{3,2,1,0:T(8,128)S(1)}, u32[]{:S(2)}, u32[]{:S(2)}) async-start(f32[8,2,128,128]{3,2,1,0:T(8,128)} %broadcast_in_dim.24), calls=%async_computation.2 | async-start | bytes 2097152 | tf_op jit(solution)/shard_map/all_to_all | solution.py:31
  171.6 3.0 reshape_squeeze.6
  174.6 12.0 %all-to-all-done.2 = f32[8,2,128,128]{3,2,1,0:T(8,128)S(1)} async-done(((f32[8,2,128,128]{3,2,1,0:T(8,128)}), f32[8,2,128,128]{3,2,1,0:T(8,128)S(1)}, u32[]{:S(2)}, u32[]{:S(2)}) %all-to-all-start.2) | async-done | bytes 1048608 | tf_op jit(solution)/shard_map/all_to_all | solution.py:31
  190.2 4.3 %collective-permute-done.2 = f32[128,128]{1,0:T(8,128)S(1)} collective-permute-done((f32[128,128]{1,0:T(8,128)S(1)}, f32[128,128]{1,0:T(8,128)S(1)}, u32[]{:S(2)}, u32[]{:S(2)}) %collective-permute-start.2) | collective-permute-done | bytes 65568 | tf_op jit(solution)/shard_map/ppermute | solution.py:20
  195.0 9.0 %all_to_all.40 = f32[8,2,6,128]{3,1,2,0:T(2,128)S(1)} all-to-all(f32[8,2,6,128]{3,1,2,0:T(2,128)S(1)} %broadcast_in_dim.25), channel_id=1, replica_groups=mesh['sub_0'=8,'sub_1'=4,'ifc_0'=4,'ifc_1'=2] {'ifc_0','ifc_1'}, dimensions={0} | all-to-all | bytes 98304 | tf_op jit(solution)/shard_map/all_to_all | solution.py:31
  204.0 21.4 %all_to_all.41 = f32[32,1,2,6,128]{4,2,3,1,0:T(2,128)S(1)} all-to-all(f32[32,1,2,6,128]{4,2,3,1,0:T(2,128)S(1)} %broadcast_in_dim.26), channel_id=1, replica_groups=mesh['sub_0'=8,'sub_1'=4,'ifc_0'=4,'ifc_1'=2] {'sub_0','sub_1'}, dimensions={0} | all-to-all | bytes 393216 | tf_op jit(solution)/shard_map/all_to_all | solution.py:31
  232.0 6.5 %all-to-all-start.5 = ((f32[8,2,128,128]{3,2,1,0:T(8,128)}), f32[8,2,128,128]{3,2,1,0:T(8,128)S(1)}, u32[]{:S(2)}, u32[]{:S(2)}) async-start(f32[8,2,128,128]{3,2,1,0:T(8,128)} %broadcast_in_dim.27), calls=%async_computation.5 | async-start | bytes 2097152 | tf_op jit(solution)/shard_map/all_to_all | solution.py:31
  238.6 3.0 reshape_squeeze.7
  241.6 12.0 %all-to-all-done.5 = f32[8,2,128,128]{3,2,1,0:T(8,128)S(1)} async-done(((f32[8,2,128,128]{3,2,1,0:T(8,128)}), f32[8,2,128,128]{3,2,1,0:T(8,128)S(1)}, u32[]{:S(2)}, u32[]{:S(2)}) %all-to-all-start.5) | async-done | bytes 1048608 | tf_op jit(solution)/shard_map/all_to_all | solution.py:31
  257.2 4.3 %collective-permute-done.4 = f32[128,128]{1,0:T(8,128)S(1)} collective-permute-done((f32[128,128]{1,0:T(8,128)S(1)}, f32[128,128]{1,0:T(8,128)S(1)}, u32[]{:S(2)}, u32[]{:S(2)}) %collective-permute-start.4) | collective-permute-done | bytes 65568 | tf_op jit(solution)/shard_map/ppermute | solution.py:20
  262.0 9.0 %all_to_all.42 = f32[8,2,6,128]{3,1,2,0:T(2,128)S(1)} all-to-all(f32[8,2,6,128]{3,1,2,0:T(2,128)S(1)} %broadcast_in_dim.28), channel_id=1, replica_groups=mesh['sub_0'=8,'sub_1'=4,'ifc_0'=4,'ifc_1'=2] {'ifc_0','ifc_1'}, dimensions={0} | all-to-all | bytes 98304 | tf_op jit(solution)/shard_map/all_to_all | solution.py:31
  271.0 18.4 %all_to_all.43 = f32[32,1,2,6,128]{4,2,3,1,0:T(2,128)S(1)} all-to-all(f32[32,1,2,6,128]{4,2,3,1,0:T(2,128)S(1)} %broadcast_in_dim.29), channel_id=1, replica_groups=mesh['sub_0'=8,'sub_1'=4,'ifc_0'=4,'ifc_1'=2] {'sub_0','sub_1'}, dimensions={0} | all-to-all | bytes 393216 | tf_op jit(solution)/shard_map/all_to_all | solution.py:31
  291.8 11.6 %all-reduce.9 = (f32[128]{0:T(128)S(1)}, f32[128]{0:T(128)S(1)}) all-reduce(f32[128]{0:T(128)S(1)} %get-tuple-element.69, f32[128]{0:T(128)S(1)} %get-tuple-element.68), channel_id=1, replica_groups=mesh['sub_0'=8,'sub_1'=4,'ifc_0'=4,'ifc_1'=2] {'sub_0'}, use_global_device_ids=true, to_apply=%region_8.0 | all-reduce | flops 256 | bytes 2048 | tf_op jit(solution)/shard_map/psum | solution.py:41
  303.3 7.0 %all-reduce.11 = (f32[128]{0:T(128)S(1)}, f32[128]{0:T(128)S(1)}) all-reduce(f32[128]{0:T(128)S(1)} %get-tuple-element.70, f32[128]{0:T(128)S(1)} %get-tuple-element.71), channel_id=1, replica_groups=mesh['sub_0'=8,'sub_1'=4,'ifc_0'=4,'ifc_1'=2] {'sub_1'}, use_global_device_ids=true, to_apply=%region_9.0 | all-reduce | flops 256 | bytes 2048 | tf_op jit(solution)/shard_map/psum | solution.py:41
  310.3 6.9 %all-reduce.10 = (f32[128]{0:T(128)S(1)}, f32[128]{0:T(128)S(1)}) all-reduce(f32[128]{0:T(128)S(1)} %get-tuple-element.74, f32[128]{0:T(128)S(1)} %get-tuple-element.75), channel_id=1, replica_groups=mesh['sub_0'=8,'sub_1'=4,'ifc_0'=4,'ifc_1'=2] {'ifc_0'}, use_global_device_ids=true, to_apply=%region_10.0 | all-reduce | flops 256 | bytes 2048 | tf_op jit(solution)/shard_map/psum | solution.py:41
  317.2 12.2 %all-reduce.12 = (f32[128]{0:T(128)S(1)}, f32[128]{0:T(128)S(1)}) all-reduce(f32[128]{0:T(128)S(1)} %get-tuple-element.72, f32[128]{0:T(128)S(1)} %get-tuple-element.73), channel_id=1, replica_groups=mesh['sub_0'=8,'sub_1'=4,'ifc_0'=4,'ifc_1'=2] {'ifc_1'}, use_global_device_ids=true, to_apply=%region_11.0 | all-reduce | flops 256 | bytes 2048 | tf_op jit(solution)/shard_map/psum | solution.py:41
  (133 shorter events, 35.5 us)
Async XLA Ops:
  2.1 5.0 %collective-permute-start = (f32[6,128]{1,0:T(8,128)S(1)}, f32[6,128]{1,0:T(8,128)S(1)}, u32[]{:S(2)}, u32[]{:S(2)}) collective-permute-start(f32[6,128]{1,0:T(8,128)S(1)} %fusion.67), channel_id=1, source_target_pairs={{8,0},{16,8},{24,16},{32,24},{40,32},{48,40},{56,48},{64,56},{72,6... | collective-permute-start | bytes 9224 | tf_op jit(solution)/shard_map/ppermute | solution.py:20
  86.9 33.4 %copy-start.2 = (f32[1,128,128]{2,1,0:T(8,128)S(1)}, f32[1,128,128]{2,1,0:T(8,128)}, u32[]{:S(2)}) copy-start(f32[1,128,128]{2,1,0:T(8,128)} %param.9) | copy-start | bytes 196612
  121.2 8.8 %all-to-all-start = ((f32[8,2,6,128]{3,1,2,0:T(2,128)}), f32[8,2,6,128]{3,1,2,0:T(2,128)S(1)}, u32[]{:S(2)}, u32[]{:S(2)}) async-start(f32[8,2,6,128]{3,1,2,0:T(2,128)} %broadcast_in_dim.22), calls=%async_computation | async-start | bytes 98304 | tf_op jit(solution)/shard_map/all_to_all | solution.py:31
  130.8 27.4 %all-to-all-start.1 = ((f32[32,1,2,6,128]{4,2,3,1,0:T(2,128)}), f32[32,1,2,6,128]{4,2,3,1,0:T(2,128)S(1)}, u32[]{:S(2)}, u32[]{:S(2)}) async-start(f32[32,1,2,6,128]{4,2,3,1,0:T(2,128)} %broadcast_in_dim.23), calls=%async_computation.1 | async-start | bytes 393216 | tf_op jit(solution)/shard_map/all_to_all | solution.py:31
  160.4 4.5 %collective-permute-start.1 = (f32[128,128]{1,0:T(8,128)S(1)}, f32[128,128]{1,0:T(8,128)S(1)}, u32[]{:S(2)}, u32[]{:S(2)}) collective-permute-start(f32[128,128]{1,0:T(8,128)S(1)} %fusion.14), channel_id=1, source_target_pairs={{0,8},{8,16},{16,24},{24,32},{32,40},{40,48},{48,56},{56,64},{64,7... | collective-permute-start | bytes 196616 | tf_op jit(solution)/shard_map/ppermute | solution.py:20
  166.0 20.6 %all-to-all-start.2 = ((f32[8,2,128,128]{3,2,1,0:T(8,128)}), f32[8,2,128,128]{3,2,1,0:T(8,128)S(1)}, u32[]{:S(2)}, u32[]{:S(2)}) async-start(f32[8,2,128,128]{3,2,1,0:T(8,128)} %broadcast_in_dim.24), calls=%async_computation.2 | async-start | bytes 2097152 | tf_op jit(solution)/shard_map/all_to_all | solution.py:31
  188.9 5.6 %collective-permute-start.2 = (f32[128,128]{1,0:T(8,128)S(1)}, f32[128,128]{1,0:T(8,128)S(1)}, u32[]{:S(2)}, u32[]{:S(2)}) collective-permute-start(f32[128,128]{1,0:T(8,128)S(1)} %slice_bitcast_fusion.11), channel_id=1, source_target_pairs={{8,0},{16,8},{24,16},{32,24},{40,32},{48,40},{56,48},{64,56},{72,6... | collective-permute-start | bytes 196616 | tf_op jit(solution)/shard_map/ppermute | solution.py:20
  227.7 4.3 %copy-start = (f32[128,128]{1,0:T(8,128)}, f32[128,128]{1,0:T(8,128)S(1)}, u32[]{:S(2)}) copy-start(f32[128,128]{1,0:T(8,128)S(1)} %fusion.13) | copy-start | bytes 196612
  227.7 3.2 collective-permute-start.3
  232.0 21.5 %all-to-all-start.5 = ((f32[8,2,128,128]{3,2,1,0:T(8,128)}), f32[8,2,128,128]{3,2,1,0:T(8,128)S(1)}, u32[]{:S(2)}, u32[]{:S(2)}) async-start(f32[8,2,128,128]{3,2,1,0:T(8,128)} %broadcast_in_dim.27), calls=%async_computation.5 | async-start | bytes 2097152 | tf_op jit(solution)/shard_map/all_to_all | solution.py:31
  253.6 37.8 %copy-start.1 = (f32[128,128]{1,0:T(8,128)S(1)}, f32[128,128]{1,0:T(8,128)}, u32[]{:S(2)}) copy-start(f32[128,128]{1,0:T(8,128)} %copy-done) | copy-start | bytes 196612
  255.9 5.6 %collective-permute-start.4 = (f32[128,128]{1,0:T(8,128)S(1)}, f32[128,128]{1,0:T(8,128)S(1)}, u32[]{:S(2)}, u32[]{:S(2)}) collective-permute-start(f32[128,128]{1,0:T(8,128)S(1)} %slice_bitcast_fusion.9), channel_id=1, source_target_pairs={{8,0},{16,8},{24,16},{32,24},{40,32},{48,40},{56,48},{64,56},{72,6... | collective-permute-start | bytes 196616 | tf_op jit(solution)/shard_map/ppermute | solution.py:20
where the time goes:
time: 331 us; the launch traced here: 330 us
  blocking collectives  157 us (47%)
  other arithmetic  54.5 us (16%)
  waiting for transfers between devices  41 us (12%)
  starting transfers between devices  32.7 us (10%)
  local copies, waits for them, and re-layouts  28.2 us (9%)
  matrix products  13.3 us (4%)
  between operations  3.45 us (1%)
    all_gather x4, blocking collectives, all_blocks(): pieces = lax.all_gather(pieces, axes[k])  61.5 us
    all_to_all x4, blocking collectives, from_everyone(): lax.all_to_all(jnp.broadcast_to(value[None], (count, *value.shape)), axis...  57.8 us
    psum x4, blocking collectives, one_axis_at_a_time(): return functools.reduce(lax.psum, axes, value)  37.6 us
    another operation x7, other arithmetic, per_device(): jnp.linalg.cholesky(assemble(gathered[:, 0], gathered[:, 1], gathered[:,...  28.8 us
    all_to_all x4, waiting for transfers between devices, from_everyone(): lax.all_to_all(jnp.broadcast_to(value[None], (count, *value.shape)), axis...  27.3 us
    all_to_all x4, starting transfers between devices, from_everyone(): lax.all_to_all(jnp.broadcast_to(value[None], (count, *value.shape)), axis...  23.8 us
    another operation x9, other arithmetic, coarse_solve(): lax.linalg.triangular_solve(factor, forward, left_side=True, lower=True,...  19.8 us
    ppermute x5, waiting for transfers between devices, shifted_2(): return lax.ppermute(block, axis, route)  13.6 us
  transfers between devices with their start and end apart: 9, of which 8 were waited for; matrix products, arithmetic and copies ran while one was open for 8% of the time, Pallas kernels for 0%

commit v1 on v0

v1 whole, which is shorter than its diff:
```python
import jax
import jax.numpy as jnp
from jax import lax
from jax.experimental import pallas as pl
from jax.experimental.pallas import tpu as pltpu
from jax.sharding import Mesh
from jax.sharding import PartitionSpec as P

SUB = ("z", "y")
IFC = ("x", "c")
HIGH = lax.Precision.HIGHEST
PAD = 8


def dot(a, b):
    return jnp.dot(a, b, precision=HIGH, preferred_element_type=jnp.float32)


def dot_nt(a, b):
    return lax.dot_general(
        a, b, (((1,), (1,)), ((), ())), precision=HIGH, preferred_element_type=jnp.float32
    )


def inverse_kernel(subs, modes, m_ref, out_ref, cols_ref):
    lanes = 128
    for i in range(PAD):
        rows = m_ref[pl.ds(i, subs, stride=PAD), :]
        turned = jnp.concatenate([rows] * (lanes // subs), axis=0).T
        cols_ref[pl.ds(i, 3 * PAD, stride=PAD), :] = turned[: 3 * PAD]

    def column(b, j):
        start = (b * PAD + j) * PAD
        return cols_ref[start : start + PAD, :]

    sublane = lax.broadcasted_iota(jnp.int32, (PAD, lanes), 0)
    lane = lax.broadcasted_iota(jnp.int32, (PAD, lanes), 1)
    lane_mode = lane // subs
    row_sub = lax.broadcasted_iota(jnp.int32, (subs, lanes), 0)
    lane_sub = lax.broadcasted_iota(jnp.int32, (subs, lanes), 1) % subs

    def inverse(a):
        a = list(a)
        for k in range(modes):
            pivot = 1.0 / a[k][k : k + 1, :]
            is_k = sublane == k
            for j in range(modes):
                if j != k:
                    scaled = a[j][k : k + 1, :] * pivot
                    a[j] = jnp.where(is_k, scaled, a[j] - a[k] * scaled)
            a[k] = jnp.where(is_k, pivot, -a[k] * pivot)
        return a

    def product(a, b):
        out = []
        for j in range(modes):
            total = a[0] * b[j][0:1, :]
            for k in range(1, modes):
                total = total + a[k] * b[j][k : k + 1, :]
            out.append(total)
        return out

    def moved(a, shift):
        return [pltpu.roll(x, shift % lanes, 1) for x in a]

    def dense(parts):
        halves = []
        for half in range(2):
            rows_of = []
            for a, shift in parts:
                chosen = jnp.zeros((PAD, lanes), jnp.float32)
                for q in range(lanes // subs):
                    k = half * (lanes // subs) + q
                    if k < modes:
                        chosen = jnp.where(lane_mode == q, a[k], chosen)
                rows_of.append((chosen, row_sub == lane_sub + shift))
            strips = []
            for i in range(PAD):
                strip = jnp.zeros((subs, lanes), jnp.float32)
                for chosen, mask in rows_of:
                    strip = jnp.where(mask, chosen[i : i + 1, :], strip)
                strips.append(strip)
            halves.append(jnp.concatenate(strips, axis=0))
        return jnp.concatenate(halves, axis=1)

    lower = [column(0, j) for j in range(modes)]
    diag = [column(1, j) for j in range(modes)]
    upper = [column(2, j) for j in range(modes)]
    ident = [jnp.where(sublane == k, 1.0, 0.0) for k in range(modes)]
    total = None
    h = 1
    while h < subs:
        inv = inverse(diag)
        alpha = product(lower, moved(inv, h))
        gamma = product(upper, moved(inv, -h))
        upper_before, lower_before = moved(upper, h), moved(lower, h)
        upper_after, lower_after = moved(upper, -h), moved(lower, -h)
        first = product(alpha, upper_before)
        second = product(gamma, lower_after)
        diag = [d - f - g for d, f, g in zip(diag, first, second)]
        lower = [-x for x in product(alpha, lower_before)]
        upper = [-x for x in product(gamma, upper_after)]
        step = dense(
            [
                (ident, 0),
                ([-x for x in moved(alpha, -h)], h),
                ([-x for x in moved(gamma, h)], -h),
            ]
        )
        total = step if total is None else dot(step, total)
        h *= 2
    out_ref[...] = dot(dense([(inverse(diag), 0)]), total)


def coarse_inverse(rows, subs, modes):
    size = subs * PAD
    return pl.pallas_call(
        lambda *refs: inverse_kernel(subs, modes, *refs),
        out_shape=jax.ShapeDtypeStruct((size, size), jnp.float32),
        in_specs=[pl.BlockSpec(memory_space=pltpu.VMEM)],
        out_specs=pl.BlockSpec(memory_space=pltpu.VMEM),
        scratch_shapes=[pltpu.VMEM((3 * PAD * PAD, 128), jnp.float32)],
        name="coarse_inverse",
    )(rows)


def moved_along(block, distance):
    n = lax.axis_size(SUB)
    return lax.ppermute(
        block, SUB, [(i - distance, i) for i in range(n) if 0 <= i - distance < n]
    )


def core_swap(block):
    return lax.ppermute(block, "c", [(0, 1), (1, 0)])


def from_all(value, axis):
    count = lax.axis_size(axis)
    return lax.all_to_all(
        jnp.broadcast_to(value[None], (count, *value.shape)), axis, 0, 0, tiled=True
    )


def gathered(piece):
    own = from_all(piece, "x")
    other = core_swap(own)
    on_first = lax.axis_index("c") == 0
    return jnp.stack([jnp.where(on_first, own, other), jnp.where(on_first, other, own)], 1)


def per_device(gap, flexibility, stiffness, modes, mode_counts):
    subs = lax.axis_size(SUB)
    sub = lax.axis_index(SUB)
    rows, loads = gap.shape[1], gap.shape[2]
    lanes = lax.axis_size(IFC)
    face = rows * lanes
    mode_count = modes.shape[1]
    live = (sub < subs - 1).astype(jnp.float32)
    inner = (sub > 0).astype(jnp.float32)
    flex = flexibility.reshape(2 * rows, 2 * face)
    stiff = stiffness.reshape(2 * rows, 2 * face)

    active = (jnp.arange(PAD) < jnp.minimum(mode_counts[0], mode_count)).astype(jnp.float32)
    padded = jnp.pad(modes[0], ((0, PAD - mode_count), (0, 0), (0, 0))) * active[:, None, None]
    left, right = padded[:, 0], padded[:, 1] * live
    field = gap[0] * live

    from_before = moved_along(jnp.concatenate([field, right], 0), 1)
    left_after = moved_along(left, -1)
    field_before, right_before = from_before[:rows], from_before[rows:]
    piece = jnp.concatenate(
        [-field_before, field, -right_before, left * inner, right, -left_after], 0
    )
    whole = gathered(piece)

    def traces_of(pieces):
        pieces = pieces.reshape(lanes, 2, rows, loads)
        return pieces.transpose(1, 0, 2, 3).reshape(2 * face, loads)

    gap_traces = traces_of(whole[:, :, : 2 * rows])
    faces = whole[:, :, 2 * rows :].reshape(lanes, 4, PAD, rows)
    faces = faces.transpose(1, 2, 0, 3).reshape(4, PAD, face)
    none = jnp.zeros((PAD, face), jnp.float32)
    basis = jnp.concatenate(
        [
            jnp.concatenate([faces[0], faces[1], none], 0),
            jnp.concatenate([none, faces[2], faces[3]], 0),
        ],
        1,
    )
    own_basis = jnp.concatenate(
        [
            jnp.concatenate([-right_before, left * inner, jnp.zeros_like(left)], 0),
            jnp.concatenate([jnp.zeros_like(left), right, -left_after], 0),
        ],
        1,
    )
    here = basis[PAD : 2 * PAD]

    rest = jnp.pad(
        jnp.eye(PAD, dtype=jnp.float32) * (1.0 - active)[:, None], ((0, 0), (PAD, PAD))
    )
    blocks = dot_nt(here, basis) + rest
    rhs = dot(here, gap_traces)
    sent = jnp.concatenate([rhs, jnp.pad(blocks, ((0, 0), (0, 128 - 3 * PAD)))], 0)
    first = from_all(sent, SUB)
    inverse = coarse_inverse(first[:, PAD:].reshape(subs * PAD, 128), subs, mode_count)
    near = jnp.pad(inverse.reshape(PAD, subs, PAD * subs), ((0, 0), (1, 1), (0, 0)))
    near = lax.dynamic_slice_in_dim(near, sub, 3, 1)
    near = near.transpose(1, 0, 2).reshape(3 * PAD, PAD * subs)

    def weights_of(all_rhs):
        return dot(near, all_rhs.transpose(1, 0, 2).reshape(PAD * subs, loads))

    def spread(part, weights):
        return lax.dot_general(
            part, weights, (((0,), (0,)), ((), ())), precision=HIGH,
            preferred_element_type=jnp.float32,
        )

    weights = weights_of(first[:, :PAD])
    res_traces = gap_traces - spread(basis, weights)
    own_res = field - spread(own_basis[:, rows:], weights)

    image = 0.25 * dot(stiff, res_traces)
    before = moved_along(image[rows:], 1)
    after = moved_along(image[:rows], -1)
    own_search = (image[rows:] - after) * live
    before_search = (before - image[:rows]) * inner
    own_traces = jnp.concatenate([-before_search, own_search], 0)
    search_traces = traces_of(gathered(own_traces))
    second = from_all(dot(here, search_traces), SUB)
    pre_image = dot(flex, search_traces)
    flex_basis = dot_nt(flex, basis)
    weights = weights_of(second)
    image = pre_image - dot(flex_basis, weights)
    direction = own_traces - spread(own_basis, weights)

    after = moved_along(image[:rows], -1)
    sums = jnp.stack(
        [jnp.sum(own_res * own_search, 0), jnp.sum(direction * image, 0)], 0
    )
    partial = jnp.concatenate([dot(own_basis, image), jnp.pad(sums, ((0, PAD - 2), (0, 0)))], 0)
    partial = partial + core_swap(partial)
    partial = from_all(partial, "x").sum(0)
    third = from_all(partial, SUB)
    totals = third[:, 3 * PAD :].sum(0)
    parts = third[:, : 3 * PAD].reshape(subs, 3, PAD, loads)
    none = jnp.zeros((1, PAD, loads), jnp.float32)
    all_rhs = (
        parts[:, 1]
        + jnp.concatenate([parts[1:, 0], none], 0)
        + jnp.concatenate([none, parts[:-1, 2]], 0)
    )
    weights = weights_of(all_rhs)
    step = totals[0] / totals[1]
    own_image = (image[rows:] - after) * live - spread(own_basis[:, rows:], weights)
    return (step * direction[rows:])[None], (own_res - step * own_image)[None]


def solution(mesh):
    finer = Mesh(mesh.devices.reshape(8, 4, 4, 2), ("z", "y", "x", "c"))
    return jax.shard_map(
        per_device,
        mesh=finer,
        in_specs=(
            P(SUB, IFC, None),
            P(SUB, None, IFC, None),
            P(SUB, None, IFC, None),
            P(SUB, None, None, IFC),
            P(SUB),
        ),
        out_specs=(P(SUB, IFC, None), P(SUB, IFC, None)),
        check_vma=False,
    )
```

time: 331 us -> 155 us (0.47)
  blocking collectives: 157 us -> 28.3 us
  other arithmetic: 54.5 us -> 1.74 us
  local copies, waits for them, and re-layouts: 28.2 us -> 12.8 us
  starting transfers between devices: 32.7 us -> 47.9 us
  Pallas kernels: 0 us -> 4.75 us
    all_gather x4 -> x0, blocking collectives: 61.5 us -> none  [all_blocks(): pieces = lax.all_gather(pieces, axes[k])]
    another operation x25 -> x6, other arithmetic: 48.7 us -> 1.39 us  [the longest x5 1.38 us: gathered(): jnp.stack([jnp.where(on_first, own, other), jnp.where(on_first, other, ow...]
    psum x4 -> x0, blocking collectives: 37.6 us -> none  [one_axis_at_a_time(): return functools.reduce(lax.psum, axes, value)]
    all_to_all x4 -> x3, blocking collectives: 57.8 us -> 28.3 us  [from_all(): lax.all_to_all(jnp.broadcast_to(value[None], (count, *value.shape)), axis...]
    ppermute x5 -> x8, starting transfers between devices: 8.9 us -> 20.4 us  [the longest x5 10.7 us: moved_along(): lax.ppermute(block, SUB, [(i - distance, i) for i in range(n) if 0 <= i -...]
    add x5 -> x0, local copies, waits for them, and re-layouts: 10.1 us -> none  [the longest x1 9.58 us: assemble(): whole + jnp.einsum('st,sij->sitj', upper, off_blocks, precision=precise)]
    another operation x9 -> x1, local copies, waits for them, and re-layouts: 6.13 us -> 0.01 us  [the longest x2 6.06 us: apply_jump(): block_rows = matrix[0].reshape(2, own_rows, 2, face_len)]
    dot_general x17 -> x15, matrix products: 8.85 us -> 14.8 us  [the longest x9 6.71 us: dot(): return jnp.dot(a, b, precision=HIGH, preferred_element_type=jnp.float32)]
  transfers between devices with their start and end apart: 9 -> 11, of which waited for: 8 -> 8; matrix products, arithmetic and copies ran while one was open for 8% -> 4% of each run, Pallas kernels for 0% -> 0%
where the time goes in v1:
time: 155 us; the launch traced here: 153 us
  starting transfers between devices  47.9 us (31%)
  waiting for transfers between devices  40.5 us (26%)
  blocking collectives  28.3 us (18%)
  matrix products  14.8 us (10%)
  local copies, waits for them, and re-layouts  12.8 us (8%)
  Pallas kernels  4.75 us (3%)
  between operations  2.16 us (1%)
  other arithmetic  1.74 us (1%)
    all_to_all x3, waiting for transfers between devices, from_all(): lax.all_to_all(jnp.broadcast_to(value[None], (count, *value.shape)), axis...  31.7 us
    all_to_all x3, blocking collectives, from_all(): lax.all_to_all(jnp.broadcast_to(value[None], (count, *value.shape)), axis...  28.3 us
    all_to_all x3, starting transfers between devices, from_all(): lax.all_to_all(jnp.broadcast_to(value[None], (count, *value.shape)), axis...  27.6 us
    ppermute x5, starting transfers between devices, moved_along(): lax.ppermute(block, SUB, [(i - distance, i) for i in range(n) if 0 <= i -...  10.7 us
    ppermute x3, starting transfers between devices, core_swap(): return lax.ppermute(block, 'c', [(0, 1), (1, 0)])  9.68 us
    dot_general x9, matrix products, dot(): return jnp.dot(a, b, precision=HIGH, preferred_element_type=jnp.float32)  6.71 us
    unnamed x67, local copies, waits for them, and re-layouts  6.06 us
    ppermute x5, waiting for transfers between devices, moved_along(): lax.ppermute(block, SUB, [(i - distance, i) for i in range(n) if 0 <= i -...  5.45 us
  transfers between devices with their start and end apart: 11, of which 8 were waited for; matrix products, arithmetic and copies ran while one was open for 4% of the time, Pallas kernels for 0%

profile of v1, /device:TPU:1, one launch (start us, length us, event | category | flops | bytes accessed | tf_op | source)
XLA Modules:
  0.0 153.0 jit_solution(555621597459729839)
XLA Ops:
  2.3 1.3 collective-permute-start.1
  3.6 0.9 copy.57
  4.6 4.7 %collective-permute-start = (f32[136,128]{0,1:T(8,128)S(1)}, f32[136,128]{0,1:T(8,128)S(1)}, u32[]{:S(2)}, u32[]{:S(2)}) collective-permute-start(f32[136,128]{0,1:T(8,128)S(1)} %pad_maximum_fusion.2), channel_id=1, source_target_pairs={{0,8},{8,16},{16,24},{24,32},{32,40},{40,48},{48,56},{56,64},{64,7... | collective-permute-start | bytes 208904 | tf_op jit(solution)/shard_map/ppermute | solution.py:129
  9.3 1.9 %collective-permute-done = f32[136,128]{0,1:T(8,128)S(1)} collective-permute-done((f32[136,128]{0,1:T(8,128)S(1)}, f32[136,128]{0,1:T(8,128)S(1)}, u32[]{:S(2)}, u32[]{:S(2)}) %collective-permute-start) | collective-permute-done | bytes 69664 | tf_op jit(solution)/shard_map/ppermute | solution.py:129
  11.9 12.2 %all_to_all.30 = f32[4,288,128]{2,1,0:T(8,128)S(1)} all-to-all(f32[4,288,128]{2,1,0:T(8,128)S(1)} %broadcast_in_dim.18), channel_id=1, replica_groups=mesh['z'=8,'y'=4,'x'=4,'c'=2] {'x'}, dimensions={0} | all-to-all | bytes 1179648 | tf_op jit(solution)/shard_map/all_to_all | solution.py:140
  24.1 2.9 %collective-permute-start.2 = (f32[4,288,128]{2,1,0:T(8,128)S(1)}, f32[4,288,128]{2,1,0:T(8,128)}, u32[]{:S(2)}, u32[]{:S(2)}) collective-permute-start(f32[4,288,128]{2,1,0:T(8,128)S(1)} %all_to_all.30), channel_id=1, source_target_pairs={{0,1},{1,0},{2,3},{3,2},{4,5},{5,4},{6,7},{7,6},{8,9},{9,8},{10,11... | collective-permute-start | bytes 1769480 | tf_op jit(solution)/shard_map/ppermute | solution.py:135
  27.1 1.7 %collective-permute-done.2 = f32[4,288,128]{2,1,0:T(8,128)} collective-permute-done((f32[4,288,128]{2,1,0:T(8,128)S(1)}, f32[4,288,128]{2,1,0:T(8,128)}, u32[]{:S(2)}, u32[]{:S(2)}) %collective-permute-start.2) | collective-permute-done | bytes 589856 | tf_op jit(solution)/shard_map/ppermute | solution.py:135
  28.8 1.2 select_bitcast_fusion.1
  32.1 14.6 %all-to-all-start.1 = ((f32[32,16,128]{2,1,0:T(8,128)}), f32[32,16,128]{2,1,0:T(8,128)S(1)}, u32[]{:S(2)}, u32[]{:S(2)}) async-start(f32[32,16,128]{2,1,0:T(8,128)} %broadcast_in_dim.20), calls=%async_computation.1 | async-start | bytes 524288 | tf_op jit(solution)/shard_map/all_to_all | solution.py:140
  46.7 11.6 %all-to-all-done.1 = f32[32,16,128]{2,1,0:T(8,128)S(1)} async-done(((f32[32,16,128]{2,1,0:T(8,128)}), f32[32,16,128]{2,1,0:T(8,128)S(1)}, u32[]{:S(2)}, u32[]{:S(2)}) %all-to-all-start.1) | async-done | bytes 262176 | tf_op jit(solution)/shard_map/all_to_all | solution.py:140
  59.0 4.8 %coarse_inverse.1 = f32[256,256]{1,0:T(8,128)} custom-call(f32[256,128]{1,0:T(8,128)} %get-tuple-element.18.refs_0_), custom_call_target="tpu_custom_call" | custom-call | tf_op jit(solution)/shard_map/coarse_inverse/pallas_call | solution.py:117
  63.7 1.3 copy.66
  65.0 0.9 copy.83
  66.1 2.6 %convolution_subtract_fusion = f32[2048,128]{1,0:T(8,128)S(1)} fusion(f32[2048,128]{1,0:T(8,128)S(1)} %bitcast.109, f32[24,128]{1,0:T(8,128)S(1)} %fusion.30, f32[8,1024]{1,0:T(8,128)} %copy-done.6, f32[8,1024]{1,0:T(8,128)} %copy-done.8, f32[8,1024]{1,0:T(8,128)S(1)} %broadcast_in_dim.19, f32[8,1024]{1,0:T(8,128)} %copy-done.10, ...), kind=kOutput, calls=%fused_computation | convolution fusion | flops 76005376 | bytes 2273280 | tf_op jit(solution)/shard_map/dot_general | solution.py:217
  68.8 1.9 %fusion.1 = f32[256,128]{0,1:T(8,128)S(1)} fusion(f32[2048,128]{1,0:T(8,128)S(1)} %convolution_subtract_fusion, f32[256,2048]{1,0:T(8,128)S(1)} %bitcast.114), kind=kOutput, calls=%fused_computation.6 | convolution fusion | flops 805339136 | bytes 3276800 | tf_op jit(solution)/shard_map/dot_general | solution.py:16
  70.7 2.1 %collective-permute-start.3 = (f32[128,128]{0,1:T(8,128)S(1)}, f32[128,128]{0,1:T(8,128)S(1)}, u32[]{:S(2)}, u32[]{:S(2)}) collective-permute-start(f32[128,128]{0,1:T(8,128)S(1)} %get-tuple-element.21), channel_id=1, source_target_pairs={{0,8},{8,16},{16,24},{24,32},{32,40},{40,48},{48,56},{56,64},{64,7... | collective-permute-start | bytes 196616 | tf_op jit(solution)/shard_map/ppermute | solution.py:129
  72.9 1.3 collective-permute-start.4
  74.3 3.6 %collective-permute-done.4 = f32[128,128]{0,1:T(8,128)S(1)} collective-permute-done((f32[128,128]{0,1:T(8,128)S(1)}, f32[128,128]{0,1:T(8,128)S(1)}, u32[]{:S(2)}, u32[]{:S(2)}) %collective-permute-start.4) | collective-permute-done | bytes 65568 | tf_op jit(solution)/shard_map/ppermute | solution.py:129
  77.9 1.4 multiply_reduce_fusion.1
  80.0 9.3 %all_to_all.31 = f32[4,256,128]{2,1,0:T(8,128)S(1)} all-to-all(f32[4,256,128]{2,1,0:T(8,128)S(1)} %broadcast_in_dim.21), channel_id=1, replica_groups=mesh['z'=8,'y'=4,'x'=4,'c'=2] {'x'}, dimensions={0} | all-to-all | bytes 1048576 | tf_op jit(solution)/shard_map/all_to_all | solution.py:140
  89.3 4.6 %collective-permute-start.5 = (f32[4,256,128]{2,1,0:T(8,128)S(1)}, f32[4,256,128]{2,1,0:T(8,128)S(1)}, u32[]{:S(2)}, u32[]{:S(2)}) collective-permute-start(f32[4,256,128]{2,1,0:T(8,128)S(1)} %all_to_all.31), channel_id=1, source_target_pairs={{0,1},{1,0},{2,3},{3,2},{4,5},{5,4},{6,7},{7,6},{8,9},{9,8},{10,11... | collective-permute-start | bytes 1572872 | tf_op jit(solution)/shard_map/ppermute | solution.py:135
  97.6 9.0 %all-to-all-start.3 = ((f32[32,8,128]{2,1,0:T(8,128)}), f32[32,8,128]{2,1,0:T(8,128)}, u32[]{:S(2)}, u32[]{:S(2)}) async-start(f32[32,8,128]{2,1,0:T(8,128)} %broadcast_in_dim.22), calls=%async_computation.3 | async-start | bytes 262144 | tf_op jit(solution)/shard_map/all_to_all | solution.py:140
  106.6 3.1 %fusion.15 = f32[24,256]{1,0:T(8,128)} fusion(f32[256,2048]{1,0:T(8,128)S(1)} %bitcast.107, f32[8,1024]{1,0:T(8,128)S(1)} %copy-done.7, f32[8,1024]{1,0:T(8,128)S(1)} %copy-done.9, f32[8,1024]{1,0:T(8,128)S(1)} %copy-done.3, f32[8,1024]{1,0:T(8,128)} %copy-done.10, f32[8,1024]{1,0:T(8,128)S(1)} %copy-done.5), kind=kOutput, calls=%fused_computation.61 | convolution fusion | flops 151240704 | bytes 2285568 | tf_op jit(solution)/shard_map/dot_general | solution.py:20
  109.7 6.0 %all-to-all-done.3 = f32[32,8,128]{2,1,0:T(8,128)} async-done(((f32[32,8,128]{2,1,0:T(8,128)}), f32[32,8,128]{2,1,0:T(8,128)}, u32[]{:S(2)}, u32[]{:S(2)}) %all-to-all-start.3) | async-done | bytes 131104 | tf_op jit(solution)/shard_map/all_to_all | solution.py:140
  115.7 1.0 copy.71
  116.9 1.0 fusion.35
  118.0 1.8 %fusion = f32[256,128]{0,1:T(8,128)S(1)} fusion(f32[256,128]{0,1:T(8,128)S(1)} %fusion.35, f32[2048,128]{1,0:T(8,128)S(1)} %bitcast.111, f32[256,2048]{1,0:T(8,128)S(1)} %bitcast.106), kind=kOutput, calls=%fused_computation.4 | convolution fusion | flops 805339136 | bytes 3407872 | tf_op jit(solution)/shard_map/dot_general | solution.py:16
  120.5 2.2 %collective-permute-start.6 = (f32[32,128]{1,0:T(8,128)S(1)}, f32[32,128]{1,0:T(8,128)S(1)}, u32[]{:S(2)}, u32[]{:S(2)}) collective-permute-start(f32[32,128]{1,0:T(8,128)S(1)} %pad_maximum_fusion.4), channel_id=1, source_target_pairs={{0,1},{1,0},{2,3},{3,2},{4,5},{5,4},{6,7},{7,6},{8,9},{9,8},{10,11... | collective-permute-start | bytes 49160 | tf_op jit(solution)/shard_map/ppermute | solution.py:135
  123.5 6.8 %all_to_all.32 = f32[4,32,128]{2,1,0:T(8,128)S(1)} all-to-all(f32[4,32,128]{2,1,0:T(8,128)S(1)} %broadcast_in_dim.23), channel_id=1, replica_groups=mesh['z'=8,'y'=4,'x'=4,'c'=2] {'x'}, dimensions={0} | all-to-all | bytes 131072 | tf_op jit(solution)/shard_map/all_to_all | solution.py:140
  131.2 4.0 %all-to-all-start.5 = ((f32[32,32,128]{2,1,0:T(8,128)}), f32[32,32,128]{2,1,0:T(8,128)S(1)}, u32[]{:S(2)}, u32[]{:S(2)}) async-start(f32[32,32,128]{2,1,0:T(8,128)} %broadcast_in_dim.24), calls=%async_computation.5 | async-start | bytes 1048576 | tf_op jit(solution)/shard_map/all_to_all | solution.py:140
  135.3 1.3 collective-permute-start.7
  136.6 14.1 %all-to-all-done.5 = f32[32,32,128]{2,1,0:T(8,128)S(1)} async-done(((f32[32,32,128]{2,1,0:T(8,128)}), f32[32,32,128]{2,1,0:T(8,128)S(1)}, u32[]{:S(2)}, u32[]{:S(2)}) %all-to-all-start.5) | async-done | bytes 524320 | tf_op jit(solution)/shard_map/all_to_all | solution.py:140
  (128 shorter events, 13.8 us)
Async XLA Ops:
  0.6 105.9 %copy-start = (f32[1,2,128,2048]{3,2,1,0:T(8,128)S(1)}, f32[1,2,128,2048]{3,2,1,0:T(8,128)}, u32[]{:S(2)}) copy-start(f32[1,2,128,2048]{3,2,1,0:T(8,128)} %param.6) | copy-start | bytes 6291460
  2.3 7.0 %collective-permute-start.1 = (f32[8,128]{0,1:T(8,128)S(1)}, f32[8,128]{0,1:T(8,128)S(1)}, u32[]{:S(2)}, u32[]{:S(2)}) collective-permute-start(f32[8,128]{0,1:T(8,128)S(1)} %get-tuple-element.27), channel_id=1, source_target_pairs={{8,0},{16,8},{24,16},{32,24},{40,32},{48,40},{56,48},{64,56},{72,6... | collective-permute-start | bytes 12296 | tf_op jit(solution)/shard_map/ppermute | solution.py:129
  4.6 6.6 %copy-start.18 = (f32[1,128,128]{1,2,0:T(8,128)}, f32[1,128,128]{1,2,0:T(8,128)S(1)}, u32[]{:S(2)}) copy-start(f32[1,128,128]{1,2,0:T(8,128)S(1)} %copy.57) | copy-start | bytes 196612
  4.6 6.6 %collective-permute-start = (f32[136,128]{0,1:T(8,128)S(1)}, f32[136,128]{0,1:T(8,128)S(1)}, u32[]{:S(2)}, u32[]{:S(2)}) collective-permute-start(f32[136,128]{0,1:T(8,128)S(1)} %pad_maximum_fusion.2), channel_id=1, source_target_pairs={{0,8},{8,16},{16,24},{24,32},{32,40},{40,48},{48,56},{56,64},{64,7... | collective-permute-start | bytes 208904 | tf_op jit(solution)/shard_map/ppermute | solution.py:129
  9.3 20.6 %copy-start.12 = (f32[8,128]{0,1:T(8,128)}, f32[8,128]{0,1:T(8,128)S(1)}, u32[]{:S(2)}) copy-start(f32[8,128]{0,1:T(8,128)S(1)} %broadcast_multiply_fusion) | copy-start | bytes 12292
  9.3 2.1 %copy-start.16 = (f32[8,128]{0,1:T(8,128)}, f32[8,128]{0,1:T(8,128)S(1)}, u32[]{:S(2)}) copy-start(f32[8,128]{0,1:T(8,128)S(1)} %neg.15) | copy-start | bytes 12292
  24.1 4.7 %collective-permute-start.2 = (f32[4,288,128]{2,1,0:T(8,128)S(1)}, f32[4,288,128]{2,1,0:T(8,128)}, u32[]{:S(2)}, u32[]{:S(2)}) collective-permute-start(f32[4,288,128]{2,1,0:T(8,128)S(1)} %all_to_all.30), channel_id=1, source_target_pairs={{0,1},{1,0},{2,3},{3,2},{4,5},{5,4},{6,7},{7,6},{8,9},{9,8},{10,11... | collective-permute-start | bytes 1769480 | tf_op jit(solution)/shard_map/ppermute | solution.py:135
  30.1 1.2 copy-start.10
  30.2 36.0 %copy-start.4 = (f32[8,1024]{1,0:T(8,128)}, f32[8,1024]{1,0:T(8,128)S(1)}, u32[]{:S(2)}) copy-start(f32[8,1024]{1,0:T(8,128)S(1)} %get-tuple-element.23) | copy-start | bytes 98308
  30.2 36.0 %copy-start.2 = (f32[8,1024]{1,0:T(8,128)}, f32[8,1024]{1,0:T(8,128)S(1)}, u32[]{:S(2)}) copy-start(f32[8,1024]{1,0:T(8,128)S(1)} %broadcast_in_dim.19) | copy-start | bytes 98308
  32.1 26.2 %all-to-all-start.1 = ((f32[32,16,128]{2,1,0:T(8,128)}), f32[32,16,128]{2,1,0:T(8,128)S(1)}, u32[]{:S(2)}, u32[]{:S(2)}) async-start(f32[32,16,128]{2,1,0:T(8,128)} %broadcast_in_dim.20), calls=%async_computation.1 | async-start | bytes 524288 | tf_op jit(solution)/shard_map/all_to_all | solution.py:140
  63.7 5.0 %copy-start.1 = (f32[1,2,128,2048]{3,2,1,0:T(8,128)S(1)}, f32[1,2,128,2048]{3,2,1,0:T(8,128)}, u32[]{:S(2)}) copy-start(f32[1,2,128,2048]{3,2,1,0:T(8,128)} %param.7) | copy-start | bytes 6291460
  68.8 5.5 %copy-start.17 = (f32[8,128]{0,1:T(8,128)S(1)}, f32[8,128]{0,1:T(8,128)}, u32[]{:S(2)}) copy-start(f32[8,128]{0,1:T(8,128)} %copy-done.16) | copy-start | bytes 12292
  68.8 9.1 %copy-start.19 = (f32[1,128,128]{1,2,0:T(8,128)S(1)}, f32[1,128,128]{1,2,0:T(8,128)}, u32[]{:S(2)}) copy-start(f32[1,128,128]{1,2,0:T(8,128)} %copy-done.18) | copy-start | bytes 196612
  70.7 23.2 %copy-start.13 = (f32[8,128]{0,1:T(8,128)S(1)}, f32[8,128]{0,1:T(8,128)}, u32[]{:S(2)}) copy-start(f32[8,128]{0,1:T(8,128)} %copy-done.12) | copy-start | bytes 12292
  70.7 23.2 %copy-start.15 = (f32[8,128]{0,1:T(8,128)S(1)}, f32[8,128]{0,1:T(8,128)}, u32[]{:S(2)}) copy-start(f32[8,128]{0,1:T(8,128)} %copy-done.14) | copy-start | bytes 12292
  70.7 3.6 %collective-permute-start.3 = (f32[128,128]{0,1:T(8,128)S(1)}, f32[128,128]{0,1:T(8,128)S(1)}, u32[]{:S(2)}, u32[]{:S(2)}) collective-permute-start(f32[128,128]{0,1:T(8,128)S(1)} %get-tuple-element.21), channel_id=1, source_target_pairs={{0,8},{8,16},{16,24},{24,32},{32,40},{40,48},{48,56},{56,64},{64,7... | collective-permute-start | bytes 196616 | tf_op jit(solution)/shard_map/ppermute | solution.py:129
  72.9 5.0 %collective-permute-start.4 = (f32[128,128]{0,1:T(8,128)S(1)}, f32[128,128]{0,1:T(8,128)S(1)}, u32[]{:S(2)}, u32[]{:S(2)}) collective-permute-start(f32[128,128]{0,1:T(8,128)S(1)} %get-tuple-element.22), channel_id=1, source_target_pairs={{8,0},{16,8},{24,16},{32,24},{40,32},{48,40},{56,48},{64,56},{72,6... | collective-permute-start | bytes 196616 | tf_op jit(solution)/shard_map/ppermute | solution.py:129
  74.3 5.0 %copy-start.25 = (f32[8,128]{1,0:T(8,128)}, f32[8,128]{1,0:T(8,128)S(1)}, u32[]{:S(2)}) copy-start(f32[8,128]{1,0:T(8,128)S(1)} %copy.62) | copy-start | bytes 12292
  77.9 1.4 copy-start.27
  89.3 6.1 %collective-permute-start.5 = (f32[4,256,128]{2,1,0:T(8,128)S(1)}, f32[4,256,128]{2,1,0:T(8,128)S(1)}, u32[]{:S(2)}, u32[]{:S(2)}) collective-permute-start(f32[4,256,128]{2,1,0:T(8,128)S(1)} %all_to_all.31), channel_id=1, source_target_pairs={{0,1},{1,0},{2,3},{3,2},{4,5},{5,4},{6,7},{7,6},{8,9},{9,8},{10,11... | collective-permute-start | bytes 1572872 | tf_op jit(solution)/shard_map/ppermute | solution.py:135
  97.6 18.1 %all-to-all-start.3 = ((f32[32,8,128]{2,1,0:T(8,128)}), f32[32,8,128]{2,1,0:T(8,128)}, u32[]{:S(2)}, u32[]{:S(2)}) async-start(f32[32,8,128]{2,1,0:T(8,128)} %broadcast_in_dim.22), calls=%async_computation.3 | async-start | bytes 262144 | tf_op jit(solution)/shard_map/all_to_all | solution.py:140
  109.7 10.1 %copy-start.26 = (f32[8,128]{1,0:T(8,128)S(1)}, f32[8,128]{1,0:T(8,128)}, u32[]{:S(2)}) copy-start(f32[8,128]{1,0:T(8,128)} %copy-done.25) | copy-start | bytes 12292
  109.7 10.1 %copy-start.28 = (f32[8,128]{1,0:T(8,128)S(1)}, f32[8,128]{1,0:T(8,128)}, u32[]{:S(2)}) copy-start(f32[8,128]{1,0:T(8,128)} %copy-done.27) | copy-start | bytes 12292
  115.7 4.1 %copy-start.21 = (f32[128,128]{0,1:T(8,128)S(1)}, f32[128,128]{0,1:T(8,128)}, u32[]{:S(2)}) copy-start(f32[128,128]{0,1:T(8,128)} %copy-done.20) | copy-start | bytes 196612
  115.7 4.1 %copy-start.23 = (f32[128,128]{0,1:T(8,128)S(1)}, f32[128,128]{0,1:T(8,128)}, u32[]{:S(2)}) copy-start(f32[128,128]{0,1:T(8,128)} %copy-done.22) | copy-start | bytes 196612
  115.7 4.1 %copy-start.29 = (f32[8,128]{1,0:T(8,128)S(1)}, f32[8,128]{1,0:T(8,128)}, u32[]{:S(2)}) copy-start(f32[8,128]{1,0:T(8,128)} %copy.59) | copy-start | bytes 12292
  116.9 3.6 %copy-start.30 = (f32[128]{0:T(128)S(1)}, f32[128]{0:T(128)}, u32[]{:S(2)}) copy-start(f32[128]{0:T(128)} %get-tuple-element.10) | copy-start | bytes 1540
  120.5 3.0 %collective-permute-start.6 = (f32[32,128]{1,0:T(8,128)S(1)}, f32[32,128]{1,0:T(8,128)S(1)}, u32[]{:S(2)}, u32[]{:S(2)}) collective-permute-start(f32[32,128]{1,0:T(8,128)S(1)} %pad_maximum_fusion.4), channel_id=1, source_target_pairs={{0,1},{1,0},{2,3},{3,2},{4,5},{5,4},{6,7},{7,6},{8,9},{9,8},{10,11... | collective-permute-start | bytes 49160 | tf_op jit(solution)/shard_map/ppermute | solution.py:135
  131.2 20.7 %copy-start.24 = (f32[128,128]{0,1:T(8,128)S(1)}, f32[128,128]{0,1:T(8,128)}, u32[]{:S(2)}) copy-start(f32[128,128]{0,1:T(8,128)} %get-tuple-element.29) | copy-start | bytes 196612
  131.2 19.4 %all-to-all-start.5 = ((f32[32,32,128]{2,1,0:T(8,128)}), f32[32,32,128]{2,1,0:T(8,128)S(1)}, u32[]{:S(2)}, u32[]{:S(2)}) async-start(f32[32,32,128]{2,1,0:T(8,128)} %broadcast_in_dim.24), calls=%async_computation.5 | async-start | bytes 1048576 | tf_op jit(solution)/shard_map/all_to_all | solution.py:140
  135.3 16.7 %collective-permute-start.7 = (f32[128,128]{0,1:T(8,128)S(1)}, f32[128,128]{0,1:T(8,128)S(1)}, u32[]{:S(2)}, u32[]{:S(2)}) collective-permute-start(f32[128,128]{0,1:T(8,128)S(1)} %slice.123), channel_id=1, source_target_pairs={{8,0},{16,8},{24,16},{32,24},{40,32},{48,40},{56,48},{64,56},{72,6... | collective-permute-start | bytes 196616 | tf_op jit(solution)/shard_map/ppermute | solution.py:129
  (10 other events, 7.6 us)

commit v2 on v1

--- a/solution.py
+++ b/solution.py
@@ -6,9 +6,12 @@
 from jax.sharding import Mesh
 from jax.sharding import PartitionSpec as P
 
+
 SUB = ("z", "y")
 IFC = ("x", "c")
+ALL = SUB + IFC
 HIGH = lax.Precision.HIGHEST
+NEAR = 5
 PAD = 8
 
 
@@ -22,10 +25,10 @@
     )
 
 
-def inverse_kernel(subs, modes, m_ref, out_ref, cols_ref):
+def inverse_kernel(subs, modes, sub_ref, sent_ref, inverse_ref, near_ref, weights_ref, cols_ref):
     lanes = 128
     for i in range(PAD):
-        rows = m_ref[pl.ds(i, subs, stride=PAD), :]
+        rows = sent_ref[pl.ds(PAD + i, subs, stride=2 * PAD), :]
         turned = jnp.concatenate([rows] * (lanes // subs), axis=0).T
         cols_ref[pl.ds(i, 3 * PAD, stride=PAD), :] = turned[: 3 * PAD]
 
@@ -109,19 +112,79 @@
         )
         total = step if total is None else dot(step, total)
         h *= 2
-    out_ref[...] = dot(dense([(inverse(diag), 0)]), total)
-
-
-def coarse_inverse(rows, subs, modes):
+    whole = dot(dense([(inverse(diag), 0)]), total)
+    inverse_ref[...] = whole
+    row = lax.broadcasted_iota(jnp.int32, (NEAR * PAD, PAD * subs), 0)
+    col = lax.broadcasted_iota(jnp.int32, (NEAR * PAD, PAD * subs), 1)
+    wanted = (row % PAD) * subs + row // PAD + (sub_ref[0] - NEAR // 2)
+    inside = (row // PAD + sub_ref[0] >= NEAR // 2) & (row // PAD + sub_ref[0] < subs + NEAR // 2)
+    near = dot(jnp.where((col == wanted) & inside, 1.0, 0.0), whole)
+    near_ref[...] = near
+    rhs = jnp.concatenate(
+        [sent_ref[pl.ds(i, subs, stride=2 * PAD), :] for i in range(PAD)], axis=0
+    )
+    weights_ref[...] = dot(near, rhs)
+
+
+def coarse_inverse(sub, sent, subs, modes):
     size = subs * PAD
+    vmem = pl.BlockSpec(memory_space=pltpu.VMEM)
     return pl.pallas_call(
         lambda *refs: inverse_kernel(subs, modes, *refs),
-        out_shape=jax.ShapeDtypeStruct((size, size), jnp.float32),
-        in_specs=[pl.BlockSpec(memory_space=pltpu.VMEM)],
-        out_specs=pl.BlockSpec(memory_space=pltpu.VMEM),
+        out_shape=[
+            jax.ShapeDtypeStruct((size, size), jnp.float32),
+            jax.ShapeDtypeStruct((NEAR * PAD, size), jnp.float32),
+            jax.ShapeDtypeStruct((NEAR * PAD, 128), jnp.float32),
+        ],
+        in_specs=[pl.BlockSpec(memory_space=pltpu.SMEM), vmem],
+        out_specs=[vmem] * 3,
         scratch_shapes=[pltpu.VMEM((3 * PAD * PAD, 128), jnp.float32)],
         name="coarse_inverse",
-    )(rows)
+    )(sub, sent)
+
+
+def assemble_kernel(count, rows, own_ref, other_ref, place_ref, traces_ref, extra_ref):
+    x, core = place_ref[0], place_ref[1]
+    head = 0 if traces_ref is None else 2 * rows
+    for q in range(count):
+        d = lax.rem(x - q + count, count)
+        for c in range(2):
+            at = 2 * q + c
+
+            def copy(ref):
+                if traces_ref is not None:
+                    for face in range(2):
+                        start = (face * 2 * count + at) * rows
+                        traces_ref[start : start + rows, :] = ref[d, face * rows : (face + 1) * rows, :]
+                extra_ref[:, at * 128 : (at + 1) * 128] = ref[d, head:, :]
+
+            @pl.when(core == c)
+            def _():
+                copy(own_ref)
+
+            @pl.when(core != c)
+            def _():
+                copy(other_ref)
+
+
+def assemble(own, other, place, rows, with_traces):
+    count, pieces, _ = own.shape
+    vmem = pl.BlockSpec(memory_space=pltpu.VMEM)
+    head = 2 * rows if with_traces else 0
+    extra = jax.ShapeDtypeStruct((pieces - head, 2 * count * 128), jnp.float32)
+    traces = jax.ShapeDtypeStruct((2 * rows * 2 * count, 128), jnp.float32)
+
+    def kernel(own_ref, other_ref, place_ref, *outs):
+        outs = outs if with_traces else (None, *outs)
+        assemble_kernel(count, rows, own_ref, other_ref, place_ref, *outs)
+
+    return pl.pallas_call(
+        kernel,
+        out_shape=[traces, extra] if with_traces else [extra],
+        in_specs=[vmem, vmem, pl.BlockSpec(memory_space=pltpu.SMEM)],
+        out_specs=[vmem] * (2 if with_traces else 1),
+        name="assemble",
+    )(own, other, place)
 
 
 def moved_along(block, distance):
@@ -142,16 +205,28 @@
     )
 
 
-def gathered(piece):
-    own = from_all(piece, "x")
-    other = core_swap(own)
-    on_first = lax.axis_index("c") == 0
-    return jnp.stack([jnp.where(on_first, own, other), jnp.where(on_first, other, own)], 1)
+def along_x(piece):
+    n = lax.axis_size("x")
+    return [piece] + [
+        lax.ppermute(piece, "x", [(i, (i + d) % n) for i in range(n)]) for d in range(1, n)
+    ]
+
+
+def gathered(piece, place, rows, with_traces=True):
+    own = jnp.stack(along_x(piece))
+    return assemble(own, core_swap(own), place, rows, with_traces)
+
+
+def spread(part, weights):
+    return lax.dot_general(
+        part, weights, (((0,), (0,)), ((), ())), precision=HIGH, preferred_element_type=jnp.float32
+    )
 
 
 def per_device(gap, flexibility, stiffness, modes, mode_counts):
     subs = lax.axis_size(SUB)
     sub = lax.axis_index(SUB)
+    place = jnp.stack([lax.axis_index("x"), lax.axis_index("c")]).astype(jnp.int32)
     rows, loads = gap.shape[1], gap.shape[2]
     lanes = lax.axis_size(IFC)
     face = rows * lanes
@@ -169,98 +244,124 @@
     from_before = moved_along(jnp.concatenate([field, right], 0), 1)
     left_after = moved_along(left, -1)
     field_before, right_before = from_before[:rows], from_before[rows:]
-    piece = jnp.concatenate(
-        [-field_before, field, -right_before, left * inner, right, -left_after], 0
-    )
-    whole = gathered(piece)
-
-    def traces_of(pieces):
-        pieces = pieces.reshape(lanes, 2, rows, loads)
-        return pieces.transpose(1, 0, 2, 3).reshape(2 * face, loads)
-
-    gap_traces = traces_of(whole[:, :, : 2 * rows])
-    faces = whole[:, :, 2 * rows :].reshape(lanes, 4, PAD, rows)
-    faces = faces.transpose(1, 2, 0, 3).reshape(4, PAD, face)
+    left_in = left * inner
+    piece = jnp.concatenate([-field_before, field, -right_before, left_in, right, -left_after], 0)
+    gap_traces, faces = gathered(piece, place, rows)
     none = jnp.zeros((PAD, face), jnp.float32)
     basis = jnp.concatenate(
         [
-            jnp.concatenate([faces[0], faces[1], none], 0),
-            jnp.concatenate([none, faces[2], faces[3]], 0),
+            jnp.concatenate([faces[: 2 * PAD], none], 0),
+            jnp.concatenate([none, faces[2 * PAD :]], 0),
         ],
         1,
     )
+    none = jnp.zeros_like(left)
     own_basis = jnp.concatenate(
         [
-            jnp.concatenate([-right_before, left * inner, jnp.zeros_like(left)], 0),
-            jnp.concatenate([jnp.zeros_like(left), right, -left_after], 0),
+            jnp.concatenate([-right_before, left_in, none], 0),
+            jnp.concatenate([none, right, -left_after], 0),
         ],
         1,
     )
     here = basis[PAD : 2 * PAD]
-
     rest = jnp.pad(
         jnp.eye(PAD, dtype=jnp.float32) * (1.0 - active)[:, None], ((0, 0), (PAD, PAD))
     )
     blocks = dot_nt(here, basis) + rest
     rhs = dot(here, gap_traces)
     sent = jnp.concatenate([rhs, jnp.pad(blocks, ((0, 0), (0, 128 - 3 * PAD)))], 0)
-    first = from_all(sent, SUB)
-    inverse = coarse_inverse(first[:, PAD:].reshape(subs * PAD, 128), subs, mode_count)
-    near = jnp.pad(inverse.reshape(PAD, subs, PAD * subs), ((0, 0), (1, 1), (0, 0)))
-    near = lax.dynamic_slice_in_dim(near, sub, 3, 1)
-    near = near.transpose(1, 0, 2).reshape(3 * PAD, PAD * subs)
-
-    def weights_of(all_rhs):
-        return dot(near, all_rhs.transpose(1, 0, 2).reshape(PAD * subs, loads))
-
-    def spread(part, weights):
-        return lax.dot_general(
-            part, weights, (((0,), (0,)), ((), ())), precision=HIGH,
-            preferred_element_type=jnp.float32,
+
+    image = 0.25 * dot(stiff, gap_traces)
+    modes_image = 0.25 * dot_nt(basis, stiff)
+    first = from_all(sent, SUB).reshape(subs * 2 * PAD, 128)
+    before = moved_along(jnp.concatenate([image[rows:], modes_image[:, rows:]], 0), 1)
+    after = moved_along(jnp.concatenate([image[:rows], modes_image[:, :rows]], 0), -1)
+    top = (image[:rows] - before[:rows]) * inner
+    bottom = (image[rows:] - after[:rows]) * live
+    own_traces = jnp.concatenate([top, bottom], 0)
+    gone = jnp.zeros((PAD, rows), jnp.float32)
+    modes_top = jnp.concatenate([gone, modes_image[:, :rows], gone], 0)
+    modes_top = modes_top - jnp.concatenate([before[rows:], gone, gone], 0)
+    modes_bottom = jnp.concatenate([gone, modes_image[:, rows:], gone], 0)
+    modes_bottom = modes_bottom - jnp.concatenate([gone, gone, after[rows:]], 0)
+    own_modes = jnp.concatenate([modes_top * inner, modes_bottom * live], 1)
+
+    flex_modes = dot_nt(basis, flex)
+    small = dot_nt(flex_modes, jnp.concatenate([own_modes, own_basis], 0))
+    cross = jnp.pad(dot_nt(own_basis[PAD : 2 * PAD], own_modes), ((0, 2 * PAD), (0, 0)))
+    small = jnp.concatenate([small, cross], 1)
+    small = jnp.pad(small, ((0, 0), (0, 128 - small.shape[1])))
+    piece = jnp.concatenate([own_traces, dot(flex_modes, own_traces), small], 0)
+    search_traces, extra = gathered(piece, place, rows)
+    extra = extra.reshape(6 * PAD, lanes, 128).sum(1)
+    flex_search, small = extra[: 3 * PAD], extra[3 * PAD :]
+    wide = NEAR * PAD
+
+    inverse, near, weights = coarse_inverse(sub.astype(jnp.int32)[None], first, subs, mode_count)
+    near = near[PAD : 4 * PAD]
+    rhs = dot(here, search_traces) - dot(small[:PAD, wide + 3 * PAD : 2 * wide + 3 * PAD], weights)
+    flex_search = flex_search - dot(small[:, :wide], weights)
+    mine = (place[0] * 2 + place[1]) * (loads // lanes)
+    share = loads // lanes
+
+    def folded(block):
+        return jnp.concatenate([block[b * PAD : (b + 1) * PAD] for b in range(3)], 1)
+
+    flex_search = lax.dynamic_slice_in_dim(flex_search, mine, share, 1)
+    last = jnp.concatenate([folded(flex_search), folded(small[:, wide : wide + 3 * PAD])], 1)
+    last = jnp.pad(last, ((0, 0), (0, 128 - last.shape[1])))
+    second = from_all(jnp.concatenate([rhs, last], 0), SUB)
+
+    (modes_traces,) = gathered(
+        jnp.concatenate([own_modes[:, :rows], own_modes[:, rows:]], 0), place, rows, False
+    )
+    modes_traces = jnp.concatenate([modes_traces[:wide], modes_traces[wide:]], 1)
+    image = dot(flex, search_traces) - dot(dot_nt(flex, modes_traces), weights)
+    own_search = own_traces - spread(own_modes, weights)
+    own_res = field - spread(own_basis[:, rows:], weights[PAD : 4 * PAD])
+
+    all_rhs = second[:, :PAD].transpose(1, 0, 2).reshape(PAD * subs, loads)
+    weights = dot(near, all_rhs)
+    image = image - spread(flex_modes, weights)
+    direction = own_search - spread(own_basis, weights)
+    sums = jnp.stack(
+        [jnp.sum(own_res * own_search[rows:], 0), jnp.sum(direction * image, 0)], 0
+    )
+    totals = from_all(sums, ALL).sum(0)
+
+    after = moved_along(image[:rows], -1)
+    my_rhs = lax.dynamic_slice_in_dim(all_rhs, mine, share, 1)
+    my_weights = dot(inverse, my_rhs).reshape(PAD, subs, share).transpose(1, 0, 2)
+    my_weights = jnp.pad(my_weights, ((1, 1), (0, 0), (0, 0)))
+    my_weights = jnp.concatenate([my_weights[b : b + subs] for b in range(3)], 1)
+    tail = second[:, PAD:]
+    parts = []
+    for b in range(3):
+        start = 3 * share + b * 3 * PAD
+        product = lax.dot_general(
+            tail[:, :, start : start + 3 * PAD], my_weights, (((2,), (1,)), ((0,), (0,))),
+            precision=HIGH, preferred_element_type=jnp.float32,
         )
-
-    weights = weights_of(first[:, :PAD])
-    res_traces = gap_traces - spread(basis, weights)
-    own_res = field - spread(own_basis[:, rows:], weights)
-
-    image = 0.25 * dot(stiff, res_traces)
-    before = moved_along(image[rows:], 1)
-    after = moved_along(image[:rows], -1)
-    own_search = (image[rows:] - after) * live
-    before_search = (before - image[:rows]) * inner
-    own_traces = jnp.concatenate([-before_search, own_search], 0)
-    search_traces = traces_of(gathered(own_traces))
-    second = from_all(dot(here, search_traces), SUB)
-    pre_image = dot(flex, search_traces)
-    flex_basis = dot_nt(flex, basis)
-    weights = weights_of(second)
-    image = pre_image - dot(flex_basis, weights)
-    direction = own_traces - spread(own_basis, weights)
-
-    after = moved_along(image[:rows], -1)
-    sums = jnp.stack(
-        [jnp.sum(own_res * own_search, 0), jnp.sum(direction * image, 0)], 0
-    )
-    partial = jnp.concatenate([dot(own_basis, image), jnp.pad(sums, ((0, PAD - 2), (0, 0)))], 0)
-    partial = partial + core_swap(partial)
-    partial = from_all(partial, "x").sum(0)
-    third = from_all(partial, SUB)
-    totals = third[:, 3 * PAD :].sum(0)
-    parts = third[:, : 3 * PAD].reshape(subs, 3, PAD, loads)
-    none = jnp.zeros((1, PAD, loads), jnp.float32)
-    all_rhs = (
-        parts[:, 1]
-        + jnp.concatenate([parts[1:, 0], none], 0)
-        + jnp.concatenate([none, parts[:-1, 2]], 0)
-    )
-    weights = weights_of(all_rhs)
+        parts.append(tail[:, :, b * share : (b + 1) * share] - product)
+    none = jnp.zeros((1, PAD, share), jnp.float32)
+    last_rhs = (
+        parts[1]
+        + jnp.concatenate([parts[0][1:], none], 0)
+        + jnp.concatenate([none, parts[2][:-1]], 0)
+    )
+    weights = dot(near, last_rhs.transpose(1, 0, 2).reshape(PAD * subs, share))
+    weights = lax.dynamic_update_slice_in_dim(
+        jnp.zeros((3 * PAD, loads), jnp.float32), weights, mine, 1
+    )
+    weights = weights + core_swap(weights)
+    weights = sum(along_x(weights))
+    own_image = (image[rows:] - after) * live - spread(own_basis[:, rows:], weights)
     step = totals[0] / totals[1]
-    own_image = (image[rows:] - after) * live - spread(own_basis[:, rows:], weights)
     return (step * direction[rows:])[None], (own_res - step * own_image)[None]
 
 
 def solution(mesh):
-    finer = Mesh(mesh.devices.reshape(8, 4, 4, 2), ("z", "y", "x", "c"))
+    finer = Mesh(mesh.devices.reshape(8, 4, 4, 2), ALL)
     return jax.shard_map(
         per_device,
         mesh=finer,

time: 155 us -> 153 us (0.987)
  blocking collectives: 28.3 us -> 0 us
  matrix products: 14.8 us -> 27.8 us
  starting transfers between devices: 47.9 us -> 59.8 us
  Pallas kernels: 4.75 us -> 12.1 us
  waiting for transfers between devices: 40.5 us -> 34.1 us
  other arithmetic: 1.74 us -> 4.99 us
  local copies, waits for them, and re-layouts: 12.8 us -> 10 us
    all_to_all x3 -> x0, blocking collectives: 28.3 us -> none  [from_all(): lax.all_to_all(jnp.broadcast_to(value[None], (count, *value.shape)), axis...]
    all_to_all x3, waiting for transfers between devices: 31.7 us -> 15.8 us  [from_all(): lax.all_to_all(jnp.broadcast_to(value[None], (count, *value.shape)), axis...]
    ppermute x0 -> x12, starting transfers between devices: none -> 12.3 us  [along_x(): lax.ppermute(piece, 'x', [(i, (i + d) % n) for i in range(n)])]
    ppermute x0 -> x12, waiting for transfers between devices: none -> 11.9 us  [along_x(): lax.ppermute(piece, 'x', [(i, (i + d) % n) for i in range(n)])]
    pallas_call x0 -> x3, Pallas kernels: none -> 6.76 us  [assemble(): pl.pallas_call(kernel, out_shape=[traces, extra] if with_traces else [ext...]
    dot_general x9 -> x11, matrix products: 6.71 us -> 13.3 us  [dot(): return jnp.dot(a, b, precision=HIGH, preferred_element_type=jnp.float32)]
    dot_general x2 -> x6, matrix products: 3.38 us -> 6.67 us  [dot_nt(): lax.dot_general(a, b, (((1,), (1,)), ((), ())), precision=HIGH, preferred...]
    ppermute x3 -> x4, waiting for transfers between devices: 3.32 us -> 1.01 us  [core_swap(): return lax.ppermute(block, 'c', [(0, 1), (1, 0)])]
  transfers between devices with their start and end apart: 11 -> 24, of which waited for: 8 -> 11; matrix products, arithmetic and copies ran while one was open for 4% -> 12% of each run, Pallas kernels for 0% -> 5%
where the time goes in v2:
time: 153 us; the launch traced here: 151 us
  starting transfers between devices  59.8 us (39%)
  waiting for transfers between devices  34.1 us (22%)
  matrix products  27.8 us (18%)
  Pallas kernels  12.1 us (8%)
  local copies, waits for them, and re-layouts  10 us (7%)
  other arithmetic  4.99 us (3%)
  between operations  2.04 us (1%)
    all_to_all x3, starting transfers between devices, from_all(): lax.all_to_all(jnp.broadcast_to(value[None], (count, *value.shape)), axis...  28.5 us
    all_to_all x3, waiting for transfers between devices, from_all(): lax.all_to_all(jnp.broadcast_to(value[None], (count, *value.shape)), axis...  15.8 us
    dot_general x11, matrix products, dot(): return jnp.dot(a, b, precision=HIGH, preferred_element_type=jnp.float32)  13.3 us
    ppermute x12, starting transfers between devices, along_x(): lax.ppermute(piece, 'x', [(i, (i + d) % n) for i in range(n)])  12.3 us
    ppermute x12, waiting for transfers between devices, along_x(): lax.ppermute(piece, 'x', [(i, (i + d) % n) for i in range(n)])  11.9 us
    ppermute x5, starting transfers between devices, moved_along(): lax.ppermute(block, SUB, [(i - distance, i) for i in range(n) if 0 <= i -...  11.1 us
    ppermute x4, starting transfers between devices, core_swap(): return lax.ppermute(block, 'c', [(0, 1), (1, 0)])  7.94 us
    pallas_call x3, Pallas kernels, assemble(): pl.pallas_call(kernel, out_shape=[traces, extra] if with_traces else [ext...  6.76 us
  transfers between devices with their start and end apart: 24, of which 11 were waited for; matrix products, arithmetic and copies ran while one was open for 12% of the time, Pallas kernels for 5%

profile of v2, /device:TPU:1, one launch (start us, length us, event | category | flops | bytes accessed | tf_op | source)
XLA Modules:
  0.0 150.9 jit_solution(10900764829226756875)
XLA Ops:
  3.7 4.0 %collective-permute-start.1 = (f32[136,128]{1,0:T(8,128)S(1)}, f32[136,128]{1,0:T(8,128)S(1)}, u32[]{:S(2)}, u32[]{:S(2)}) collective-permute-start(f32[136,128]{1,0:T(8,128)S(1)} %pad_maximum_fusion.8), channel_id=1, source_target_pairs={{0,8},{8,16},{16,24},{24,32},{32,40},{40,48},{48,56},{56,64},{64,7... | collective-permute-start | bytes 208904 | tf_op jit(solution)/shard_map/ppermute | solution.py:192
  10.0 2.1 %collective-permute-done = f32[8,128]{1,0:T(8,128)S(1)} collective-permute-done((f32[8,128]{1,0:T(8,128)S(1)}, f32[8,128]{1,0:T(8,128)S(1)}, u32[]{:S(2)}, u32[]{:S(2)}) %collective-permute-start) | collective-permute-done | bytes 4128 | tf_op jit(solution)/shard_map/ppermute | solution.py:192
  12.1 2.5 %collective-permute-start.4 = (f32[288,128]{1,0:T(8,128)S(1)}, f32[288,128]{1,0:T(8,128)S(1)}, u32[]{:S(2)}, u32[]{:S(2)}) collective-permute-start(f32[288,128]{1,0:T(8,128)S(1)} %get-tuple-element.45), channel_id=1, source_target_pairs={{0,6},{2,0},{4,2},{6,4},{1,7},{3,1},{5,3},{7,5},{8,14},{10,8},{12,... | collective-permute-start | bytes 442376 | tf_op jit(solution)/shard_map/ppermute | solution.py:211
  15.7 2.0 %collective-permute-done.4 = f32[288,128]{1,0:T(8,128)S(1)} collective-permute-done((f32[288,128]{1,0:T(8,128)S(1)}, f32[288,128]{1,0:T(8,128)S(1)}, u32[]{:S(2)}, u32[]{:S(2)}) %collective-permute-start.4) | collective-permute-done | bytes 147488 | tf_op jit(solution)/shard_map/ppermute | solution.py:211
  17.7 2.5 %collective-permute-done.3 = f32[288,128]{1,0:T(8,128)S(1)} collective-permute-done((f32[288,128]{1,0:T(8,128)S(1)}, f32[288,128]{1,0:T(8,128)S(1)}, u32[]{:S(2)}, u32[]{:S(2)}) %collective-permute-start.3) | collective-permute-done | bytes 147488 | tf_op jit(solution)/shard_map/ppermute | solution.py:211
  20.2 2.2 %collective-permute-done.2 = f32[288,128]{1,0:T(8,128)S(1)} collective-permute-done((f32[288,128]{1,0:T(8,128)S(1)}, f32[288,128]{1,0:T(8,128)S(1)}, u32[]{:S(2)}, u32[]{:S(2)}) %collective-permute-start.2) | collective-permute-done | bytes 147488 | tf_op jit(solution)/shard_map/ppermute | solution.py:211
  22.4 3.3 %collective-permute-start.5 = (f32[4,288,128]{2,1,0:T(8,128)S(1)}, f32[4,288,128]{2,1,0:T(8,128)S(1)}, u32[]{:S(2)}, u32[]{:S(2)}) collective-permute-start(f32[4,288,128]{2,1,0:T(8,128)S(1)} %pad_maximum_fusion.1.own_ref), channel_id=1, source_target_pairs={{0,1},{1,0},{2,3},{3,2},{4,5},{5,4},{6,7},{7,6},{8,9},{9,8},{10,11... | collective-permute-start | bytes 1769480 | tf_op jit(solution)/shard_map/ppermute | solution.py:198
  28.1 2.4 %assemble.3 = (f32[2048,128]{1,0:T(8,128)}, f32[32,1024]{1,0:T(8,128)}) custom-call(f32[4,288,128]{2,1,0:T(8,128)} %copy-done.5, f32[4,288,128]{2,1,0:T(8,128)} %copy-done.14, s32[2]{0:T(128)} %pad_add_fusion.place_ref), custom_call_target="tpu_custom_call" | custom-call | tf_op jit(solution)/shard_map/assemble/pallas_call | solution.py:181
  34.4 1.7 %convolution_multiply_fusion.1 = f32[24,256]{1,0:T(8,128)S(1)} fusion(f32[256,2048]{1,0:T(8,128)S(1)} %bitcast.93, f32[16,1024]{1,0:T(8,128)S(1)} %slice.164, f32[24,1024]{1,0:T(8,128)S(1)} %slice_select_fusion), kind=kOutput, calls=%fused_computation.12 | convolution fusion | flops 151148544 | bytes 2285568 | tf_op jit(solution)/shard_map/dot_general | solution.py:23
  36.1 1.8 %fusion.5 = f32[256,128]{1,0:T(8,128)S(1)} fusion(f32[2048,128]{1,0:T(8,128)S(1)} %copy-done.3, f32[256,2048]{1,0:T(8,128)S(1)} %bitcast.94), kind=kOutput, calls=%fused_computation.8 | convolution fusion | flops 805339136 | bytes 3276800 | tf_op jit(solution)/shard_map/dot_general | solution.py:19
  38.0 3.2 %collective-permute-start.6 = (f32[152,128]{1,0:T(8,128)S(1)}, f32[152,128]{1,0:T(8,128)S(1)}, u32[]{:S(2)}, u32[]{:S(2)}) collective-permute-start(f32[152,128]{1,0:T(8,128)S(1)} %pad_maximum_fusion.6), channel_id=1, source_target_pairs={{0,8},{8,16},{16,24},{24,32},{32,40},{40,48},{48,56},{56,64},{64,7... | collective-permute-start | bytes 233480 | tf_op jit(solution)/shard_map/ppermute | solution.py:192
  43.1 3.2 %collective-permute-done.7 = f32[152,128]{1,0:T(8,128)S(1)} collective-permute-done((f32[152,128]{1,0:T(8,128)S(1)}, f32[152,128]{1,0:T(8,128)S(1)}, u32[]{:S(2)}, u32[]{:S(2)}) %collective-permute-start.7) | collective-permute-done | bytes 77856 | tf_op jit(solution)/shard_map/ppermute | solution.py:192
  48.1 2.5 %collective-permute-start.9 = (f32[304,128]{1,0:T(8,128)S(1)}, f32[304,128]{1,0:T(8,128)S(1)}, u32[]{:S(2)}, u32[]{:S(2)}) collective-permute-start(f32[304,128]{1,0:T(8,128)S(1)} %get-tuple-element.25), channel_id=1, source_target_pairs={{0,4},{2,6},{4,0},{6,2},{1,5},{3,7},{5,1},{7,3},{8,12},{10,14},{12... | collective-permute-start | bytes 466952 | tf_op jit(solution)/shard_map/ppermute | solution.py:211
  50.5 2.1 %collective-permute-start.13 = (f32[80,128]{1,0:T(8,128)S(1)}, f32[80,128]{1,0:T(8,128)S(1)}, u32[]{:S(2)}, u32[]{:S(2)}) collective-permute-start(f32[80,128]{1,0:T(8,128)S(1)} %get-tuple-element.33), channel_id=1, source_target_pairs={{0,4},{2,6},{4,0},{6,2},{1,5},{3,7},{5,1},{7,3},{8,12},{10,14},{12... | collective-permute-start | bytes 122888 | tf_op jit(solution)/shard_map/ppermute | solution.py:211
  54.1 2.9 %collective-permute-done.13 = f32[80,128]{1,0:T(8,128)S(1)} collective-permute-done((f32[80,128]{1,0:T(8,128)S(1)}, f32[80,128]{1,0:T(8,128)S(1)}, u32[]{:S(2)}, u32[]{:S(2)}) %collective-permute-start.13) | collective-permute-done | bytes 40992 | tf_op jit(solution)/shard_map/ppermute | solution.py:211
  57.0 2.3 %collective-permute-done.12 = f32[80,128]{1,0:T(8,128)S(1)} collective-permute-done((f32[80,128]{1,0:T(8,128)S(1)}, f32[80,128]{1,0:T(8,128)S(1)}, u32[]{:S(2)}, u32[]{:S(2)}) %collective-permute-start.12) | collective-permute-done | bytes 40992 | tf_op jit(solution)/shard_map/ppermute | solution.py:211
  59.3 2.4 %collective-permute-start.15 = (f32[4,80,128]{2,1,0:T(8,128)S(1)}, f32[4,80,128]{2,1,0:T(8,128)S(1)}, u32[]{:S(2)}, u32[]{:S(2)}) collective-permute-start(f32[4,80,128]{2,1,0:T(8,128)S(1)} %pad_maximum_fusion.3.own_ref), channel_id=1, source_target_pairs={{0,1},{1,0},{2,3},{3,2},{4,5},{5,4},{6,7},{7,6},{8,9},{9,8},{10,11... | collective-permute-start | bytes 491528 | tf_op jit(solution)/shard_map/ppermute | solution.py:198
  62.7 15.1 %all-to-all-start = ((f32[32,16,128]{2,1,0:T(8,128)}), f32[32,16,128]{2,1,0:T(8,128)S(1)}, u32[]{:S(2)}, u32[]{:S(2)}) async-start(f32[32,16,128]{2,1,0:T(8,128)} %broadcast_in_dim.15), calls=%async_computation | async-start | bytes 524288 | tf_op jit(solution)/shard_map/all_to_all | solution.py:203
  78.5 1.8 %assemble.5 = f32[80,1024]{1,0:T(8,128)} custom-call(f32[4,80,128]{2,1,0:T(8,128)} %copy-done.12, f32[4,80,128]{2,1,0:T(8,128)} %copy-done.19, s32[2]{0:T(128)} %pad_add_fusion.place_ref), custom_call_target="tpu_custom_call" | custom-call | tf_op jit(solution)/shard_map/assemble/pallas_call | solution.py:181
  81.3 2.6 %fusion.6 = f32[40,256]{1,0:T(8,128)} fusion(f32[256,2048]{1,0:T(8,128)S(1)} %bitcast.92, f32[40,1024]{1,0:T(8,128)S(1)} %get-tuple-element.19, f32[40,1024]{1,0:T(8,128)S(1)} %get-tuple-element.18), kind=kOutput, calls=%fused_computation.17 | convolution fusion | flops 251740160 | bytes 2465792 | tf_op jit(solution)/shard_map/dot_general | solution.py:23
  83.9 5.5 %all-to-all-done = f32[32,16,128]{2,1,0:T(8,128)S(1)} async-done(((f32[32,16,128]{2,1,0:T(8,128)}), f32[32,16,128]{2,1,0:T(8,128)S(1)}, u32[]{:S(2)}, u32[]{:S(2)}) %all-to-all-start) | async-done | bytes 262176 | tf_op jit(solution)/shard_map/all_to_all | solution.py:203
  90.1 5.4 %coarse_inverse.1 = (f32[256,256]{1,0:T(8,128)}, f32[40,256]{1,0:T(8,128)}, f32[40,128]{1,0:T(8,128)}) custom-call(s32[1]{0:T(128)} %bitcast.5.refs_0_, f32[512,128]{1,0:T(8,128)} %bitcast.99), custom_call_target="tpu_custom_call" | custom-call | tf_op jit(solution)/shard_map/coarse_inverse/pallas_call | solution.py:132
  95.5 2.5 %assemble.4 = (f32[2048,128]{1,0:T(8,128)}, f32[48,1024]{1,0:T(8,128)}) custom-call(f32[4,304,128]{2,1,0:T(8,128)} %copy-done.4, f32[4,304,128]{2,1,0:T(8,128)} %collective-permute-done.11.other_ref, s32[2]{0:T(128)} %pad_add_fusion.place_ref), custom_call_target="tpu_custom_call" | custom-call | tf_op jit(solution)/shard_map/assemble/pallas_call | solution.py:181
  101.0 1.8 %convolution_subtract_fusion.4 = f32[8,128]{1,0:T(8,128)S(1)} fusion(f32[8,128]{1,0:T(8,128)S(1)} %fusion.88, f32[2048,128]{1,0:T(8,128)} %get-tuple-element.13, f32[24,2048]{1,0:T(8,128)S(1)} %select_maximum_fusion), kind=kOutput, calls=%fused_computation.13 | convolution fusion | flops 25166848 | bytes 1122304 | tf_op jit(solution)/shard_map/dot_general | solution.py:19
  103.7 4.8 %all-to-all-start.1 = ((f32[32,16,128]{2,1,0:T(8,128)}), f32[32,16,128]{2,1,0:T(8,128)S(1)}, u32[]{:S(2)}, u32[]{:S(2)}) async-start(f32[32,16,128]{2,1,0:T(8,128)} %broadcast_in_dim.16), calls=%async_computation.1 | async-start | bytes 524288 | tf_op jit(solution)/shard_map/all_to_all | solution.py:203
  109.9 1.9 %fusion.112 = f32[256,128]{1,0:T(8,128)} fusion(f32[40,256]{1,0:T(8,128)} %fusion.6, f32[40,128]{1,0:T(8,128)} %get-tuple-element.11), kind=kOutput, calls=%fused_computation.178 | convolution fusion | flops 15728640 | bytes 192512 | tf_op jit(solution)/shard_map/dot_general | solution.py:19
  111.8 2.3 %fusion.24 = (f32[128]{0:T(128)}, f32[128,128]{1,0:T(8,128)}) fusion(f32[256,128]{1,0:T(8,128)S(1)} %convolution_subtract_fusion.2, f32[128,128]{1,0:T(8,128)} %copy-done.13, f32[40,128]{1,0:T(8,128)} %get-tuple-element.11, f32[8,128]{1,0:T(8,128)S(1)} %get-tuple-element.44, f32[8,128]{1,0:T(8,128)S(1)} %get-tuple-element.43, f32[8,128]{1,0:T(8,128)S(1)} %broadcast.61), kind=kOutput, calls=%fused_computation.56 | convolution fusion | flops 4773760 | bytes 221696 | tf_op jit(solution)/shard_map/dot_general | solution.py:221
  114.1 4.9 %all-to-all-done.1 = f32[32,16,128]{2,1,0:T(8,128)S(1)} async-done(((f32[32,16,128]{2,1,0:T(8,128)}), f32[32,16,128]{2,1,0:T(8,128)S(1)}, u32[]{:S(2)}, u32[]{:S(2)}) %all-to-all-start.1) | async-done | bytes 262176 | tf_op jit(solution)/shard_map/all_to_all | solution.py:203
  121.2 2.7 %fusion.4 = f32[256,128]{1,0:T(8,128)S(1)} fusion(f32[256,128]{1,0:T(8,128)S(1)} %fusion.113, f32[256,128]{1,0:T(8,128)} %fusion.112, f32[2048,128]{1,0:T(8,128)S(1)} %copy-done.2, f32[256,2048]{1,0:T(8,128)S(1)} %bitcast.91), kind=kOutput, calls=%fused_computation.6 | convolution fusion | flops 805371904 | bytes 3538944 | tf_op jit(solution)/shard_map/dot_general | solution.py:19
  125.1 8.6 %all-to-all-start.2 = ((f32[256,2,128]{2,1,0:T(2,128)}), f32[256,2,128]{2,1,0:T(2,128)S(1)}, u32[]{:S(2)}, u32[]{:S(2)}) async-start(f32[256,2,128]{2,1,0:T(2,128)} %broadcast_in_dim.17), calls=%async_computation.2 | async-start | bytes 524288 | tf_op jit(solution)/shard_map/all_to_all | solution.py:203
  138.0 2.2 %collective-permute-start.17 = (f32[24,128]{0,1:T(8,128)S(1)}, f32[24,128]{0,1:T(8,128)S(1)}, u32[]{:S(2)}, u32[]{:S(2)}) collective-permute-start(f32[24,128]{0,1:T(8,128)S(1)} %get-tuple-element.52), channel_id=1, source_target_pairs={{0,1},{1,0},{2,3},{3,2},{4,5},{5,4},{6,7},{7,6},{8,9},{9,8},{10,11... | collective-permute-start | bytes 36872 | tf_op jit(solution)/shard_map/ppermute | solution.py:198
  143.6 5.5 %all-to-all-done.2 = f32[256,2,128]{2,1,0:T(2,128)S(1)} async-done(((f32[256,2,128]{2,1,0:T(2,128)}), f32[256,2,128]{2,1,0:T(2,128)S(1)}, u32[]{:S(2)}, u32[]{:S(2)}) %all-to-all-start.2) | async-done | bytes 262176 | tf_op jit(solution)/shard_map/all_to_all | solution.py:203
  (158 shorter events, 38.3 us)
Async XLA Ops:
  0.6 31.9 %copy-start = (f32[1,2,128,2048]{3,2,1,0:T(8,128)S(1)}, f32[1,2,128,2048]{3,2,1,0:T(8,128)}, u32[]{:S(2)}) copy-start(f32[1,2,128,2048]{3,2,1,0:T(8,128)} %param.6) | copy-start | bytes 6291460
  0.6 30.9 %copy-start.24 = (pred[24]{0:T(512)(128)(4,1)S(1)}, pred[24]{0:T(512)(128)(4,1)}, u32[]{:S(2)}) copy-start(pred[24]{0:T(512)(128)(4,1)} %constant.12.clone.1) | copy-start | bytes 76
  3.7 5.4 %collective-permute-start.1 = (f32[136,128]{1,0:T(8,128)S(1)}, f32[136,128]{1,0:T(8,128)S(1)}, u32[]{:S(2)}, u32[]{:S(2)}) collective-permute-start(f32[136,128]{1,0:T(8,128)S(1)} %pad_maximum_fusion.8), channel_id=1, source_target_pairs={{0,8},{8,16},{16,24},{24,32},{32,40},{40,48},{48,56},{56,64},{64,7... | collective-permute-start | bytes 208904 | tf_op jit(solution)/shard_map/ppermute | solution.py:192
  7.8 4.4 %collective-permute-start = (f32[8,128]{1,0:T(8,128)S(1)}, f32[8,128]{1,0:T(8,128)S(1)}, u32[]{:S(2)}, u32[]{:S(2)}) collective-permute-start(f32[8,128]{1,0:T(8,128)S(1)} %get-tuple-element.42), channel_id=1, source_target_pairs={{8,0},{16,8},{24,16},{32,24},{40,32},{48,40},{56,48},{64,56},{72,6... | collective-permute-start | bytes 12296 | tf_op jit(solution)/shard_map/ppermute | solution.py:192
  10.0 36.6 %copy-start.21 = (f32[8,128]{1,0:T(8,128)}, f32[8,128]{1,0:T(8,128)S(1)}, u32[]{:S(2)}) copy-start(f32[8,128]{1,0:T(8,128)S(1)} %get-tuple-element.17) | copy-start | bytes 12292
  12.1 5.6 %collective-permute-start.4 = (f32[288,128]{1,0:T(8,128)S(1)}, f32[288,128]{1,0:T(8,128)S(1)}, u32[]{:S(2)}, u32[]{:S(2)}) collective-permute-start(f32[288,128]{1,0:T(8,128)S(1)} %get-tuple-element.45), channel_id=1, source_target_pairs={{0,6},{2,0},{4,2},{6,4},{1,7},{3,1},{5,3},{7,5},{8,14},{10,8},{12,... | collective-permute-start | bytes 442376 | tf_op jit(solution)/shard_map/ppermute | solution.py:211
  14.6 5.6 %collective-permute-start.3 = (f32[288,128]{1,0:T(8,128)S(1)}, f32[288,128]{1,0:T(8,128)S(1)}, u32[]{:S(2)}, u32[]{:S(2)}) collective-permute-start(f32[288,128]{1,0:T(8,128)S(1)} %get-tuple-element.45), channel_id=1, source_target_pairs={{0,4},{2,6},{4,0},{6,2},{1,5},{3,7},{5,1},{7,3},{8,12},{10,14},{12... | collective-permute-start | bytes 442376 | tf_op jit(solution)/shard_map/ppermute | solution.py:211
  15.1 7.2 %collective-permute-start.2 = (f32[288,128]{1,0:T(8,128)S(1)}, f32[288,128]{1,0:T(8,128)S(1)}, u32[]{:S(2)}, u32[]{:S(2)}) collective-permute-start(f32[288,128]{1,0:T(8,128)S(1)} %get-tuple-element.45), channel_id=1, source_target_pairs={{0,2},{2,4},{4,6},{6,0},{1,3},{3,5},{5,7},{7,1},{8,10},{10,12},{12... | collective-permute-start | bytes 442376 | tf_op jit(solution)/shard_map/ppermute | solution.py:211
  22.4 4.9 %collective-permute-start.5 = (f32[4,288,128]{2,1,0:T(8,128)S(1)}, f32[4,288,128]{2,1,0:T(8,128)S(1)}, u32[]{:S(2)}, u32[]{:S(2)}) collective-permute-start(f32[4,288,128]{2,1,0:T(8,128)S(1)} %pad_maximum_fusion.1.own_ref), channel_id=1, source_target_pairs={{0,1},{1,0},{2,3},{3,2},{4,5},{5,4},{6,7},{7,6},{8,9},{9,8},{10,11... | collective-permute-start | bytes 1769480 | tf_op jit(solution)/shard_map/ppermute | solution.py:198
  38.0 5.1 %collective-permute-start.6 = (f32[152,128]{1,0:T(8,128)S(1)}, f32[152,128]{1,0:T(8,128)S(1)}, u32[]{:S(2)}, u32[]{:S(2)}) collective-permute-start(f32[152,128]{1,0:T(8,128)S(1)} %pad_maximum_fusion.6), channel_id=1, source_target_pairs={{0,8},{8,16},{16,24},{24,32},{32,40},{40,48},{48,56},{56,64},{64,7... | collective-permute-start | bytes 233480 | tf_op jit(solution)/shard_map/ppermute | solution.py:192
  41.2 5.1 %collective-permute-start.7 = (f32[152,128]{1,0:T(8,128)S(1)}, f32[152,128]{1,0:T(8,128)S(1)}, u32[]{:S(2)}, u32[]{:S(2)}) collective-permute-start(f32[152,128]{1,0:T(8,128)S(1)} %pad_maximum_fusion.7), channel_id=1, source_target_pairs={{8,0},{16,8},{24,16},{32,24},{40,32},{48,40},{56,48},{64,56},{72,6... | collective-permute-start | bytes 233480 | tf_op jit(solution)/shard_map/ppermute | solution.py:192
  46.7 5.9 %collective-permute-start.14 = (f32[80,128]{1,0:T(8,128)S(1)}, f32[80,128]{1,0:T(8,128)S(1)}, u32[]{:S(2)}, u32[]{:S(2)}) collective-permute-start(f32[80,128]{1,0:T(8,128)S(1)} %get-tuple-element.33), channel_id=1, source_target_pairs={{0,6},{2,0},{4,2},{6,4},{1,7},{3,1},{5,3},{7,5},{8,14},{10,8},{12,... | collective-permute-start | bytes 122888 | tf_op jit(solution)/shard_map/ppermute | solution.py:211
  47.2 14.5 %copy-start.8 = (f32[128,128]{1,0:T(8,128)}, f32[128,128]{1,0:T(8,128)S(1)}, u32[]{:S(2)}) copy-start(f32[128,128]{1,0:T(8,128)S(1)} %get-tuple-element.26) | copy-start | bytes 196612
  47.2 14.5 %copy-start.9 = (f32[128,128]{1,0:T(8,128)}, f32[128,128]{1,0:T(8,128)S(1)}, u32[]{:S(2)}) copy-start(f32[128,128]{1,0:T(8,128)S(1)} %get-tuple-element.27) | copy-start | bytes 196612
  47.5 14.2 %collective-permute-start.10 = (f32[304,128]{1,0:T(8,128)S(1)}, f32[304,128]{1,0:T(8,128)S(1)}, u32[]{:S(2)}, u32[]{:S(2)}) collective-permute-start(f32[304,128]{1,0:T(8,128)S(1)} %get-tuple-element.25), channel_id=1, source_target_pairs={{0,6},{2,0},{4,2},{6,4},{1,7},{3,1},{5,3},{7,5},{8,14},{10,8},{12,... | collective-permute-start | bytes 466952 | tf_op jit(solution)/shard_map/ppermute | solution.py:211
  48.1 13.6 %collective-permute-start.9 = (f32[304,128]{1,0:T(8,128)S(1)}, f32[304,128]{1,0:T(8,128)S(1)}, u32[]{:S(2)}, u32[]{:S(2)}) collective-permute-start(f32[304,128]{1,0:T(8,128)S(1)} %get-tuple-element.25), channel_id=1, source_target_pairs={{0,4},{2,6},{4,0},{6,2},{1,5},{3,7},{5,1},{7,3},{8,12},{10,14},{12... | collective-permute-start | bytes 466952 | tf_op jit(solution)/shard_map/ppermute | solution.py:211
  50.5 11.2 %collective-permute-start.8 = (f32[304,128]{1,0:T(8,128)S(1)}, f32[304,128]{1,0:T(8,128)S(1)}, u32[]{:S(2)}, u32[]{:S(2)}) collective-permute-start(f32[304,128]{1,0:T(8,128)S(1)} %get-tuple-element.25), channel_id=1, source_target_pairs={{0,2},{2,4},{4,6},{6,0},{1,3},{3,5},{5,7},{7,1},{8,10},{10,12},{12... | collective-permute-start | bytes 466952 | tf_op jit(solution)/shard_map/ppermute | solution.py:211
  50.5 6.5 %collective-permute-start.13 = (f32[80,128]{1,0:T(8,128)S(1)}, f32[80,128]{1,0:T(8,128)S(1)}, u32[]{:S(2)}, u32[]{:S(2)}) collective-permute-start(f32[80,128]{1,0:T(8,128)S(1)} %get-tuple-element.33), channel_id=1, source_target_pairs={{0,4},{2,6},{4,0},{6,2},{1,5},{3,7},{5,1},{7,3},{8,12},{10,14},{12... | collective-permute-start | bytes 122888 | tf_op jit(solution)/shard_map/ppermute | solution.py:211
  52.6 6.7 %collective-permute-start.12 = (f32[80,128]{1,0:T(8,128)S(1)}, f32[80,128]{1,0:T(8,128)S(1)}, u32[]{:S(2)}, u32[]{:S(2)}) collective-permute-start(f32[80,128]{1,0:T(8,128)S(1)} %get-tuple-element.33), channel_id=1, source_target_pairs={{0,2},{2,4},{4,6},{6,0},{1,3},{3,5},{5,7},{7,1},{8,10},{10,12},{12... | collective-permute-start | bytes 122888 | tf_op jit(solution)/shard_map/ppermute | solution.py:211
  59.3 18.5 %copy-start.12 = (f32[4,80,128]{2,1,0:T(8,128)}, f32[4,80,128]{2,1,0:T(8,128)S(1)}, u32[]{:S(2)}) copy-start(f32[4,80,128]{2,1,0:T(8,128)S(1)} %pad_maximum_fusion.3.own_ref) | copy-start | bytes 491524
  59.3 18.5 %collective-permute-start.15 = (f32[4,80,128]{2,1,0:T(8,128)S(1)}, f32[4,80,128]{2,1,0:T(8,128)S(1)}, u32[]{:S(2)}, u32[]{:S(2)}) collective-permute-start(f32[4,80,128]{2,1,0:T(8,128)S(1)} %pad_maximum_fusion.3.own_ref), channel_id=1, source_target_pairs={{0,1},{1,0},{2,3},{3,2},{4,5},{5,4},{6,7},{7,6},{8,9},{9,8},{10,11... | collective-permute-start | bytes 491528 | tf_op jit(solution)/shard_map/ppermute | solution.py:198
  61.8 22.1 %copy-start.4 = (f32[4,304,128]{2,1,0:T(8,128)}, f32[4,304,128]{2,1,0:T(8,128)S(1)}, u32[]{:S(2)}) copy-start(f32[4,304,128]{2,1,0:T(8,128)S(1)} %pad_maximum_fusion.own_ref) | copy-start | bytes 1867780
  61.8 33.7 %collective-permute-start.11 = (f32[4,304,128]{2,1,0:T(8,128)S(1)}, f32[4,304,128]{2,1,0:T(8,128)}, u32[]{:S(2)}, u32[]{:S(2)}) collective-permute-start(f32[4,304,128]{2,1,0:T(8,128)S(1)} %pad_maximum_fusion.own_ref), channel_id=1, source_target_pairs={{0,1},{1,0},{2,3},{3,2},{4,5},{5,4},{6,7},{7,6},{8,9},{9,8},{10,11... | collective-permute-start | bytes 1867784 | tf_op jit(solution)/shard_map/ppermute | solution.py:198
  62.7 26.6 %all-to-all-start = ((f32[32,16,128]{2,1,0:T(8,128)}), f32[32,16,128]{2,1,0:T(8,128)S(1)}, u32[]{:S(2)}, u32[]{:S(2)}) async-start(f32[32,16,128]{2,1,0:T(8,128)} %broadcast_in_dim.15), calls=%async_computation | async-start | bytes 524288 | tf_op jit(solution)/shard_map/all_to_all | solution.py:203
  98.0 23.2 %copy-start.2 = (f32[2048,128]{1,0:T(8,128)S(1)}, f32[2048,128]{1,0:T(8,128)}, u32[]{:S(2)}) copy-start(f32[2048,128]{1,0:T(8,128)} %get-tuple-element.13) | copy-start | bytes 3145732
  103.7 15.3 %all-to-all-start.1 = ((f32[32,16,128]{2,1,0:T(8,128)}), f32[32,16,128]{2,1,0:T(8,128)S(1)}, u32[]{:S(2)}, u32[]{:S(2)}) async-start(f32[32,16,128]{2,1,0:T(8,128)} %broadcast_in_dim.16), calls=%async_computation.1 | async-start | bytes 524288 | tf_op jit(solution)/shard_map/all_to_all | solution.py:203
  125.1 23.9 %all-to-all-start.2 = ((f32[256,2,128]{2,1,0:T(2,128)}), f32[256,2,128]{2,1,0:T(2,128)S(1)}, u32[]{:S(2)}, u32[]{:S(2)}) async-start(f32[256,2,128]{2,1,0:T(2,128)} %broadcast_in_dim.17), calls=%async_computation.2 | async-start | bytes 524288 | tf_op jit(solution)/shard_map/all_to_all | solution.py:203
  138.0 3.5 %collective-permute-start.17 = (f32[24,128]{0,1:T(8,128)S(1)}, f32[24,128]{0,1:T(8,128)S(1)}, u32[]{:S(2)}, u32[]{:S(2)}) collective-permute-start(f32[24,128]{0,1:T(8,128)S(1)} %get-tuple-element.52), channel_id=1, source_target_pairs={{0,1},{1,0},{2,3},{3,2},{4,5},{5,4},{6,7},{7,6},{8,9},{9,8},{10,11... | collective-permute-start | bytes 36872 | tf_op jit(solution)/shard_map/ppermute | solution.py:198
  140.2 9.8 %collective-permute-start.16 = (f32[128,128]{1,0:T(8,128)S(1)}, f32[128,128]{1,0:T(8,128)S(1)}, u32[]{:S(2)}, u32[]{:S(2)}) collective-permute-start(f32[128,128]{1,0:T(8,128)S(1)} %slice.233), channel_id=1, source_target_pairs={{8,0},{16,8},{24,16},{32,24},{40,32},{48,40},{56,48},{64,56},{72,6... | collective-permute-start | bytes 196616 | tf_op jit(solution)/shard_map/ppermute | solution.py:192
  141.5 8.4 %collective-permute-start.20 = (f32[24,128]{0,1:T(8,128)S(1)}, f32[24,128]{0,1:T(8,128)S(1)}, u32[]{:S(2)}, u32[]{:S(2)}) collective-permute-start(f32[24,128]{0,1:T(8,128)S(1)} %add_dynamic-update-slice_fusion), channel_id=1, source_target_pairs={{0,6},{2,0},{4,2},{6,4},{1,7},{3,1},{5,3},{7,5},{8,14},{10,8},{12,... | collective-permute-start | bytes 36872 | tf_op jit(solution)/shard_map/ppermute | solution.py:211
  142.4 7.6 %collective-permute-start.19 = (f32[24,128]{0,1:T(8,128)S(1)}, f32[24,128]{0,1:T(8,128)S(1)}, u32[]{:S(2)}, u32[]{:S(2)}) collective-permute-start(f32[24,128]{0,1:T(8,128)S(1)} %add_dynamic-update-slice_fusion), channel_id=1, source_target_pairs={{0,4},{2,6},{4,0},{6,2},{1,5},{3,7},{5,1},{7,3},{8,12},{10,14},{12... | collective-permute-start | bytes 36872 | tf_op jit(solution)/shard_map/ppermute | solution.py:211
  143.0 7.0 %collective-permute-start.18 = (f32[24,128]{0,1:T(8,128)S(1)}, f32[24,128]{0,1:T(8,128)S(1)}, u32[]{:S(2)}, u32[]{:S(2)}) collective-permute-start(f32[24,128]{0,1:T(8,128)S(1)} %add_dynamic-update-slice_fusion), channel_id=1, source_target_pairs={{0,2},{2,4},{4,6},{6,0},{1,3},{3,5},{5,7},{7,1},{8,10},{10,12},{12... | collective-permute-start | bytes 36872 | tf_op jit(solution)/shard_map/ppermute | solution.py:211
  (17 other events, 63.4 us)

commit v3 on v2

--- a/solution.py
+++ b/solution.py
@@ -143,48 +143,163 @@
     )(sub, sent)
 
 
-def assemble_kernel(count, rows, own_ref, other_ref, place_ref, traces_ref, extra_ref):
-    x, core = place_ref[0], place_ref[1]
-    head = 0 if traces_ref is None else 2 * rows
+def each_piece(count, own_ref, other_ref, place_ref, copy):
     for q in range(count):
-        d = lax.rem(x - q + count, count)
+        d = lax.rem(place_ref[0] - q + count, count)
         for c in range(2):
-            at = 2 * q + c
-
-            def copy(ref):
-                if traces_ref is not None:
-                    for face in range(2):
-                        start = (face * 2 * count + at) * rows
-                        traces_ref[start : start + rows, :] = ref[d, face * rows : (face + 1) * rows, :]
-                extra_ref[:, at * 128 : (at + 1) * 128] = ref[d, head:, :]
-
-            @pl.when(core == c)
+
+            @pl.when(place_ref[1] == c)
             def _():
-                copy(own_ref)
-
-            @pl.when(core != c)
+                copy(own_ref, d, 2 * q + c)
+
+            @pl.when(place_ref[1] != c)
             def _():
-                copy(other_ref)
-
-
-def assemble(own, other, place, rows, with_traces):
-    count, pieces, _ = own.shape
-    vmem = pl.BlockSpec(memory_space=pltpu.VMEM)
-    head = 2 * rows if with_traces else 0
-    extra = jax.ShapeDtypeStruct((pieces - head, 2 * count * 128), jnp.float32)
-    traces = jax.ShapeDtypeStruct((2 * rows * 2 * count, 128), jnp.float32)
-
-    def kernel(own_ref, other_ref, place_ref, *outs):
-        outs = outs if with_traces else (None, *outs)
-        assemble_kernel(count, rows, own_ref, other_ref, place_ref, *outs)
-
+                copy(other_ref, d, 2 * q + c)
+
+
+VMEM = pl.BlockSpec(memory_space=pltpu.VMEM)
+SMEM = pl.BlockSpec(memory_space=pltpu.SMEM)
+
+
+def shapes(*dims):
+    return [jax.ShapeDtypeStruct(d, jnp.float32) for d in dims]
+
+
+def stiff_kernel(count, rows, own_ref, other_ref, place_ref, rest_ref, stiff_ref, up_ref, down_ref, basis_ref,
+                 sent_ref, ext_ref):
+    face = 2 * count * rows
+    basis_ref[2 * PAD :, :face] = jnp.zeros((PAD, face), jnp.float32)
+    basis_ref[:PAD, face:] = jnp.zeros((PAD, face), jnp.float32)
+
+    def copy(ref, d, at):
+        for side in range(2):
+            start = side * face + at * rows
+            ext_ref[start : start + rows, :128] = ref[d, side * rows : (side + 1) * rows, :]
+        lanes = slice(at * rows, (at + 1) * rows)
+        basis_ref[: 2 * PAD, lanes] = ref[d, 2 * rows : 2 * rows + 2 * PAD, :]
+        lanes = slice(face + at * rows, face + (at + 1) * rows)
+        basis_ref[PAD:, lanes] = ref[d, 2 * rows + 2 * PAD :, :]
+
+    each_piece(count, own_ref, other_ref, place_ref, copy)
+    filler = jnp.zeros((128 - 3 * PAD, 128), jnp.float32)
+    for at in range(2 * face // 128):
+        lanes = slice(at * 128, (at + 1) * 128)
+        ext_ref[lanes, 128:] = jnp.concatenate([basis_ref[:, lanes], filler], 0).T
+    ext = ext_ref[...]
+    image = 0.25 * dot(stiff_ref[...], ext)
+    modes_image = image[:, 128:].T[: 3 * PAD]
+    up_ref[:rows] = image[rows:, :128]
+    up_ref[rows:] = modes_image[:, rows:]
+    down_ref[:rows] = image[:rows, :128]
+    down_ref[rows:] = modes_image[:, :rows]
+    coarse = dot(basis_ref[PAD : 2 * PAD, :], ext)
+    coarse = jnp.concatenate([coarse[:, :128], coarse[:, 128:] + rest_ref[...]], 0)
+    for t in range(sent_ref.shape[0]):
+        sent_ref[t] = coarse
+
+
+def apply_stiffness(own, other, place, rest, stiff, subs):
+    count, rows = own.shape[0], stiff.shape[0] // 2
+    face = 2 * count * rows
     return pl.pallas_call(
-        kernel,
-        out_shape=[traces, extra] if with_traces else [extra],
-        in_specs=[vmem, vmem, pl.BlockSpec(memory_space=pltpu.SMEM)],
-        out_specs=[vmem] * (2 if with_traces else 1),
-        name="assemble",
-    )(own, other, place)
+        lambda *refs: stiff_kernel(count, rows, *refs),
+        out_shape=shapes(
+            (rows + 3 * PAD, 128), (rows + 3 * PAD, 128), (3 * PAD, 2 * face), (subs, 2 * PAD, 128)
+        ),
+        in_specs=[VMEM, VMEM, SMEM, VMEM, VMEM],
+        out_specs=[VMEM] * 4,
+        scratch_shapes=[pltpu.VMEM((2 * face, 256), jnp.float32)],
+        name="apply_stiffness",
+    )(own, other, place, rest, stiff)
+
+
+def search_kernel(count, rows, share, own_ref, other_ref, place_ref, basis_ref, weights_ref, traces_ref,
+                  modes_ref, sent_ref, sums_ref):
+    face = 2 * count * rows
+    wide = NEAR * PAD
+    head = 2 * rows
+    sums_ref[...] = own_ref[0, head : head + 7 * PAD, :] + other_ref[0, head : head + 7 * PAD, :]
+    for d in range(1, count):
+        sums_ref[...] += own_ref[d, head : head + 7 * PAD, :] + other_ref[d, head : head + 7 * PAD, :]
+
+    def copy(ref, d, at):
+        for side in range(2):
+            start = side * face + at * rows
+            traces_ref[start : start + rows, :] = ref[d, side * rows : (side + 1) * rows, :]
+            low = head + 7 * PAD + side * wide
+            modes_ref[:, start : start + rows] = ref[d, low : low + wide, :]
+
+    each_piece(count, own_ref, other_ref, place_ref, copy)
+    weights = jnp.concatenate([weights_ref[...], jnp.zeros((128 - wide, 128), jnp.float32)], 0)
+    change = dot(sums_ref[3 * PAD :, :], weights)
+    rhs = dot(basis_ref[PAD : 2 * PAD, :], traces_ref[...]) - change[3 * PAD :]
+    flex_search = sums_ref[: 3 * PAD, :] - change[: 3 * PAD]
+    lane = lax.broadcasted_iota(jnp.int32, (PAD, 128), 1)
+    mine = (place_ref[0] * 2 + place_ref[1]) * share
+    tail = jnp.zeros((PAD, 128), jnp.float32)
+    for b in range(3):
+        block = flex_search[b * PAD : (b + 1) * PAD]
+        block = pltpu.roll(block, lax.rem(128 - mine + b * share, 128), 1)
+        tail = jnp.where(lane // share == b, block, tail)
+    for b in range(3):
+        low = 3 * share + b * 3 * PAD
+        block = sums_ref[(3 + b) * PAD : (4 + b) * PAD, :]
+        block = pltpu.roll(block, (low - wide) % 128, 1)
+        tail = jnp.where((lane >= low) & (lane < low + 3 * PAD), block, tail)
+    sent = jnp.concatenate([rhs, tail], 0)
+    for t in range(sent_ref.shape[0]):
+        sent_ref[t] = sent
+
+
+def order_search(own, other, place, basis, weights, subs, rows):
+    count = own.shape[0]
+    face = 2 * count * rows
+    return pl.pallas_call(
+        lambda *refs: search_kernel(count, rows, 128 // (2 * count), *refs),
+        out_shape=shapes((2 * face, 128), (NEAR * PAD, 2 * face), (subs, 2 * PAD, 128)),
+        in_specs=[VMEM, VMEM, SMEM, VMEM, VMEM],
+        out_specs=[VMEM] * 3,
+        scratch_shapes=[pltpu.VMEM((7 * PAD, 128), jnp.float32)],
+        name="order_search",
+    )(own, other, place, basis, weights)
+
+
+def direction_kernel(subs, second_ref, near_ref, turned_ref, image_ref, search_ref, res_ref, low_ref, high_ref,
+                     direction_ref, sums_ref):
+    rows = res_ref.shape[0]
+    rhs = jnp.concatenate(
+        [second_ref[pl.ds(i, subs, stride=2 * PAD), :] for i in range(PAD)], axis=0
+    )
+    weights = dot(near_ref[PAD : 4 * PAD, :], rhs)
+    none = jnp.zeros((128 - 6 * PAD, 128), jnp.float32)
+    gap = jnp.zeros((3 * PAD, 128), jnp.float32)
+    both = jnp.concatenate(
+        [
+            jnp.concatenate([weights, gap, none], 0),
+            jnp.concatenate([gap, weights, none], 0),
+        ],
+        1,
+    )
+    change = dot(turned_ref[...], both)
+    image = image_ref[...] - change[:, :128]
+    direction = search_ref[...] - change[:, 128:]
+    low_ref[...] = image[:rows]
+    high_ref[...] = image[rows:]
+    direction_ref[...] = direction[rows:]
+    first = jnp.sum(res_ref[...] * search_ref[rows:, :], axis=0, keepdims=True)
+    second = jnp.sum(direction * image, axis=0, keepdims=True)
+    sums_ref[...] = jnp.concatenate([first, second], 0)
+
+
+def project_direction(second, near, turned, image, search, res, subs):
+    rows = res.shape[0]
+    return pl.pallas_call(
+        lambda *refs: direction_kernel(subs, *refs),
+        out_shape=shapes((rows, 128), (rows, 128), (rows, 128), (2, 128)),
+        in_specs=[VMEM] * 6,
+        out_specs=[VMEM] * 4,
+        name="project_direction",
+    )(second, near, turned, image, search, res)
 
 
 def moved_along(block, distance):
@@ -212,9 +327,13 @@
     ]
 
 
-def gathered(piece, place, rows, with_traces=True):
+def to_all(values, axis):
+    return lax.all_to_all(values, axis, 0, 0, tiled=True)
+
+
+def gathered(piece):
     own = jnp.stack(along_x(piece))
-    return assemble(own, core_swap(own), place, rows, with_traces)
+    return own, core_swap(own)
 
 
 def spread(part, weights):
@@ -246,15 +365,6 @@
     field_before, right_before = from_before[:rows], from_before[rows:]
     left_in = left * inner
     piece = jnp.concatenate([-field_before, field, -right_before, left_in, right, -left_after], 0)
-    gap_traces, faces = gathered(piece, place, rows)
-    none = jnp.zeros((PAD, face), jnp.float32)
-    basis = jnp.concatenate(
-        [
-            jnp.concatenate([faces[: 2 * PAD], none], 0),
-            jnp.concatenate([none, faces[2 * PAD :]], 0),
-        ],
-        1,
-    )
     none = jnp.zeros_like(left)
     own_basis = jnp.concatenate(
         [
@@ -263,73 +373,58 @@
         ],
         1,
     )
-    here = basis[PAD : 2 * PAD]
     rest = jnp.pad(
-        jnp.eye(PAD, dtype=jnp.float32) * (1.0 - active)[:, None], ((0, 0), (PAD, PAD))
-    )
-    blocks = dot_nt(here, basis) + rest
-    rhs = dot(here, gap_traces)
-    sent = jnp.concatenate([rhs, jnp.pad(blocks, ((0, 0), (0, 128 - 3 * PAD)))], 0)
-
-    image = 0.25 * dot(stiff, gap_traces)
-    modes_image = 0.25 * dot_nt(basis, stiff)
-    first = from_all(sent, SUB).reshape(subs * 2 * PAD, 128)
-    before = moved_along(jnp.concatenate([image[rows:], modes_image[:, rows:]], 0), 1)
-    after = moved_along(jnp.concatenate([image[:rows], modes_image[:, :rows]], 0), -1)
-    top = (image[:rows] - before[:rows]) * inner
-    bottom = (image[rows:] - after[:rows]) * live
+        jnp.eye(PAD, dtype=jnp.float32) * (1.0 - active)[:, None], ((0, 0), (PAD, 128 - 2 * PAD))
+    )
+    up, down, basis, sent = apply_stiffness(*gathered(piece), place, rest, stiff, subs)
+    image, modes_image = (down[:rows], up[:rows]), (down[rows:], up[rows:])
+    first = to_all(sent, SUB).reshape(subs * 2 * PAD, 128)
+    before = moved_along(up, 1)
+    after = moved_along(down, -1)
+    top = (image[0] - before[:rows]) * inner
+    bottom = (image[1] - after[:rows]) * live
     own_traces = jnp.concatenate([top, bottom], 0)
     gone = jnp.zeros((PAD, rows), jnp.float32)
-    modes_top = jnp.concatenate([gone, modes_image[:, :rows], gone], 0)
+    modes_top = jnp.concatenate([gone, modes_image[0], gone], 0)
     modes_top = modes_top - jnp.concatenate([before[rows:], gone, gone], 0)
-    modes_bottom = jnp.concatenate([gone, modes_image[:, rows:], gone], 0)
+    modes_bottom = jnp.concatenate([gone, modes_image[1], gone], 0)
     modes_bottom = modes_bottom - jnp.concatenate([gone, gone, after[rows:]], 0)
     own_modes = jnp.concatenate([modes_top * inner, modes_bottom * live], 1)
 
     flex_modes = dot_nt(basis, flex)
     small = dot_nt(flex_modes, jnp.concatenate([own_modes, own_basis], 0))
-    cross = jnp.pad(dot_nt(own_basis[PAD : 2 * PAD], own_modes), ((0, 2 * PAD), (0, 0)))
-    small = jnp.concatenate([small, cross], 1)
+    cross = dot_nt(own_basis[PAD : 2 * PAD], own_modes)
     small = jnp.pad(small, ((0, 0), (0, 128 - small.shape[1])))
-    piece = jnp.concatenate([own_traces, dot(flex_modes, own_traces), small], 0)
-    search_traces, extra = gathered(piece, place, rows)
-    extra = extra.reshape(6 * PAD, lanes, 128).sum(1)
-    flex_search, small = extra[: 3 * PAD], extra[3 * PAD :]
-    wide = NEAR * PAD
-
+    cross = jnp.pad(cross, ((0, 0), (0, 128 - cross.shape[1])))
+    piece = jnp.concatenate(
+        [
+            own_traces, dot(flex_modes, own_traces), small, cross, own_modes[:, :rows],
+            own_modes[:, rows:],
+        ],
+        0,
+    )
+    pieces = gathered(piece)
     inverse, near, weights = coarse_inverse(sub.astype(jnp.int32)[None], first, subs, mode_count)
-    near = near[PAD : 4 * PAD]
-    rhs = dot(here, search_traces) - dot(small[:PAD, wide + 3 * PAD : 2 * wide + 3 * PAD], weights)
-    flex_search = flex_search - dot(small[:, :wide], weights)
+    search_traces, modes_traces, sent = order_search(*pieces, place, basis, weights, subs, rows)
     mine = (place[0] * 2 + place[1]) * (loads // lanes)
     share = loads // lanes
-
-    def folded(block):
-        return jnp.concatenate([block[b * PAD : (b + 1) * PAD] for b in range(3)], 1)
-
-    flex_search = lax.dynamic_slice_in_dim(flex_search, mine, share, 1)
-    last = jnp.concatenate([folded(flex_search), folded(small[:, wide : wide + 3 * PAD])], 1)
-    last = jnp.pad(last, ((0, 0), (0, 128 - last.shape[1])))
-    second = from_all(jnp.concatenate([rhs, last], 0), SUB)
-
-    (modes_traces,) = gathered(
-        jnp.concatenate([own_modes[:, :rows], own_modes[:, rows:]], 0), place, rows, False
-    )
-    modes_traces = jnp.concatenate([modes_traces[:wide], modes_traces[wide:]], 1)
+    second = to_all(sent, SUB)
+
     image = dot(flex, search_traces) - dot(dot_nt(flex, modes_traces), weights)
     own_search = own_traces - spread(own_modes, weights)
     own_res = field - spread(own_basis[:, rows:], weights[PAD : 4 * PAD])
 
+    turned = jnp.concatenate([flex_modes, own_basis], 0)
+    turned = jnp.pad(turned, ((0, 128 - 6 * PAD), (0, 0))).T
+    low, high, direction, sums = project_direction(
+        second.reshape(subs * 2 * PAD, 128), near, turned, image, own_search, own_res, subs
+    )
+    totals = from_all(sums, ALL).sum(0)
+
+    low, second = lax.optimization_barrier((low, second))
+    near = near[PAD : 4 * PAD]
+    after = moved_along(low, -1)
     all_rhs = second[:, :PAD].transpose(1, 0, 2).reshape(PAD * subs, loads)
-    weights = dot(near, all_rhs)
-    image = image - spread(flex_modes, weights)
-    direction = own_search - spread(own_basis, weights)
-    sums = jnp.stack(
-        [jnp.sum(own_res * own_search[rows:], 0), jnp.sum(direction * image, 0)], 0
-    )
-    totals = from_all(sums, ALL).sum(0)
-
-    after = moved_along(image[:rows], -1)
     my_rhs = lax.dynamic_slice_in_dim(all_rhs, mine, share, 1)
     my_weights = dot(inverse, my_rhs).reshape(PAD, subs, share).transpose(1, 0, 2)
     my_weights = jnp.pad(my_weights, ((1, 1), (0, 0), (0, 0)))
@@ -355,9 +450,9 @@
     )
     weights = weights + core_swap(weights)
     weights = sum(along_x(weights))
-    own_image = (image[rows:] - after) * live - spread(own_basis[:, rows:], weights)
+    own_image = (high - after) * live - spread(own_basis[:, rows:], weights)
     step = totals[0] / totals[1]
-    return (step * direction[rows:])[None], (own_res - step * own_image)[None]
+    return (step * direction)[None], (own_res - step * own_image)[None]
 
 
 def solution(mesh):

time: 153 us -> 139 us (0.908)
  matrix products: 27.8 us -> 17.5 us
  waiting for transfers between devices: 34.1 us -> 26.4 us
  Pallas kernels: 12.1 us -> 16.5 us
  local copies, waits for them, and re-layouts: 10 us -> 7.23 us
  starting transfers between devices: 59.8 us -> 62.2 us
  other arithmetic: 4.99 us -> 6.57 us
    all_to_all x0 -> x2, starting transfers between devices: none -> 21 us  [to_all(): return lax.all_to_all(values, axis, 0, 0, tiled=True)]
    all_to_all x3 -> x1, starting transfers between devices: 28.5 us -> 8.8 us  [from_all(): lax.all_to_all(jnp.broadcast_to(value[None], (count, *value.shape)), axis...]
    all_to_all x0 -> x2, waiting for transfers between devices: none -> 11.1 us  [to_all(): return lax.all_to_all(values, axis, 0, 0, tiled=True)]
    dot_general x11 -> x5, matrix products: 13.3 us -> 4.54 us  [dot(): return jnp.dot(a, b, precision=HIGH, preferred_element_type=jnp.float32)]
    all_to_all x3 -> x1, waiting for transfers between devices: 15.8 us -> 7.63 us  [from_all(): lax.all_to_all(jnp.broadcast_to(value[None], (count, *value.shape)), axis...]
    ppermute x12 -> x9, waiting for transfers between devices: 11.9 us -> 3.75 us  [along_x(): lax.ppermute(piece, 'x', [(i, (i + d) % n) for i in range(n)])]
    pallas_call x3, Pallas kernels: 6.76 us -> 11.1 us  [the longest x1 5.83 us: apply_stiffness(): pl.pallas_call(lambda *refs: stiff_kernel(count, rows, *refs), out_shape=...]
    slice x8 -> x2, local copies, waits for them, and re-layouts: 2.11 us -> 0.01 us  [per_device(): image, modes_image = ((down[:rows], up[:rows]), (down[rows:], up[rows:]))]
  transfers between devices with their start and end apart: 24 -> 20, of which waited for: 11 -> 9; matrix products, arithmetic and copies ran while one was open for 12% -> 12% of each run, Pallas kernels for 5% -> 4%
where the time goes in v3:
time: 139 us; the launch traced here: 138 us
  starting transfers between devices  62.2 us (45%)
  waiting for transfers between devices  26.4 us (19%)
  matrix products  17.5 us (13%)
  Pallas kernels  16.5 us (12%)
  local copies, waits for them, and re-layouts  7.23 us (5%)
  other arithmetic  6.57 us (5%)
  between operations  2.11 us (2%)
    all_to_all x2, starting transfers between devices, to_all(): return lax.all_to_all(values, axis, 0, 0, tiled=True)  21 us
    ppermute x9, starting transfers between devices, along_x(): lax.ppermute(piece, 'x', [(i, (i + d) % n) for i in range(n)])  12.3 us
    ppermute x5, starting transfers between devices, moved_along(): lax.ppermute(block, SUB, [(i - distance, i) for i in range(n) if 0 <= i -...  11.2 us
    all_to_all x2, waiting for transfers between devices, to_all(): return lax.all_to_all(values, axis, 0, 0, tiled=True)  11.1 us
    ppermute x3, starting transfers between devices, core_swap(): return lax.ppermute(block, 'c', [(0, 1), (1, 0)])  8.9 us
    all_to_all x1, starting transfers between devices, from_all(): lax.all_to_all(jnp.broadcast_to(value[None], (count, *value.shape)), axis...  8.8 us
    all_to_all x1, waiting for transfers between devices, from_all(): lax.all_to_all(jnp.broadcast_to(value[None], (count, *value.shape)), axis...  7.63 us
    dot_general x4, matrix products, dot_nt(): lax.dot_general(a, b, (((1,), (1,)), ((), ())), precision=HIGH, preferred...  5.99 us
  transfers between devices with their start and end apart: 20, of which 9 were waited for; matrix products, arithmetic and copies ran while one was open for 12% of the time, Pallas kernels for 4%

profile of v3, /device:TPU:1, one launch (start us, length us, event | category | flops | bytes accessed | tf_op | source)
XLA Modules:
  0.0 138.4 jit_solution(2814002941674262658)
XLA Ops:
  3.1 4.0 %collective-permute-start = (f32[136,128]{1,0:T(8,128)S(1)}, f32[136,128]{1,0:T(8,128)S(1)}, u32[]{:S(2)}, u32[]{:S(2)}) collective-permute-start(f32[136,128]{1,0:T(8,128)S(1)} %pad_maximum_fusion.5), channel_id=1, source_target_pairs={{0,8},{8,16},{16,24},{24,32},{32,40},{40,48},{48,56},{56,64},{64,7... | collective-permute-start | bytes 208904 | tf_op jit(solution)/shard_map/ppermute | solution.py:307
  7.1 1.3 collective-permute-start.1
  9.4 2.1 %collective-permute-done.1 = f32[8,128]{1,0:T(8,128)S(1)} collective-permute-done((f32[8,128]{1,0:T(8,128)S(1)}, f32[8,128]{1,0:T(8,128)S(1)}, u32[]{:S(2)}, u32[]{:S(2)}) %collective-permute-start.1) | collective-permute-done | bytes 4128 | tf_op jit(solution)/shard_map/ppermute | solution.py:307
  12.7 2.5 %collective-permute-start.3 = (f32[288,128]{1,0:T(8,128)S(1)}, f32[288,128]{1,0:T(8,128)S(1)}, u32[]{:S(2)}, u32[]{:S(2)}) collective-permute-start(f32[288,128]{1,0:T(8,128)S(1)} %get-tuple-element.51), channel_id=1, source_target_pairs={{0,4},{2,6},{4,0},{6,2},{1,5},{3,7},{5,1},{7,3},{8,12},{10,14},{12... | collective-permute-start | bytes 442376 | tf_op jit(solution)/shard_map/ppermute | solution.py:326
  16.7 3.2 %collective-permute-done.3 = f32[288,128]{1,0:T(8,128)S(1)} collective-permute-done((f32[288,128]{1,0:T(8,128)S(1)}, f32[288,128]{1,0:T(8,128)S(1)}, u32[]{:S(2)}, u32[]{:S(2)}) %collective-permute-start.3) | collective-permute-done | bytes 147488 | tf_op jit(solution)/shard_map/ppermute | solution.py:326
  20.1 3.2 %collective-permute-start.5 = (f32[4,288,128]{2,1,0:T(8,128)S(1)}, f32[4,288,128]{2,1,0:T(8,128)}, u32[]{:S(2)}, u32[]{:S(2)}) collective-permute-start(f32[4,288,128]{2,1,0:T(8,128)S(1)} %pad_maximum_fusion.1.refs_0_), channel_id=1, source_target_pairs={{0,1},{1,0},{2,3},{3,2},{4,5},{5,4},{6,7},{7,6},{8,9},{9,8},{10,11... | collective-permute-start | bytes 1769480 | tf_op jit(solution)/shard_map/ppermute | solution.py:313
  25.0 5.8 %apply_stiffness.1 = (f32[152,128]{1,0:T(8,128)}, f32[152,128]{1,0:T(8,128)}, f32[24,2048]{1,0:T(8,128)}, f32[32,16,128]{2,1,0:T(8,128)}) custom-call(f32[4,288,128]{2,1,0:T(8,128)} %copy-done.4, f32[4,288,128]{2,1,0:T(8,128)} %collective-permute-done.5.refs_1_, s32[2]{0:T(128)} %pad_add_fusion.refs_2_, f32[8,128]{1,0:T(8,128)} %pad.29.refs_3_, ...), custom_call_target="tpu_custom_call" | custom-call | tf_op jit(solution)/shard_map/apply_stiffness/pallas_call | solution.py:204
  30.9 3.3 %collective-permute-start.6 = (f32[152,128]{1,0:T(8,128)}, f32[152,128]{1,0:T(8,128)S(1)}, u32[]{:S(2)}, u32[]{:S(2)}) collective-permute-start(f32[152,128]{1,0:T(8,128)} %get-tuple-element.19), channel_id=1, source_target_pairs={{0,8},{8,16},{16,24},{24,32},{32,40},{40,48},{48,56},{56,64},{64,7... | collective-permute-start | bytes 233480 | tf_op jit(solution)/shard_map/ppermute | solution.py:307
  34.2 1.3 collective-permute-start.7
  35.5 2.7 %fusion.74 = f32[24,256]{1,0:T(8,128)S(1)} fusion(f32[24,2048]{1,0:T(8,128)} %get-tuple-element.20.refs_3_, f32[256,2048]{1,0:T(8,128)S(1)} %bitcast.68), kind=kOutput, calls=%fused_computation.126 | convolution fusion | flops 150994944 | bytes 2318336 | tf_op jit(solution)/shard_map/dot_general | solution.py:23
  38.3 1.3 collective-permute-done.7
  41.7 2.4 %collective-permute-start.9 = (f32[392,128]{1,0:T(8,128)S(1)}, f32[392,128]{1,0:T(8,128)S(1)}, u32[]{:S(2)}, u32[]{:S(2)}) collective-permute-start(f32[392,128]{1,0:T(8,128)S(1)} %constant_dynamic-update-slice_fusion.5), channel_id=1, source_target_pairs={{0,4},{2,6},{4,0},{6,2},{1,5},{3,7},{5,1},{7,3},{8,12},{10,14},{12... | collective-permute-start | bytes 602120 | tf_op jit(solution)/shard_map/ppermute | solution.py:326
  45.2 15.0 %all-to-all-start = ((f32[32,16,128]{2,1,0:T(8,128)}), f32[32,16,128]{2,1,0:T(8,128)S(1)}, u32[]{:S(2)}, u32[]{:S(2)}) async-start(f32[32,16,128]{2,1,0:T(8,128)} %get-tuple-element.21), calls=%async_computation | async-start | bytes 524288 | tf_op jit(solution)/shard_map/all_to_all | solution.py:331
  62.3 3.2 %collective-permute-start.11 = (f32[4,392,128]{2,1,0:T(8,128)S(1)}, f32[4,392,128]{2,1,0:T(8,128)}, u32[]{:S(2)}, u32[]{:S(2)}) collective-permute-start(f32[4,392,128]{2,1,0:T(8,128)S(1)} %pad_maximum_fusion.refs_0_), channel_id=1, source_target_pairs={{0,1},{1,0},{2,3},{3,2},{4,5},{5,4},{6,7},{7,6},{8,9},{9,8},{10,11... | collective-permute-start | bytes 2408456 | tf_op jit(solution)/shard_map/ppermute | solution.py:313
  67.1 3.6 %all-to-all-done = f32[32,16,128]{2,1,0:T(8,128)S(1)} async-done(((f32[32,16,128]{2,1,0:T(8,128)}), f32[32,16,128]{2,1,0:T(8,128)S(1)}, u32[]{:S(2)}, u32[]{:S(2)}) %all-to-all-start) | async-done | bytes 262176 | tf_op jit(solution)/shard_map/all_to_all | solution.py:331
  71.4 5.4 %coarse_inverse.1 = (f32[256,256]{1,0:T(8,128)}, f32[40,256]{1,0:T(8,128)}, f32[40,128]{1,0:T(8,128)}) custom-call(s32[1]{0:T(128)} %bitcast.17.refs_0_, f32[512,128]{1,0:T(8,128)} %bitcast.75), custom_call_target="tpu_custom_call" | custom-call | tf_op jit(solution)/shard_map/coarse_inverse/pallas_call | solution.py:132
  76.8 1.6 %convolution_subtract_fusion.2.refs_5_ = f32[128,128]{1,0:T(8,128)} fusion(f32[128,128]{1,0:T(8,128)S(1)} %multiply_bitcast_fusion.1, f32[40,128]{1,0:T(8,128)} %get-tuple-element.22.refs_4_, f32[8,128]{1,0:T(8,128)} %copy-done.18, f32[8,128]{1,0:T(8,128)} %copy-done.10, f32[8,128]{1,0:T(8,128)} %copy-done.15), kind=kOutput, calls=%fused_computation.7 | convolution fusion | flops 4741120 | bytes 155648 | tf_op jit(solution)/shard_map/dot_general | solution.py:340
  78.4 1.8 %convolution_subtract_fusion.1.refs_4_ = f32[256,128]{1,0:T(8,128)} fusion(f32[40,128]{1,0:T(8,128)} %get-tuple-element.22.refs_4_, f32[128,128]{1,0:T(8,128)S(1)} %get-tuple-element.35, f32[128,128]{1,0:T(8,128)S(1)} %get-tuple-element.37, f32[40,128]{1,0:T(8,128)S(1)} %get-tuple-element.49, f32[40,128]{1,0:T(8,128)S(1)} %get-tuple-element.48), kind=kOutput, calls=%fused_computation.6 | convolution fusion | flops 15804416 | bytes 323584 | tf_op jit(solution)/shard_map/dot_general | solution.py:340
  80.2 2.9 %order_search.1 = (f32[2048,128]{1,0:T(8,128)}, f32[40,2048]{1,0:T(8,128)}, f32[32,16,128]{2,1,0:T(8,128)}) custom-call(f32[4,392,128]{2,1,0:T(8,128)} %copy-done.3, f32[4,392,128]{2,1,0:T(8,128)} %collective-permute-done.11.refs_1_, s32[2]{0:T(128)} %pad_add_fusion.refs_2_, f32[24,2048]{1,0:T(8,128)} %get-tuple-element.20.refs_3_, ...), custom_call_target="tpu_custom_call" | custom-call | tf_op jit(solution)/shard_map/order_search/pallas_call | solution.py:257
  83.1 3.0 %fusion.75 = f32[40,256]{1,0:T(8,128)S(1)} fusion(f32[40,2048]{1,0:T(8,128)} %get-tuple-element.26, f32[256,2048]{1,0:T(8,128)S(1)} %bitcast.70), kind=kOutput, calls=%fused_computation.127 | convolution fusion | flops 251658240 | bytes 2465792 | tf_op jit(solution)/shard_map/dot_general | solution.py:23
  86.1 5.9 %all-to-all-start.1 = ((f32[32,16,128]{2,1,0:T(8,128)}), f32[32,16,128]{2,1,0:T(8,128)S(1)}, u32[]{:S(2)}, u32[]{:S(2)}) async-start(f32[32,16,128]{2,1,0:T(8,128)} %get-tuple-element.23), calls=%async_computation.1 | async-start | bytes 524288 | tf_op jit(solution)/shard_map/all_to_all | solution.py:331
  92.5 2.5 %fusion.3.refs_3_ = f32[256,128]{1,0:T(8,128)} fusion(f32[256,128]{1,0:T(8,128)S(1)} %fusion.76, f32[2048,128]{1,0:T(8,128)S(1)} %copy-done.5, f32[256,2048]{1,0:T(8,128)S(1)} %bitcast.69), kind=kOutput, calls=%fused_computation.5 | convolution fusion | flops 805339136 | bytes 3407872 | tf_op jit(solution)/shard_map/dot_general | solution.py:19
  95.0 7.5 %all-to-all-done.1 = f32[32,16,128]{2,1,0:T(8,128)S(1)} async-done(((f32[32,16,128]{2,1,0:T(8,128)}), f32[32,16,128]{2,1,0:T(8,128)S(1)}, u32[]{:S(2)}, u32[]{:S(2)}) %all-to-all-start.1) | async-done | bytes 262176 | tf_op jit(solution)/shard_map/all_to_all | solution.py:331
  103.2 2.3 %project_direction.1 = (f32[128,128]{1,0:T(8,128)}, f32[128,128]{1,0:T(8,128)}, f32[128,128]{1,0:T(8,128)}, f32[2,128]{1,0:T(2,128)}) custom-call(f32[512,128]{1,0:T(8,128)} %bitcast.71, f32[40,256]{1,0:T(8,128)} %get-tuple-element.24.refs_1_, f32[256,128]{1,0:T(8,128)} %copy.25.refs_2_, f32[256,128]{1,0:T(8,128)} %fusion.3.refs_3_, ...), custom_call_target="tpu_custom_call" | custom-call | tf_op jit(solution)/shard_map/project_direction/pallas_call | solution.py:296
  106.6 1.4 fusion.20
  110.6 8.8 %all-to-all-start.2 = ((f32[256,2,128]{2,1,0:T(2,128)}), f32[256,2,128]{2,1,0:T(2,128)S(1)}, u32[]{:S(2)}, u32[]{:S(2)}) async-start(f32[256,2,128]{2,1,0:T(2,128)} %broadcast_in_dim.11), calls=%async_computation.2 | async-start | bytes 524288 | tf_op jit(solution)/shard_map/all_to_all | solution.py:318
  120.4 2.5 %collective-permute-start.13 = (f32[24,128]{0,1:T(8,128)S(1)}, f32[24,128]{0,1:T(8,128)S(1)}, u32[]{:S(2)}, u32[]{:S(2)}) collective-permute-start(f32[24,128]{0,1:T(8,128)S(1)} %get-tuple-element.52), channel_id=1, source_target_pairs={{0,1},{1,0},{2,3},{3,2},{4,5},{5,4},{6,7},{7,6},{8,9},{9,8},{10,11... | collective-permute-start | bytes 36872 | tf_op jit(solution)/shard_map/ppermute | solution.py:313
  123.0 1.3 collective-permute-start.12
  124.4 1.7 %collective-permute-start.15 = (f32[24,128]{0,1:T(8,128)S(1)}, f32[24,128]{0,1:T(8,128)S(1)}, u32[]{:S(2)}, u32[]{:S(2)}) collective-permute-start(f32[24,128]{0,1:T(8,128)S(1)} %add_dynamic-update-slice_fusion), channel_id=1, source_target_pairs={{0,4},{2,6},{4,0},{6,2},{1,5},{3,7},{5,1},{7,3},{8,12},{10,14},{12... | collective-permute-start | bytes 36872 | tf_op jit(solution)/shard_map/ppermute | solution.py:326
  127.2 7.6 %all-to-all-done.2 = f32[256,2,128]{2,1,0:T(2,128)S(1)} async-done(((f32[256,2,128]{2,1,0:T(2,128)}), f32[256,2,128]{2,1,0:T(2,128)S(1)}, u32[]{:S(2)}, u32[]{:S(2)}) %all-to-all-start.2) | async-done | bytes 262176 | tf_op jit(solution)/shard_map/all_to_all | solution.py:318
  135.1 1.5 %multiply_bitcast_fusion = f32[1,128,128]{2,1,0:T(8,128)} fusion(f32[128,128]{1,0:T(8,128)} %get-tuple-element.28, f32[128]{0:T(128)S(1)} %fusion.63), kind=kLoop, calls=%fused_computation.67 | loop fusion | flops 16384 | bytes 131584 | tf_op jit(solution)/shard_map/broadcast_in_dim | solution.py:455
  136.7 1.8 %subtract_bitcast_fusion = f32[1,128,128]{2,1,0:T(8,128)} fusion(f32[128,128]{1,0:T(8,128)S(1)} %copy-done.7, f32[128,128]{1,0:T(8,128)} %get-tuple-element.29, f32[128,128]{1,0:T(8,128)S(1)} %collective-permute-done.12, f32[128]{0:T(128)S(1)} %fusion.63, f32[]{:T(128)S(6)} %convert_element_type.30, f32[24,128]{0,1:T(8,128)S(1)} %collective-permute-done.16, ...), kind=kOutput, calls=%fused_computation.62 | convolution fusion | flops 4815872 | bytes 324100 | tf_op jit(solution)/shard_map/dot_general | solution.py:340
  (125 shorter events, 22.0 us)
Async XLA Ops:
  0.6 34.9 %copy-start = (f32[1,2,128,2048]{3,2,1,0:T(8,128)S(1)}, f32[1,2,128,2048]{3,2,1,0:T(8,128)}, u32[]{:S(2)}) copy-start(f32[1,2,128,2048]{3,2,1,0:T(8,128)} %param.6) | copy-start | bytes 6291460
  2.2 37.5 %copy-start.10 = (f32[8,128]{1,0:T(8,128)}, f32[8,128]{1,0:T(8,128)S(1)}, u32[]{:S(2)}) copy-start(f32[8,128]{1,0:T(8,128)S(1)} %get-tuple-element.47) | copy-start | bytes 12292
  3.1 5.4 %collective-permute-start = (f32[136,128]{1,0:T(8,128)S(1)}, f32[136,128]{1,0:T(8,128)S(1)}, u32[]{:S(2)}, u32[]{:S(2)}) collective-permute-start(f32[136,128]{1,0:T(8,128)S(1)} %pad_maximum_fusion.5), channel_id=1, source_target_pairs={{0,8},{8,16},{16,24},{24,32},{32,40},{40,48},{48,56},{56,64},{64,7... | collective-permute-start | bytes 208904 | tf_op jit(solution)/shard_map/ppermute | solution.py:307
  7.1 4.4 %collective-permute-start.1 = (f32[8,128]{1,0:T(8,128)S(1)}, f32[8,128]{1,0:T(8,128)S(1)}, u32[]{:S(2)}, u32[]{:S(2)}) collective-permute-start(f32[8,128]{1,0:T(8,128)S(1)} %get-tuple-element.46), channel_id=1, source_target_pairs={{8,0},{16,8},{24,16},{32,24},{40,32},{48,40},{56,48},{64,56},{72,6... | collective-permute-start | bytes 12296 | tf_op jit(solution)/shard_map/ppermute | solution.py:307
  9.3 30.4 %copy-start.22 = (f32[8,128]{1,0:T(8,128)}, f32[8,128]{1,0:T(8,128)S(1)}, u32[]{:S(2)}) copy-start(f32[8,128]{1,0:T(8,128)S(1)} %get-tuple-element.44) | copy-start | bytes 12292
  9.4 30.4 %copy-start.23 = (f32[8,128]{1,0:T(8,128)}, f32[8,128]{1,0:T(8,128)S(1)}, u32[]{:S(2)}) copy-start(f32[8,128]{1,0:T(8,128)S(1)} %get-tuple-element.39) | copy-start | bytes 12292
  11.5 28.3 %copy-start.18 = (f32[8,128]{1,0:T(8,128)}, f32[8,128]{1,0:T(8,128)S(1)}, u32[]{:S(2)}) copy-start(f32[8,128]{1,0:T(8,128)S(1)} %get-tuple-element.50) | copy-start | bytes 12292
  11.5 5.2 %collective-permute-start.2 = (f32[288,128]{1,0:T(8,128)S(1)}, f32[288,128]{1,0:T(8,128)S(1)}, u32[]{:S(2)}, u32[]{:S(2)}) collective-permute-start(f32[288,128]{1,0:T(8,128)S(1)} %get-tuple-element.51), channel_id=1, source_target_pairs={{0,2},{2,4},{4,6},{6,0},{1,3},{3,5},{5,7},{7,1},{8,10},{10,12},{12... | collective-permute-start | bytes 442376 | tf_op jit(solution)/shard_map/ppermute | solution.py:326
  12.7 7.2 %collective-permute-start.3 = (f32[288,128]{1,0:T(8,128)S(1)}, f32[288,128]{1,0:T(8,128)S(1)}, u32[]{:S(2)}, u32[]{:S(2)}) collective-permute-start(f32[288,128]{1,0:T(8,128)S(1)} %get-tuple-element.51), channel_id=1, source_target_pairs={{0,4},{2,6},{4,0},{6,2},{1,5},{3,7},{5,1},{7,3},{8,12},{10,14},{12... | collective-permute-start | bytes 442376 | tf_op jit(solution)/shard_map/ppermute | solution.py:326
  15.1 4.9 %collective-permute-start.4 = (f32[288,128]{1,0:T(8,128)S(1)}, f32[288,128]{1,0:T(8,128)S(1)}, u32[]{:S(2)}, u32[]{:S(2)}) collective-permute-start(f32[288,128]{1,0:T(8,128)S(1)} %get-tuple-element.51), channel_id=1, source_target_pairs={{0,6},{2,0},{4,2},{6,4},{1,7},{3,1},{5,3},{7,5},{8,14},{10,8},{12,... | collective-permute-start | bytes 442376 | tf_op jit(solution)/shard_map/ppermute | solution.py:326
  20.1 4.9 %collective-permute-start.5 = (f32[4,288,128]{2,1,0:T(8,128)S(1)}, f32[4,288,128]{2,1,0:T(8,128)}, u32[]{:S(2)}, u32[]{:S(2)}) collective-permute-start(f32[4,288,128]{2,1,0:T(8,128)S(1)} %pad_maximum_fusion.1.refs_0_), channel_id=1, source_target_pairs={{0,1},{1,0},{2,3},{3,2},{4,5},{5,4},{6,7},{7,6},{8,9},{9,8},{10,11... | collective-permute-start | bytes 1769480 | tf_op jit(solution)/shard_map/ppermute | solution.py:313
  30.9 7.4 %collective-permute-start.6 = (f32[152,128]{1,0:T(8,128)}, f32[152,128]{1,0:T(8,128)S(1)}, u32[]{:S(2)}, u32[]{:S(2)}) collective-permute-start(f32[152,128]{1,0:T(8,128)} %get-tuple-element.19), channel_id=1, source_target_pairs={{0,8},{8,16},{16,24},{24,32},{32,40},{40,48},{48,56},{56,64},{64,7... | collective-permute-start | bytes 233480 | tf_op jit(solution)/shard_map/ppermute | solution.py:307
  34.2 5.4 %collective-permute-start.7 = (f32[152,128]{1,0:T(8,128)}, f32[152,128]{1,0:T(8,128)S(1)}, u32[]{:S(2)}, u32[]{:S(2)}) collective-permute-start(f32[152,128]{1,0:T(8,128)} %get-tuple-element.18), channel_id=1, source_target_pairs={{8,0},{16,8},{24,16},{32,24},{40,32},{48,40},{56,48},{64,56},{72,6... | collective-permute-start | bytes 233480 | tf_op jit(solution)/shard_map/ppermute | solution.py:307
  40.6 19.7 %copy-start.8 = (f32[392,128]{1,0:T(8,128)}, f32[392,128]{1,0:T(8,128)S(1)}, u32[]{:S(2)}) copy-start(f32[392,128]{1,0:T(8,128)S(1)} %constant_dynamic-update-slice_fusion.5) | copy-start | bytes 602116
  40.6 19.6 %collective-permute-start.8 = (f32[392,128]{1,0:T(8,128)S(1)}, f32[392,128]{1,0:T(8,128)S(1)}, u32[]{:S(2)}, u32[]{:S(2)}) collective-permute-start(f32[392,128]{1,0:T(8,128)S(1)} %constant_dynamic-update-slice_fusion.5), channel_id=1, source_target_pairs={{0,2},{2,4},{4,6},{6,0},{1,3},{3,5},{5,7},{7,1},{8,10},{10,12},{12... | collective-permute-start | bytes 602120 | tf_op jit(solution)/shard_map/ppermute | solution.py:326
  41.7 18.5 %collective-permute-start.9 = (f32[392,128]{1,0:T(8,128)S(1)}, f32[392,128]{1,0:T(8,128)S(1)}, u32[]{:S(2)}, u32[]{:S(2)}) collective-permute-start(f32[392,128]{1,0:T(8,128)S(1)} %constant_dynamic-update-slice_fusion.5), channel_id=1, source_target_pairs={{0,4},{2,6},{4,0},{6,2},{1,5},{3,7},{5,1},{7,3},{8,12},{10,14},{12... | collective-permute-start | bytes 602120 | tf_op jit(solution)/shard_map/ppermute | solution.py:326
  44.2 16.1 %collective-permute-start.10 = (f32[392,128]{1,0:T(8,128)S(1)}, f32[392,128]{1,0:T(8,128)S(1)}, u32[]{:S(2)}, u32[]{:S(2)}) collective-permute-start(f32[392,128]{1,0:T(8,128)S(1)} %constant_dynamic-update-slice_fusion.5), channel_id=1, source_target_pairs={{0,6},{2,0},{4,2},{6,4},{1,7},{3,1},{5,3},{7,5},{8,14},{10,8},{12,... | collective-permute-start | bytes 602120 | tf_op jit(solution)/shard_map/ppermute | solution.py:326
  45.2 25.5 %all-to-all-start = ((f32[32,16,128]{2,1,0:T(8,128)}), f32[32,16,128]{2,1,0:T(8,128)S(1)}, u32[]{:S(2)}, u32[]{:S(2)}) async-start(f32[32,16,128]{2,1,0:T(8,128)} %get-tuple-element.21), calls=%async_computation | async-start | bytes 524288 | tf_op jit(solution)/shard_map/all_to_all | solution.py:331
  62.3 17.8 %copy-start.3 = (f32[4,392,128]{2,1,0:T(8,128)}, f32[4,392,128]{2,1,0:T(8,128)S(1)}, u32[]{:S(2)}) copy-start(f32[4,392,128]{2,1,0:T(8,128)S(1)} %pad_maximum_fusion.refs_0_) | copy-start | bytes 2408452
  62.3 17.8 %collective-permute-start.11 = (f32[4,392,128]{2,1,0:T(8,128)S(1)}, f32[4,392,128]{2,1,0:T(8,128)}, u32[]{:S(2)}, u32[]{:S(2)}) collective-permute-start(f32[4,392,128]{2,1,0:T(8,128)S(1)} %pad_maximum_fusion.refs_0_), channel_id=1, source_target_pairs={{0,1},{1,0},{2,3},{3,2},{4,5},{5,4},{6,7},{7,6},{8,9},{9,8},{10,11... | collective-permute-start | bytes 2408456 | tf_op jit(solution)/shard_map/ppermute | solution.py:313
  80.2 11.9 %copy-start.9 = (f32[40,128]{1,0:T(8,128)S(1)}, f32[40,128]{1,0:T(8,128)}, u32[]{:S(2)}) copy-start(f32[40,128]{1,0:T(8,128)} %get-tuple-element.22.refs_4_) | copy-start | bytes 61444
  86.1 16.3 %all-to-all-start.1 = ((f32[32,16,128]{2,1,0:T(8,128)}), f32[32,16,128]{2,1,0:T(8,128)S(1)}, u32[]{:S(2)}, u32[]{:S(2)}) async-start(f32[32,16,128]{2,1,0:T(8,128)} %get-tuple-element.23), calls=%async_computation.1 | async-start | bytes 524288 | tf_op jit(solution)/shard_map/all_to_all | solution.py:331
  109.1 27.6 %copy-start.7 = (f32[128,128]{1,0:T(8,128)S(1)}, f32[128,128]{1,0:T(8,128)}, u32[]{:S(2)}) copy-start(f32[128,128]{1,0:T(8,128)} %convolution_subtract_fusion.2.refs_5_) | copy-start | bytes 196612
  109.1 27.6 %copy-start.11 = (f32[8,128]{1,0:T(8,128)S(1)}, f32[8,128]{1,0:T(8,128)}, u32[]{:S(2)}) copy-start(f32[8,128]{1,0:T(8,128)} %copy-done.10) | copy-start | bytes 12292
  109.1 27.6 %copy-start.16 = (f32[8,128]{1,0:T(8,128)S(1)}, f32[8,128]{1,0:T(8,128)}, u32[]{:S(2)}) copy-start(f32[8,128]{1,0:T(8,128)} %copy-done.15) | copy-start | bytes 12292
  109.1 27.6 %copy-start.19 = (f32[8,128]{1,0:T(8,128)S(1)}, f32[8,128]{1,0:T(8,128)}, u32[]{:S(2)}) copy-start(f32[8,128]{1,0:T(8,128)} %copy-done.18) | copy-start | bytes 12292
  110.6 24.2 %all-to-all-start.2 = ((f32[256,2,128]{2,1,0:T(2,128)}), f32[256,2,128]{2,1,0:T(2,128)S(1)}, u32[]{:S(2)}, u32[]{:S(2)}) async-start(f32[256,2,128]{2,1,0:T(2,128)} %broadcast_in_dim.11), calls=%async_computation.2 | async-start | bytes 524288 | tf_op jit(solution)/shard_map/all_to_all | solution.py:318
  120.4 3.8 %collective-permute-start.13 = (f32[24,128]{0,1:T(8,128)S(1)}, f32[24,128]{0,1:T(8,128)S(1)}, u32[]{:S(2)}, u32[]{:S(2)}) collective-permute-start(f32[24,128]{0,1:T(8,128)S(1)} %get-tuple-element.52), channel_id=1, source_target_pairs={{0,1},{1,0},{2,3},{3,2},{4,5},{5,4},{6,7},{7,6},{8,9},{9,8},{10,11... | collective-permute-start | bytes 36872 | tf_op jit(solution)/shard_map/ppermute | solution.py:313
  123.0 13.7 %collective-permute-start.12 = (f32[128,128]{1,0:T(8,128)}, f32[128,128]{1,0:T(8,128)S(1)}, u32[]{:S(2)}, u32[]{:S(2)}) collective-permute-start(f32[128,128]{1,0:T(8,128)} %get-tuple-element.31), channel_id=1, source_target_pairs={{8,0},{16,8},{24,16},{32,24},{40,32},{48,40},{56,48},{64,56},{72,6... | collective-permute-start | bytes 196616 | tf_op jit(solution)/shard_map/ppermute | solution.py:307
  124.3 12.3 %collective-permute-start.14 = (f32[24,128]{0,1:T(8,128)S(1)}, f32[24,128]{0,1:T(8,128)S(1)}, u32[]{:S(2)}, u32[]{:S(2)}) collective-permute-start(f32[24,128]{0,1:T(8,128)S(1)} %add_dynamic-update-slice_fusion), channel_id=1, source_target_pairs={{0,2},{2,4},{4,6},{6,0},{1,3},{3,5},{5,7},{7,1},{8,10},{10,12},{12... | collective-permute-start | bytes 36872 | tf_op jit(solution)/shard_map/ppermute | solution.py:326
  124.4 12.2 %collective-permute-start.15 = (f32[24,128]{0,1:T(8,128)S(1)}, f32[24,128]{0,1:T(8,128)S(1)}, u32[]{:S(2)}, u32[]{:S(2)}) collective-permute-start(f32[24,128]{0,1:T(8,128)S(1)} %add_dynamic-update-slice_fusion), channel_id=1, source_target_pairs={{0,4},{2,6},{4,0},{6,2},{1,5},{3,7},{5,1},{7,3},{8,12},{10,14},{12... | collective-permute-start | bytes 36872 | tf_op jit(solution)/shard_map/ppermute | solution.py:326
  126.1 10.6 %collective-permute-start.16 = (f32[24,128]{0,1:T(8,128)S(1)}, f32[24,128]{0,1:T(8,128)S(1)}, u32[]{:S(2)}, u32[]{:S(2)}) collective-permute-start(f32[24,128]{0,1:T(8,128)S(1)} %add_dynamic-update-slice_fusion), channel_id=1, source_target_pairs={{0,6},{2,0},{4,2},{6,4},{1,7},{3,1},{5,3},{7,5},{8,14},{10,8},{12,... | collective-permute-start | bytes 36872 | tf_op jit(solution)/shard_map/ppermute | solution.py:326
  (13 other events, 51.2 us)

commit v4 on v3

--- a/solution.py
+++ b/solution.py
@@ -302,6 +302,31 @@
     )(second, near, turned, image, search, res)
 
 
+def result_kernel(totals_ref, direction_ref, res_ref, high_ref, after_ref, turned_ref, live_ref, *refs):
+    parts, (multipliers_ref, residual_ref) = refs[:-2], refs[-2:]
+    weights = parts[0][...]
+    for part in parts[1:]:
+        weights = weights + part[...]
+    rows = res_ref.shape[0]
+    gap = jnp.zeros((3 * PAD, 128), jnp.float32)
+    none = jnp.zeros((128 - 6 * PAD, 128), jnp.float32)
+    change = dot(turned_ref[rows:, :], jnp.concatenate([gap, weights, none], 0))
+    step = totals_ref[0:1, :] / totals_ref[1:2, :]
+    image = (high_ref[...] - after_ref[...]) * live_ref[0] - change
+    multipliers_ref[0] = step * direction_ref[...]
+    residual_ref[0] = res_ref[...] - step * image
+
+
+def results(totals, direction, res, high, after, turned, live, parts):
+    return pl.pallas_call(
+        result_kernel,
+        out_shape=shapes((1, *res.shape), (1, *res.shape)),
+        in_specs=[VMEM] * 6 + [SMEM] + [VMEM] * len(parts),
+        out_specs=[VMEM] * 2,
+        name="results",
+    )(totals, direction, res, high, after, turned, live[None], *parts)
+
+
 def moved_along(block, distance):
     n = lax.axis_size(SUB)
     return lax.ppermute(
@@ -332,7 +357,8 @@
 
 
 def gathered(piece):
-    own = jnp.stack(along_x(piece))
+    pieces = along_x(piece)
+    own = jnp.stack(pieces)
     return own, core_swap(own)
 
 
@@ -413,17 +439,16 @@
     image = dot(flex, search_traces) - dot(dot_nt(flex, modes_traces), weights)
     own_search = own_traces - spread(own_modes, weights)
     own_res = field - spread(own_basis[:, rows:], weights[PAD : 4 * PAD])
-
     turned = jnp.concatenate([flex_modes, own_basis], 0)
     turned = jnp.pad(turned, ((0, 128 - 6 * PAD), (0, 0))).T
     low, high, direction, sums = project_direction(
         second.reshape(subs * 2 * PAD, 128), near, turned, image, own_search, own_res, subs
     )
-    totals = from_all(sums, ALL).sum(0)
-
-    low, second = lax.optimization_barrier((low, second))
+    totals = from_all(sums, ALL)
+    totals = totals.sum(0)
+
+    after = moved_along(low, -1)
     near = near[PAD : 4 * PAD]
-    after = moved_along(low, -1)
     all_rhs = second[:, :PAD].transpose(1, 0, 2).reshape(PAD * subs, loads)
     my_rhs = lax.dynamic_slice_in_dim(all_rhs, mine, share, 1)
     my_weights = dot(inverse, my_rhs).reshape(PAD, subs, share).transpose(1, 0, 2)
@@ -449,10 +474,7 @@
         jnp.zeros((3 * PAD, loads), jnp.float32), weights, mine, 1
     )
     weights = weights + core_swap(weights)
-    weights = sum(along_x(weights))
-    own_image = (high - after) * live - spread(own_basis[:, rows:], weights)
-    step = totals[0] / totals[1]
-    return (step * direction)[None], (own_res - step * own_image)[None]
+    return results(totals, direction, own_res, high, after, turned, live, along_x(weights))
 
 
 def solution(mesh):

time: 139 us -> 133 us (0.957)
  waiting for transfers between devices: 26.4 us -> 19.8 us
  Pallas kernels: 16.5 us -> 18.3 us
    all_to_all x2, waiting for transfers between devices: 11.1 us -> 7.79 us  [to_all(): return lax.all_to_all(values, axis, 0, 0, tiled=True)]
    all_to_all x1, waiting for transfers between devices: 7.63 us -> 4.45 us  [from_all(): lax.all_to_all(jnp.broadcast_to(value[None], (count, *value.shape)), axis...]
    pallas_call x0 -> x1, Pallas kernels: none -> 1.85 us  [results(): pl.pallas_call(result_kernel, out_shape=shapes((1, *res.shape), (1, *res....]
    dot_general x3 -> x2, matrix products: 5.17 us -> 3.38 us  [spread(): lax.dot_general(part, weights, (((0,), (0,)), ((), ())), precision=HIGH,...]
    broadcast_in_dim x1 -> x0, other arithmetic: 1.48 us -> none  [per_device(): return ((step * direction)[None], (own_res - step * own_image)[None])]
    unnamed x55 -> x47, local copies, waits for them, and re-layouts: 3.38 us -> 2.85 us
  transfers between devices with their start and end apart: 20 -> 20, of which waited for: 9 -> 9; matrix products, arithmetic and copies ran while one was open for 12% -> 17% of each run, Pallas kernels for 4% -> 4%
where the time goes in v4:
time: 133 us; the launch traced here: 132 us
  starting transfers between devices  62.1 us (47%)
  waiting for transfers between devices  19.8 us (15%)
  Pallas kernels  18.3 us (14%)
  matrix products  16.6 us (12%)
  local copies, waits for them, and re-layouts  7.84 us (6%)
  other arithmetic  5.64 us (4%)
  between operations  2.04 us (2%)
    all_to_all x2, starting transfers between devices, to_all(): return lax.all_to_all(values, axis, 0, 0, tiled=True)  21.7 us
    ppermute x9, starting transfers between devices, along_x(): lax.ppermute(piece, 'x', [(i, (i + d) % n) for i in range(n)])  12.3 us
    ppermute x5, starting transfers between devices, moved_along(): lax.ppermute(block, SUB, [(i - distance, i) for i in range(n) if 0 <= i -...  11.2 us
    ppermute x3, starting transfers between devices, core_swap(): return lax.ppermute(block, 'c', [(0, 1), (1, 0)])  8.85 us
    all_to_all x1, starting transfers between devices, from_all(): lax.all_to_all(jnp.broadcast_to(value[None], (count, *value.shape)), axis...  7.99 us
    all_to_all x2, waiting for transfers between devices, to_all(): return lax.all_to_all(values, axis, 0, 0, tiled=True)  7.79 us
    dot_general x4, matrix products, dot_nt(): lax.dot_general(a, b, (((1,), (1,)), ((), ())), precision=HIGH, preferred...  5.93 us
    pallas_call x1, Pallas kernels, apply_stiffness(): pl.pallas_call(lambda *refs: stiff_kernel(count, rows, *refs), out_shape=...  5.82 us
  transfers between devices with their start and end apart: 20, of which 9 were waited for; matrix products, arithmetic and copies ran while one was open for 17% of the time, Pallas kernels for 4%

profile of v4, /device:TPU:1, one launch (start us, length us, event | category | flops | bytes accessed | tf_op | source)
XLA Modules:
  0.0 132.4 jit_solution(6355288254625111824)
XLA Ops:
  3.1 4.0 %collective-permute-start = (f32[136,128]{1,0:T(8,128)S(1)}, f32[136,128]{1,0:T(8,128)S(1)}, u32[]{:S(2)}, u32[]{:S(2)}) collective-permute-start(f32[136,128]{1,0:T(8,128)S(1)} %pad_maximum_fusion.5), channel_id=1, source_target_pairs={{0,8},{8,16},{16,24},{24,32},{32,40},{40,48},{48,56},{56,64},{64,7... | collective-permute-start | bytes 208904 | tf_op jit(solution)/shard_map/ppermute | solution.py:332
  7.1 1.3 collective-permute-start.1
  9.4 2.1 %collective-permute-done.1 = f32[8,128]{1,0:T(8,128)S(1)} collective-permute-done((f32[8,128]{1,0:T(8,128)S(1)}, f32[8,128]{1,0:T(8,128)S(1)}, u32[]{:S(2)}, u32[]{:S(2)}) %collective-permute-start.1) | collective-permute-done | bytes 4128 | tf_op jit(solution)/shard_map/ppermute | solution.py:332
  12.7 2.5 %collective-permute-start.3 = (f32[288,128]{1,0:T(8,128)S(1)}, f32[288,128]{1,0:T(8,128)S(1)}, u32[]{:S(2)}, u32[]{:S(2)}) collective-permute-start(f32[288,128]{1,0:T(8,128)S(1)} %get-tuple-element.47), channel_id=1, source_target_pairs={{0,4},{2,6},{4,0},{6,2},{1,5},{3,7},{5,1},{7,3},{8,12},{10,14},{12... | collective-permute-start | bytes 442376 | tf_op jit(solution)/shard_map/ppermute | solution.py:351
  16.7 3.2 %collective-permute-done.3 = f32[288,128]{1,0:T(8,128)S(1)} collective-permute-done((f32[288,128]{1,0:T(8,128)S(1)}, f32[288,128]{1,0:T(8,128)S(1)}, u32[]{:S(2)}, u32[]{:S(2)}) %collective-permute-start.3) | collective-permute-done | bytes 147488 | tf_op jit(solution)/shard_map/ppermute | solution.py:351
  20.1 3.2 %collective-permute-start.5 = (f32[4,288,128]{2,1,0:T(8,128)S(1)}, f32[4,288,128]{2,1,0:T(8,128)}, u32[]{:S(2)}, u32[]{:S(2)}) collective-permute-start(f32[4,288,128]{2,1,0:T(8,128)S(1)} %pad_maximum_fusion.1.refs_0_), channel_id=1, source_target_pairs={{0,1},{1,0},{2,3},{3,2},{4,5},{5,4},{6,7},{7,6},{8,9},{9,8},{10,11... | collective-permute-start | bytes 1769480 | tf_op jit(solution)/shard_map/ppermute | solution.py:338
  25.0 5.8 %apply_stiffness.1 = (f32[152,128]{1,0:T(8,128)}, f32[152,128]{1,0:T(8,128)}, f32[24,2048]{1,0:T(8,128)}, f32[32,16,128]{2,1,0:T(8,128)}) custom-call(f32[4,288,128]{2,1,0:T(8,128)} %copy-done.4, f32[4,288,128]{2,1,0:T(8,128)} %collective-permute-done.5.refs_1_, s32[2]{0:T(128)} %pad_add_fusion.refs_2_, f32[8,128]{1,0:T(8,128)} %pad.29.refs_3_, ...), custom_call_target="tpu_custom_call" | custom-call | tf_op jit(solution)/shard_map/apply_stiffness/pallas_call | solution.py:204
  30.8 3.3 %collective-permute-start.6 = (f32[152,128]{1,0:T(8,128)}, f32[152,128]{1,0:T(8,128)S(1)}, u32[]{:S(2)}, u32[]{:S(2)}) collective-permute-start(f32[152,128]{1,0:T(8,128)} %get-tuple-element.17), channel_id=1, source_target_pairs={{0,8},{8,16},{16,24},{24,32},{32,40},{40,48},{48,56},{56,64},{64,7... | collective-permute-start | bytes 233480 | tf_op jit(solution)/shard_map/ppermute | solution.py:332
  34.2 1.3 collective-permute-start.7
  35.5 2.7 %fusion.62 = f32[24,256]{1,0:T(8,128)S(1)} fusion(f32[24,2048]{1,0:T(8,128)} %get-tuple-element.18.refs_3_, f32[256,2048]{1,0:T(8,128)S(1)} %bitcast.63), kind=kOutput, calls=%fused_computation.109 | convolution fusion | flops 150994944 | bytes 2318336 | tf_op jit(solution)/shard_map/dot_general | solution.py:23
  38.2 1.3 collective-permute-done.7
  41.3 2.4 %collective-permute-start.9 = (f32[392,128]{1,0:T(8,128)S(1)}, f32[392,128]{1,0:T(8,128)S(1)}, u32[]{:S(2)}, u32[]{:S(2)}) collective-permute-start(f32[392,128]{1,0:T(8,128)S(1)} %constant_dynamic-update-slice_fusion.5), channel_id=1, source_target_pairs={{0,4},{2,6},{4,0},{6,2},{1,5},{3,7},{5,1},{7,3},{8,12},{10,14},{12... | collective-permute-start | bytes 602120 | tf_op jit(solution)/shard_map/ppermute | solution.py:351
  44.7 15.0 %all-to-all-start = ((f32[32,16,128]{2,1,0:T(8,128)}), f32[32,16,128]{2,1,0:T(8,128)S(1)}, u32[]{:S(2)}, u32[]{:S(2)}) async-start(f32[32,16,128]{2,1,0:T(8,128)} %get-tuple-element.19), calls=%async_computation | async-start | bytes 524288 | tf_op jit(solution)/shard_map/all_to_all | solution.py:356
  61.9 3.2 %collective-permute-start.11 = (f32[4,392,128]{2,1,0:T(8,128)S(1)}, f32[4,392,128]{2,1,0:T(8,128)}, u32[]{:S(2)}, u32[]{:S(2)}) collective-permute-start(f32[4,392,128]{2,1,0:T(8,128)S(1)} %pad_maximum_fusion.refs_0_), channel_id=1, source_target_pairs={{0,1},{1,0},{2,3},{3,2},{4,5},{5,4},{6,7},{7,6},{8,9},{9,8},{10,11... | collective-permute-start | bytes 2408456 | tf_op jit(solution)/shard_map/ppermute | solution.py:338
  67.3 2.9 %all-to-all-done = f32[32,16,128]{2,1,0:T(8,128)S(1)} async-done(((f32[32,16,128]{2,1,0:T(8,128)}), f32[32,16,128]{2,1,0:T(8,128)S(1)}, u32[]{:S(2)}, u32[]{:S(2)}) %all-to-all-start) | async-done | bytes 262176 | tf_op jit(solution)/shard_map/all_to_all | solution.py:356
  70.9 5.4 %coarse_inverse.1 = (f32[256,256]{1,0:T(8,128)}, f32[40,256]{1,0:T(8,128)}, f32[40,128]{1,0:T(8,128)}) custom-call(s32[1]{0:T(128)} %bitcast.17.refs_0_, f32[512,128]{1,0:T(8,128)} %bitcast.70), custom_call_target="tpu_custom_call" | custom-call | tf_op jit(solution)/shard_map/coarse_inverse/pallas_call | solution.py:132
  76.3 1.6 %convolution_subtract_fusion.1.refs_5_.res_ref = f32[128,128]{1,0:T(8,128)} fusion(f32[128,128]{1,0:T(8,128)S(1)} %multiply_bitcast_fusion, f32[8,128]{1,0:T(8,128)S(1)} %get-tuple-element.46, f32[8,128]{1,0:T(8,128)S(1)} %get-tuple-element.43, f32[8,128]{1,0:T(8,128)S(1)} %broadcast.49, f32[40,128]{1,0:T(8,128)} %get-tuple-element.20.refs_4_), kind=kOutput, calls=%fused_computation.3 | convolution fusion | flops 4741120 | bytes 155648 | tf_op jit(solution)/shard_map/dot_general | solution.py:366
  77.9 1.8 %convolution_subtract_fusion.refs_4_ = f32[256,128]{1,0:T(8,128)} fusion(f32[40,128]{1,0:T(8,128)} %get-tuple-element.20.refs_4_, f32[128,128]{1,0:T(8,128)S(1)} %get-tuple-element.31, f32[128,128]{1,0:T(8,128)S(1)} %get-tuple-element.33, f32[40,128]{1,0:T(8,128)S(1)} %get-tuple-element.45, f32[40,128]{1,0:T(8,128)S(1)} %get-tuple-element.44), kind=kOutput, calls=%fused_computation.2 | convolution fusion | flops 15804416 | bytes 323584 | tf_op jit(solution)/shard_map/dot_general | solution.py:366
  79.7 2.9 %order_search.1 = (f32[2048,128]{1,0:T(8,128)}, f32[40,2048]{1,0:T(8,128)}, f32[32,16,128]{2,1,0:T(8,128)}) custom-call(f32[4,392,128]{2,1,0:T(8,128)} %copy-done.3, f32[4,392,128]{2,1,0:T(8,128)} %collective-permute-done.11.refs_1_, s32[2]{0:T(128)} %pad_add_fusion.refs_2_, f32[24,2048]{1,0:T(8,128)} %get-tuple-element.18.refs_3_, ...), custom_call_target="tpu_custom_call" | custom-call | tf_op jit(solution)/shard_map/order_search/pallas_call | solution.py:257
  82.6 6.7 %all-to-all-start.1 = ((f32[32,16,128]{2,1,0:T(8,128)}), f32[32,16,128]{2,1,0:T(8,128)S(1)}, u32[]{:S(2)}, u32[]{:S(2)}) async-start(f32[32,16,128]{2,1,0:T(8,128)} %get-tuple-element.21), calls=%async_computation.1 | async-start | bytes 524288 | tf_op jit(solution)/shard_map/all_to_all | solution.py:356
  89.3 2.9 %fusion.63 = f32[40,256]{1,0:T(8,128)S(1)} fusion(f32[40,2048]{1,0:T(8,128)} %get-tuple-element.24, f32[256,2048]{1,0:T(8,128)S(1)} %bitcast.65), kind=kOutput, calls=%fused_computation.110 | convolution fusion | flops 251658240 | bytes 2465792 | tf_op jit(solution)/shard_map/dot_general | solution.py:23
  92.7 2.4 %fusion.refs_3_ = f32[256,128]{1,0:T(8,128)} fusion(f32[256,128]{1,0:T(8,128)S(1)} %fusion.64, f32[2048,128]{1,0:T(8,128)S(1)} %copy-done.5, f32[256,2048]{1,0:T(8,128)S(1)} %bitcast.64), kind=kOutput, calls=%fused_computation.1 | convolution fusion | flops 805339136 | bytes 3407872 | tf_op jit(solution)/shard_map/dot_general | solution.py:19
  95.1 4.9 %all-to-all-done.1 = f32[32,16,128]{2,1,0:T(8,128)S(1)} async-done(((f32[32,16,128]{2,1,0:T(8,128)}), f32[32,16,128]{2,1,0:T(8,128)S(1)}, u32[]{:S(2)}, u32[]{:S(2)}) %all-to-all-start.1) | async-done | bytes 262176 | tf_op jit(solution)/shard_map/all_to_all | solution.py:356
  100.0 1.4 %fusion.10 = f32[256,16]{0,1:T(8,128)S(1)} fusion(f32[256,256]{1,0:T(8,128)} %get-tuple-element.29, f32[256,128]{1,0:T(8,128)S(1)} %bitcast.71, s32[]{:T(128)S(6)} %select_n.4), kind=kOutput, calls=%fused_computation.22 | convolution fusion | flops 12582912 | bytes 409604 | tf_op jit(solution)/shard_map/dot_general | solution.py:19
  101.8 2.3 %project_direction.1 = (f32[128,128]{1,0:T(8,128)}, f32[128,128]{1,0:T(8,128)}, f32[128,128]{1,0:T(8,128)}, f32[2,128]{1,0:T(2,128)}) custom-call(f32[512,128]{1,0:T(8,128)} %bitcast.66, f32[40,256]{1,0:T(8,128)} %get-tuple-element.22.refs_1_, f32[256,128]{1,0:T(8,128)} %pad_bitcast_fusion.refs_2_.turned_ref, f32[256,128]{1,0:T(8,128)} %fusion.refs_3_, ...), custom_call_target="tpu_custom_call" | custom-call | tf_op jit(solution)/shard_map/project_direction/pallas_call | solution.py:296
  104.2 1.5 %broadcast_in_dim.9 = f32[256,2,128]{2,1,0:T(2,128)} broadcast(f32[2,128]{1,0:T(2,128)} %get-tuple-element.25), dimensions={1,2} | broadcast | bytes 263168 | tf_op jit(solution)/shard_map/broadcast_in_dim | solution.py:344
  105.6 8.0 %all-to-all-start.2 = ((f32[256,2,128]{2,1,0:T(2,128)}), f32[256,2,128]{2,1,0:T(2,128)S(1)}, u32[]{:S(2)}, u32[]{:S(2)}) async-start(f32[256,2,128]{2,1,0:T(2,128)} %broadcast_in_dim.9), calls=%async_computation.2 | async-start | bytes 524288 | tf_op jit(solution)/shard_map/all_to_all | solution.py:343
  113.9 1.5 %fusion.3 = f32[32,8,16]{2,1,0:T(8,128)S(1)} fusion(f32[32,24,16]{1,2,0:T(8,128)S(1)} %pad_maximum_fusion.2, f32[32,16,128]{2,1,0:T(8,128)} %copy-done.1), kind=kOutput, calls=%fused_computation.12 | convolution fusion | flops 1179648 | bytes 196608 | tf_op jit(solution)/shard_map/dot_general | solution.py:461
  117.4 2.5 %collective-permute-start.13 = (f32[24,128]{1,0:T(8,128)S(1)}, f32[24,128]{1,0:T(8,128)S(1)}, u32[]{:S(2)}, u32[]{:S(2)}) collective-permute-start(f32[24,128]{1,0:T(8,128)S(1)} %dynamic_update_slice.5), channel_id=1, source_target_pairs={{0,1},{1,0},{2,3},{3,2},{4,5},{5,4},{6,7},{7,6},{8,9},{9,8},{10,11... | collective-permute-start | bytes 36872 | tf_op jit(solution)/shard_map/ppermute | solution.py:338
  121.7 1.7 %collective-permute-start.15 = (f32[24,128]{1,0:T(8,128)S(1)}, f32[24,128]{1,0:T(8,128)S(1)}, u32[]{:S(2)}, u32[]{:S(2)}) collective-permute-start(f32[24,128]{1,0:T(8,128)S(1)} %add.45.refs_0_), channel_id=1, source_target_pairs={{0,4},{2,6},{4,0},{6,2},{1,5},{3,7},{5,1},{7,3},{8,12},{10,14},{12... | collective-permute-start | bytes 36872 | tf_op jit(solution)/shard_map/ppermute | solution.py:351
  124.6 4.4 %all-to-all-done.2 = f32[256,2,128]{2,1,0:T(2,128)S(1)} async-done(((f32[256,2,128]{2,1,0:T(2,128)}), f32[256,2,128]{2,1,0:T(2,128)S(1)}, u32[]{:S(2)}, u32[]{:S(2)}) %all-to-all-start.2) | async-done | bytes 262176 | tf_op jit(solution)/shard_map/all_to_all | solution.py:343
  130.5 1.8 %results.1 = (f32[1,128,128]{2,1,0:T(8,128)}, f32[1,128,128]{2,1,0:T(8,128)}) custom-call(f32[2,128]{1,0:T(2,128)} %reduce_sum.9.totals_ref, f32[128,128]{1,0:T(8,128)} %get-tuple-element.26.direction_ref, f32[128,128]{1,0:T(8,128)} %convolution_subtract_fusion.1.refs_5_.res_ref, f32[128,128]{1,0:T(8,128)} %get-tuple-element.27.high_ref, ...), custom_call_target="tpu_custom_call" | custom-call | tf_op jit(solution)/shard_map/results/pallas_call | solution.py:321
  (118 shorter events, 22.3 us)
Async XLA Ops:
  0.6 34.9 %copy-start = (f32[1,2,128,2048]{3,2,1,0:T(8,128)S(1)}, f32[1,2,128,2048]{3,2,1,0:T(8,128)}, u32[]{:S(2)}) copy-start(f32[1,2,128,2048]{3,2,1,0:T(8,128)} %param.6) | copy-start | bytes 6291460
  3.1 5.4 %collective-permute-start = (f32[136,128]{1,0:T(8,128)S(1)}, f32[136,128]{1,0:T(8,128)S(1)}, u32[]{:S(2)}, u32[]{:S(2)}) collective-permute-start(f32[136,128]{1,0:T(8,128)S(1)} %pad_maximum_fusion.5), channel_id=1, source_target_pairs={{0,8},{8,16},{16,24},{24,32},{32,40},{40,48},{48,56},{56,64},{64,7... | collective-permute-start | bytes 208904 | tf_op jit(solution)/shard_map/ppermute | solution.py:332
  7.1 4.4 %collective-permute-start.1 = (f32[8,128]{1,0:T(8,128)S(1)}, f32[8,128]{1,0:T(8,128)S(1)}, u32[]{:S(2)}, u32[]{:S(2)}) collective-permute-start(f32[8,128]{1,0:T(8,128)S(1)} %get-tuple-element.42), channel_id=1, source_target_pairs={{8,0},{16,8},{24,16},{32,24},{40,32},{48,40},{56,48},{64,56},{72,6... | collective-permute-start | bytes 12296 | tf_op jit(solution)/shard_map/ppermute | solution.py:332
  11.5 5.2 %collective-permute-start.2 = (f32[288,128]{1,0:T(8,128)S(1)}, f32[288,128]{1,0:T(8,128)S(1)}, u32[]{:S(2)}, u32[]{:S(2)}) collective-permute-start(f32[288,128]{1,0:T(8,128)S(1)} %get-tuple-element.47), channel_id=1, source_target_pairs={{0,2},{2,4},{4,6},{6,0},{1,3},{3,5},{5,7},{7,1},{8,10},{10,12},{12... | collective-permute-start | bytes 442376 | tf_op jit(solution)/shard_map/ppermute | solution.py:351
  12.7 7.2 %collective-permute-start.3 = (f32[288,128]{1,0:T(8,128)S(1)}, f32[288,128]{1,0:T(8,128)S(1)}, u32[]{:S(2)}, u32[]{:S(2)}) collective-permute-start(f32[288,128]{1,0:T(8,128)S(1)} %get-tuple-element.47), channel_id=1, source_target_pairs={{0,4},{2,6},{4,0},{6,2},{1,5},{3,7},{5,1},{7,3},{8,12},{10,14},{12... | collective-permute-start | bytes 442376 | tf_op jit(solution)/shard_map/ppermute | solution.py:351
  15.1 4.9 %collective-permute-start.4 = (f32[288,128]{1,0:T(8,128)S(1)}, f32[288,128]{1,0:T(8,128)S(1)}, u32[]{:S(2)}, u32[]{:S(2)}) collective-permute-start(f32[288,128]{1,0:T(8,128)S(1)} %get-tuple-element.47), channel_id=1, source_target_pairs={{0,6},{2,0},{4,2},{6,4},{1,7},{3,1},{5,3},{7,5},{8,14},{10,8},{12,... | collective-permute-start | bytes 442376 | tf_op jit(solution)/shard_map/ppermute | solution.py:351
  20.1 4.9 %copy-start.4 = (f32[4,288,128]{2,1,0:T(8,128)}, f32[4,288,128]{2,1,0:T(8,128)S(1)}, u32[]{:S(2)}) copy-start(f32[4,288,128]{2,1,0:T(8,128)S(1)} %pad_maximum_fusion.1.refs_0_) | copy-start | bytes 1769476
  20.1 4.9 %collective-permute-start.5 = (f32[4,288,128]{2,1,0:T(8,128)S(1)}, f32[4,288,128]{2,1,0:T(8,128)}, u32[]{:S(2)}, u32[]{:S(2)}) collective-permute-start(f32[4,288,128]{2,1,0:T(8,128)S(1)} %pad_maximum_fusion.1.refs_0_), channel_id=1, source_target_pairs={{0,1},{1,0},{2,3},{3,2},{4,5},{5,4},{6,7},{7,6},{8,9},{9,8},{10,11... | collective-permute-start | bytes 1769480 | tf_op jit(solution)/shard_map/ppermute | solution.py:338
  30.8 7.3 %copy-start.14 = (f32[152,128]{1,0:T(8,128)S(1)}, f32[152,128]{1,0:T(8,128)}, u32[]{:S(2)}) copy-start(f32[152,128]{1,0:T(8,128)} %get-tuple-element.16) | copy-start | bytes 233476
  30.8 7.4 %copy-start.13 = (f32[152,128]{1,0:T(8,128)S(1)}, f32[152,128]{1,0:T(8,128)}, u32[]{:S(2)}) copy-start(f32[152,128]{1,0:T(8,128)} %get-tuple-element.17) | copy-start | bytes 233476
  30.8 7.4 %collective-permute-start.6 = (f32[152,128]{1,0:T(8,128)}, f32[152,128]{1,0:T(8,128)S(1)}, u32[]{:S(2)}, u32[]{:S(2)}) collective-permute-start(f32[152,128]{1,0:T(8,128)} %get-tuple-element.17), channel_id=1, source_target_pairs={{0,8},{8,16},{16,24},{24,32},{32,40},{40,48},{48,56},{56,64},{64,7... | collective-permute-start | bytes 233480 | tf_op jit(solution)/shard_map/ppermute | solution.py:332
  34.2 5.4 %collective-permute-start.7 = (f32[152,128]{1,0:T(8,128)}, f32[152,128]{1,0:T(8,128)S(1)}, u32[]{:S(2)}, u32[]{:S(2)}) collective-permute-start(f32[152,128]{1,0:T(8,128)} %get-tuple-element.16), channel_id=1, source_target_pairs={{8,0},{16,8},{24,16},{32,24},{40,32},{48,40},{56,48},{64,56},{72,6... | collective-permute-start | bytes 233480 | tf_op jit(solution)/shard_map/ppermute | solution.py:332
  40.2 19.7 %copy-start.7 = (f32[392,128]{1,0:T(8,128)}, f32[392,128]{1,0:T(8,128)S(1)}, u32[]{:S(2)}) copy-start(f32[392,128]{1,0:T(8,128)S(1)} %constant_dynamic-update-slice_fusion.5) | copy-start | bytes 602116
  40.2 19.6 %collective-permute-start.8 = (f32[392,128]{1,0:T(8,128)S(1)}, f32[392,128]{1,0:T(8,128)S(1)}, u32[]{:S(2)}, u32[]{:S(2)}) collective-permute-start(f32[392,128]{1,0:T(8,128)S(1)} %constant_dynamic-update-slice_fusion.5), channel_id=1, source_target_pairs={{0,2},{2,4},{4,6},{6,0},{1,3},{3,5},{5,7},{7,1},{8,10},{10,12},{12... | collective-permute-start | bytes 602120 | tf_op jit(solution)/shard_map/ppermute | solution.py:351
  41.3 18.5 %collective-permute-start.9 = (f32[392,128]{1,0:T(8,128)S(1)}, f32[392,128]{1,0:T(8,128)S(1)}, u32[]{:S(2)}, u32[]{:S(2)}) collective-permute-start(f32[392,128]{1,0:T(8,128)S(1)} %constant_dynamic-update-slice_fusion.5), channel_id=1, source_target_pairs={{0,4},{2,6},{4,0},{6,2},{1,5},{3,7},{5,1},{7,3},{8,12},{10,14},{12... | collective-permute-start | bytes 602120 | tf_op jit(solution)/shard_map/ppermute | solution.py:351
  43.7 16.1 %collective-permute-start.10 = (f32[392,128]{1,0:T(8,128)S(1)}, f32[392,128]{1,0:T(8,128)S(1)}, u32[]{:S(2)}, u32[]{:S(2)}) collective-permute-start(f32[392,128]{1,0:T(8,128)S(1)} %constant_dynamic-update-slice_fusion.5), channel_id=1, source_target_pairs={{0,6},{2,0},{4,2},{6,4},{1,7},{3,1},{5,3},{7,5},{8,14},{10,8},{12,... | collective-permute-start | bytes 602120 | tf_op jit(solution)/shard_map/ppermute | solution.py:351
  44.7 25.5 %all-to-all-start = ((f32[32,16,128]{2,1,0:T(8,128)}), f32[32,16,128]{2,1,0:T(8,128)S(1)}, u32[]{:S(2)}, u32[]{:S(2)}) async-start(f32[32,16,128]{2,1,0:T(8,128)} %get-tuple-element.19), calls=%async_computation | async-start | bytes 524288 | tf_op jit(solution)/shard_map/all_to_all | solution.py:356
  61.9 17.8 %copy-start.3 = (f32[4,392,128]{2,1,0:T(8,128)}, f32[4,392,128]{2,1,0:T(8,128)S(1)}, u32[]{:S(2)}) copy-start(f32[4,392,128]{2,1,0:T(8,128)S(1)} %pad_maximum_fusion.refs_0_) | copy-start | bytes 2408452
  61.9 17.8 %collective-permute-start.11 = (f32[4,392,128]{2,1,0:T(8,128)S(1)}, f32[4,392,128]{2,1,0:T(8,128)}, u32[]{:S(2)}, u32[]{:S(2)}) collective-permute-start(f32[4,392,128]{2,1,0:T(8,128)S(1)} %pad_maximum_fusion.refs_0_), channel_id=1, source_target_pairs={{0,1},{1,0},{2,3},{3,2},{4,5},{5,4},{6,7},{7,6},{8,9},{9,8},{10,11... | collective-permute-start | bytes 2408456 | tf_op jit(solution)/shard_map/ppermute | solution.py:338
  79.7 12.6 %copy-start.8 = (f32[40,128]{1,0:T(8,128)S(1)}, f32[40,128]{1,0:T(8,128)}, u32[]{:S(2)}) copy-start(f32[40,128]{1,0:T(8,128)} %get-tuple-element.20.refs_4_) | copy-start | bytes 61444
  82.6 10.1 %copy-start.5 = (f32[2048,128]{1,0:T(8,128)S(1)}, f32[2048,128]{1,0:T(8,128)}, u32[]{:S(2)}) copy-start(f32[2048,128]{1,0:T(8,128)} %get-tuple-element.23) | copy-start | bytes 3145732
  82.6 17.4 %all-to-all-start.1 = ((f32[32,16,128]{2,1,0:T(8,128)}), f32[32,16,128]{2,1,0:T(8,128)S(1)}, u32[]{:S(2)}, u32[]{:S(2)}) async-start(f32[32,16,128]{2,1,0:T(8,128)} %get-tuple-element.21), calls=%async_computation.1 | async-start | bytes 524288 | tf_op jit(solution)/shard_map/all_to_all | solution.py:356
  104.1 11.2 %copy-start.2 = (f32[32,16,128]{2,1,0:T(8,128)S(1)}, f32[32,16,128]{2,1,0:T(8,128)}, u32[]{:S(2)}) copy-start(f32[32,16,128]{2,1,0:T(8,128)} %copy-done.1) | copy-start | bytes 786436
  105.6 23.4 %all-to-all-start.2 = ((f32[256,2,128]{2,1,0:T(2,128)}), f32[256,2,128]{2,1,0:T(2,128)S(1)}, u32[]{:S(2)}, u32[]{:S(2)}) async-start(f32[256,2,128]{2,1,0:T(2,128)} %broadcast_in_dim.9), calls=%async_computation.2 | async-start | bytes 524288 | tf_op jit(solution)/shard_map/all_to_all | solution.py:343
  113.6 3.3 %copy-start.12 = (f32[40,256]{1,0:T(8,128)S(1)}, f32[40,256]{1,0:T(8,128)}, u32[]{:S(2)}) copy-start(f32[40,256]{1,0:T(8,128)} %get-tuple-element.22.refs_1_) | copy-start | bytes 122884
  113.8 6.1 %copy-start.20 = (f32[128,128]{1,0:T(8,128)S(1)}, f32[128,128]{1,0:T(8,128)}, u32[]{:S(2)}) copy-start(f32[128,128]{1,0:T(8,128)} %get-tuple-element.28) | copy-start | bytes 196612
  117.4 3.8 %collective-permute-start.13 = (f32[24,128]{1,0:T(8,128)S(1)}, f32[24,128]{1,0:T(8,128)S(1)}, u32[]{:S(2)}, u32[]{:S(2)}) collective-permute-start(f32[24,128]{1,0:T(8,128)S(1)} %dynamic_update_slice.5), channel_id=1, source_target_pairs={{0,1},{1,0},{2,3},{3,2},{4,5},{5,4},{6,7},{7,6},{8,9},{9,8},{10,11... | collective-permute-start | bytes 36872 | tf_op jit(solution)/shard_map/ppermute | solution.py:338
  120.0 9.9 %collective-permute-start.12 = (f32[128,128]{1,0:T(8,128)S(1)}, f32[128,128]{1,0:T(8,128)S(1)}, u32[]{:S(2)}, u32[]{:S(2)}) collective-permute-start(f32[128,128]{1,0:T(8,128)S(1)} %copy-done.20), channel_id=1, source_target_pairs={{8,0},{16,8},{24,16},{32,24},{40,32},{48,40},{56,48},{64,56},{72,6... | collective-permute-start | bytes 196616 | tf_op jit(solution)/shard_map/ppermute | solution.py:332
  121.6 8.3 %copy-start.16 = (f32[24,128]{1,0:T(8,128)}, f32[24,128]{1,0:T(8,128)S(1)}, u32[]{:S(2)}) copy-start(f32[24,128]{1,0:T(8,128)S(1)} %add.45.refs_0_) | copy-start | bytes 36868
  121.6 8.2 %collective-permute-start.14 = (f32[24,128]{1,0:T(8,128)S(1)}, f32[24,128]{1,0:T(8,128)S(1)}, u32[]{:S(2)}, u32[]{:S(2)}) collective-permute-start(f32[24,128]{1,0:T(8,128)S(1)} %add.45.refs_0_), channel_id=1, source_target_pairs={{0,2},{2,4},{4,6},{6,0},{1,3},{3,5},{5,7},{7,1},{8,10},{10,12},{12... | collective-permute-start | bytes 36872 | tf_op jit(solution)/shard_map/ppermute | solution.py:351
  121.7 8.2 %collective-permute-start.15 = (f32[24,128]{1,0:T(8,128)S(1)}, f32[24,128]{1,0:T(8,128)S(1)}, u32[]{:S(2)}, u32[]{:S(2)}) collective-permute-start(f32[24,128]{1,0:T(8,128)S(1)} %add.45.refs_0_), channel_id=1, source_target_pairs={{0,4},{2,6},{4,0},{6,2},{1,5},{3,7},{5,1},{7,3},{8,12},{10,14},{12... | collective-permute-start | bytes 36872 | tf_op jit(solution)/shard_map/ppermute | solution.py:351
  123.4 6.4 %collective-permute-start.16 = (f32[24,128]{1,0:T(8,128)S(1)}, f32[24,128]{1,0:T(8,128)S(1)}, u32[]{:S(2)}, u32[]{:S(2)}) collective-permute-start(f32[24,128]{1,0:T(8,128)S(1)} %add.45.refs_0_), channel_id=1, source_target_pairs={{0,6},{2,0},{4,2},{6,4},{1,7},{3,1},{5,3},{7,5},{8,14},{10,8},{12,... | collective-permute-start | bytes 36872 | tf_op jit(solution)/shard_map/ppermute | solution.py:351
  (9 other events, 7.1 us)

commit v5 on v4

--- a/solution.py
+++ b/solution.py
@@ -143,18 +143,30 @@
     )(sub, sent)
 
 
-def each_piece(count, own_ref, other_ref, place_ref, copy):
-    for q in range(count):
-        d = lax.rem(place_ref[0] - q + count, count)
-        for c in range(2):
-
-            @pl.when(place_ref[1] == c)
-            def _():
-                copy(own_ref, d, 2 * q + c)
-
-            @pl.when(place_ref[1] != c)
-            def _():
-                copy(other_ref, d, 2 * q + c)
+def each_piece(pieces, place_ref, copy):
+    count = len(pieces) // 2
+    for d in range(count):
+        q = lax.rem(place_ref[0] - d + count, count)
+        copy(pieces[d], 2 * q + place_ref[1])
+        copy(pieces[count + d], 2 * q + 1 - place_ref[1])
+
+
+def dot3(a, b):
+    a_high, b_high = a.astype(jnp.bfloat16), b.astype(jnp.bfloat16)
+    a_low = (a - a_high.astype(jnp.float32)).astype(jnp.bfloat16)
+    b_low = (b - b_high.astype(jnp.float32)).astype(jnp.bfloat16)
+
+    def part(x, y):
+        return jnp.dot(x, y, preferred_element_type=jnp.float32)
+
+    return part(a_high, b_high) + (part(a_high, b_low) + part(a_low, b_high))
+
+
+def turned_into(ext_ref, rows_ref, count):
+    filler = jnp.zeros((128 - rows_ref.shape[0], 128), jnp.float32)
+    for at in range(count):
+        lanes = slice(at * 128, (at + 1) * 128)
+        ext_ref[lanes, 128:] = jnp.concatenate([rows_ref[:, lanes], filler], 0).T
 
 
 VMEM = pl.BlockSpec(memory_space=pltpu.VMEM)
@@ -165,75 +177,75 @@
     return [jax.ShapeDtypeStruct(d, jnp.float32) for d in dims]
 
 
-def stiff_kernel(count, rows, own_ref, other_ref, place_ref, rest_ref, stiff_ref, up_ref, down_ref, basis_ref,
-                 sent_ref, ext_ref):
+def stiff_kernel(rows, count, *refs):
+    pieces, refs = refs[: 2 * count], refs[2 * count :]
+    place_ref, rest_ref, stiff_ref, up_ref, down_ref, image_ref, basis_ref, sent_ref, ext_ref = refs
     face = 2 * count * rows
     basis_ref[2 * PAD :, :face] = jnp.zeros((PAD, face), jnp.float32)
     basis_ref[:PAD, face:] = jnp.zeros((PAD, face), jnp.float32)
 
-    def copy(ref, d, at):
+    def copy(ref, at):
         for side in range(2):
-            start = side * face + at * rows
-            ext_ref[start : start + rows, :128] = ref[d, side * rows : (side + 1) * rows, :]
-        lanes = slice(at * rows, (at + 1) * rows)
-        basis_ref[: 2 * PAD, lanes] = ref[d, 2 * rows : 2 * rows + 2 * PAD, :]
-        lanes = slice(face + at * rows, face + (at + 1) * rows)
-        basis_ref[PAD:, lanes] = ref[d, 2 * rows + 2 * PAD :, :]
-
-    each_piece(count, own_ref, other_ref, place_ref, copy)
-    filler = jnp.zeros((128 - 3 * PAD, 128), jnp.float32)
-    for at in range(2 * face // 128):
-        lanes = slice(at * 128, (at + 1) * 128)
-        ext_ref[lanes, 128:] = jnp.concatenate([basis_ref[:, lanes], filler], 0).T
+            start = pl.multiple_of(side * face + at * rows, rows)
+            ext_ref[pl.ds(start, rows), :128] = ref[side * rows : (side + 1) * rows, :]
+        lanes = pl.ds(pl.multiple_of(at * rows, rows), rows)
+        basis_ref[: 2 * PAD, lanes] = ref[2 * rows : 2 * rows + 2 * PAD, :]
+        lanes = pl.ds(pl.multiple_of(face + at * rows, rows), rows)
+        basis_ref[PAD:, lanes] = ref[2 * rows + 2 * PAD :, :]
+
+    each_piece(pieces, place_ref, copy)
+    turned_into(ext_ref, basis_ref, 2 * face // 128)
     ext = ext_ref[...]
-    image = 0.25 * dot(stiff_ref[...], ext)
+    image = 0.25 * dot3(stiff_ref[...], ext)
     modes_image = image[:, 128:].T[: 3 * PAD]
     up_ref[:rows] = image[rows:, :128]
     up_ref[rows:] = modes_image[:, rows:]
     down_ref[:rows] = image[:rows, :128]
     down_ref[rows:] = modes_image[:, :rows]
+    image_ref[...] = modes_image
     coarse = dot(basis_ref[PAD : 2 * PAD, :], ext)
     coarse = jnp.concatenate([coarse[:, :128], coarse[:, 128:] + rest_ref[...]], 0)
     for t in range(sent_ref.shape[0]):
         sent_ref[t] = coarse
 
 
-def apply_stiffness(own, other, place, rest, stiff, subs):
-    count, rows = own.shape[0], stiff.shape[0] // 2
-    face = 2 * count * rows
-    return pl.pallas_call(
-        lambda *refs: stiff_kernel(count, rows, *refs),
+def apply_stiffness(pieces, place, rest, stiff, subs):
+    rows, face = stiff.shape[0] // 2, stiff.shape[1] // 2
+    return pl.pallas_call(
+        lambda *refs: stiff_kernel(rows, len(pieces) // 2, *refs),
         out_shape=shapes(
-            (rows + 3 * PAD, 128), (rows + 3 * PAD, 128), (3 * PAD, 2 * face), (subs, 2 * PAD, 128)
+            (rows + 3 * PAD, 128), (rows + 3 * PAD, 128), (3 * PAD, 2 * rows), (3 * PAD, 2 * face),
+            (subs, 2 * PAD, 128),
         ),
-        in_specs=[VMEM, VMEM, SMEM, VMEM, VMEM],
-        out_specs=[VMEM] * 4,
+        in_specs=[VMEM] * len(pieces) + [SMEM, VMEM, VMEM],
+        out_specs=[VMEM] * 5,
         scratch_shapes=[pltpu.VMEM((2 * face, 256), jnp.float32)],
         name="apply_stiffness",
-    )(own, other, place, rest, stiff)
-
-
-def search_kernel(count, rows, share, own_ref, other_ref, place_ref, basis_ref, weights_ref, traces_ref,
-                  modes_ref, sent_ref, sums_ref):
+    )(*pieces, place, rest, stiff)
+
+
+def search_kernel(rows, count, share, *refs):
+    pieces, refs = refs[: 2 * count], refs[2 * count :]
+    place_ref, basis_ref, weights_ref, traces_ref, modes_ref, sent_ref = refs
     face = 2 * count * rows
     wide = NEAR * PAD
     head = 2 * rows
-    sums_ref[...] = own_ref[0, head : head + 7 * PAD, :] + other_ref[0, head : head + 7 * PAD, :]
-    for d in range(1, count):
-        sums_ref[...] += own_ref[d, head : head + 7 * PAD, :] + other_ref[d, head : head + 7 * PAD, :]
-
-    def copy(ref, d, at):
+    sums = pieces[0][head : head + 7 * PAD, :]
+    for ref in pieces[1:]:
+        sums = sums + ref[head : head + 7 * PAD, :]
+
+    def copy(ref, at):
         for side in range(2):
-            start = side * face + at * rows
-            traces_ref[start : start + rows, :] = ref[d, side * rows : (side + 1) * rows, :]
+            at_rows = pl.ds(pl.multiple_of(side * face + at * rows, rows), rows)
+            traces_ref[at_rows, :] = ref[side * rows : (side + 1) * rows, :]
             low = head + 7 * PAD + side * wide
-            modes_ref[:, start : start + rows] = ref[d, low : low + wide, :]
-
-    each_piece(count, own_ref, other_ref, place_ref, copy)
+            modes_ref[:, at_rows] = ref[low : low + wide, :]
+
+    each_piece(pieces, place_ref, copy)
     weights = jnp.concatenate([weights_ref[...], jnp.zeros((128 - wide, 128), jnp.float32)], 0)
-    change = dot(sums_ref[3 * PAD :, :], weights)
+    change = dot(sums[3 * PAD :], weights)
     rhs = dot(basis_ref[PAD : 2 * PAD, :], traces_ref[...]) - change[3 * PAD :]
-    flex_search = sums_ref[: 3 * PAD, :] - change[: 3 * PAD]
+    flex_search = sums[: 3 * PAD] - change[: 3 * PAD]
     lane = lax.broadcasted_iota(jnp.int32, (PAD, 128), 1)
     mine = (place_ref[0] * 2 + place_ref[1]) * share
     tail = jnp.zeros((PAD, 128), jnp.float32)
@@ -243,25 +255,108 @@
         tail = jnp.where(lane // share == b, block, tail)
     for b in range(3):
         low = 3 * share + b * 3 * PAD
-        block = sums_ref[(3 + b) * PAD : (4 + b) * PAD, :]
-        block = pltpu.roll(block, (low - wide) % 128, 1)
+        block = pltpu.roll(sums[(3 + b) * PAD : (4 + b) * PAD], (low - wide) % 128, 1)
         tail = jnp.where((lane >= low) & (lane < low + 3 * PAD), block, tail)
     sent = jnp.concatenate([rhs, tail], 0)
     for t in range(sent_ref.shape[0]):
         sent_ref[t] = sent
 
 
-def order_search(own, other, place, basis, weights, subs, rows):
-    count = own.shape[0]
-    face = 2 * count * rows
-    return pl.pallas_call(
-        lambda *refs: search_kernel(count, rows, 128 // (2 * count), *refs),
+def order_search(pieces, place, basis, weights, subs, rows):
+    face = len(pieces) * rows
+    return pl.pallas_call(
+        lambda *refs: search_kernel(rows, len(pieces) // 2, 128 // len(pieces), *refs),
         out_shape=shapes((2 * face, 128), (NEAR * PAD, 2 * face), (subs, 2 * PAD, 128)),
-        in_specs=[VMEM, VMEM, SMEM, VMEM, VMEM],
+        in_specs=[VMEM] * len(pieces) + [SMEM, VMEM, VMEM],
         out_specs=[VMEM] * 3,
-        scratch_shapes=[pltpu.VMEM((7 * PAD, 128), jnp.float32)],
         name="order_search",
-    )(own, other, place, basis, weights)
+    )(*pieces, place, basis, weights)
+
+
+def flex_kernel(flex_ref, traces_ref, modes_ref, weights_ref, own_ref, own_modes_ref, field_ref, own_basis_ref,
+                flex_modes_ref, image_ref, search_ref, res_ref, turned_ref, ext_ref):
+    rows = field_ref.shape[0]
+    wide = NEAR * PAD
+    weights = jnp.concatenate([weights_ref[...], jnp.zeros((128 - wide, 128), jnp.float32)], 0)
+    ext_ref[:, :128] = traces_ref[...]
+    turned_into(ext_ref, modes_ref, traces_ref.shape[0] // 128)
+    both = dot3(flex_ref[...], ext_ref[...])
+    image_ref[...] = both[:, :128] - dot(both[:, 128:], weights)
+    own_modes = jnp.concatenate(
+        [own_modes_ref[...], jnp.zeros((128 - wide, 2 * rows), jnp.float32)], 0
+    ).T
+    search_ref[...] = own_ref[...] - dot(own_modes, weights)
+    turned = jnp.concatenate(
+        [
+            flex_modes_ref[...], own_basis_ref[...],
+            jnp.zeros((128 - 6 * PAD, 2 * rows), jnp.float32),
+        ],
+        0,
+    ).T
+    turned_ref[...] = turned
+    gap = jnp.zeros((3 * PAD, 128), jnp.float32)
+    none = jnp.zeros((128 - 6 * PAD, 128), jnp.float32)
+    shifted = jnp.concatenate([gap, weights_ref[PAD : 4 * PAD, :], none], 0)
+    res_ref[...] = field_ref[...] - dot(turned[rows:], shifted)
+
+
+def apply_flexibility(flex, traces, modes, weights, own, own_modes, field, own_basis, flex_modes):
+    rows = field.shape[0]
+    return pl.pallas_call(
+        flex_kernel,
+        out_shape=shapes((2 * rows, 128), (2 * rows, 128), (rows, 128), (2 * rows, 128)),
+        in_specs=[VMEM] * 9,
+        out_specs=[VMEM] * 4,
+        scratch_shapes=[pltpu.VMEM((traces.shape[0], 256), jnp.float32)],
+        name="apply_flexibility",
+    )(flex, traces, modes, weights, own, own_modes, field, own_basis, flex_modes)
+
+
+def last_kernel(subs, modes, share, place_ref, second_ref, inverse_ref, near_ref, out_ref):
+    mine = (place_ref[0] * 2 + place_ref[1]) * share
+    lane = lax.broadcasted_iota(jnp.int32, (subs, 128), 1)
+    row = lax.broadcasted_iota(jnp.int32, (subs, 128), 0)
+    rhs = jnp.concatenate(
+        [second_ref[pl.ds(i, subs, stride=2 * PAD), :] for i in range(PAD)], axis=0
+    )
+    weights = dot(inverse_ref[...], pltpu.roll(rhs, lax.rem(128 - mine, 128), 1))
+
+    def earlier(x):
+        return jnp.where(row == 0, 0.0, pltpu.roll(x, 1, 0))
+
+    def later(x):
+        return jnp.where(row == subs - 1, 0.0, pltpu.roll(x, subs - 1, 0))
+
+    near = []
+    for k in range(modes):
+        here = weights[k * subs : (k + 1) * subs]
+        near.append((earlier(here), here, later(here)))
+    out = []
+    for i in range(PAD):
+        tail = second_ref[pl.ds(PAD + i, subs, stride=2 * PAD), :]
+        parts = []
+        for b in range(3):
+            part = tail if b == 0 else pltpu.roll(tail, 128 - b * share, 1)
+            if i < modes:
+                for c in range(3):
+                    for k in range(modes):
+                        at = 3 * share + b * 3 * PAD + c * PAD + k
+                        part = part - tail[:, at : at + 1] * near[k][c]
+            parts.append(part)
+        total = parts[1] + later(parts[0]) + earlier(parts[2])
+        out.append(jnp.where(lane < share, total, 0.0))
+    last = dot(near_ref[PAD : 4 * PAD, :], jnp.concatenate(out, 0))
+    out_ref[...] = pltpu.roll(last, mine, 1)
+
+
+def last_weights(place, second, inverse, near, subs, modes, share):
+    return pl.pallas_call(
+        lambda *refs: last_kernel(subs, modes, share, *refs),
+        out_shape=shapes((3 * PAD, 128))[0],
+        in_specs=[SMEM] + [VMEM] * 3,
+        out_specs=VMEM,
+        name="last_weights",
+    )(place, second, inverse, near)
 
 
 def direction_kernel(subs, second_ref, near_ref, turned_ref, image_ref, search_ref, res_ref, low_ref, high_ref,
@@ -358,14 +453,7 @@
 
 def gathered(piece):
     pieces = along_x(piece)
-    own = jnp.stack(pieces)
-    return own, core_swap(own)
-
-
-def spread(part, weights):
-    return lax.dot_general(
-        part, weights, (((0,), (0,)), ((), ())), precision=HIGH, preferred_element_type=jnp.float32
-    )
+    return pieces + [core_swap(part) for part in pieces]
 
 
 def per_device(gap, flexibility, stiffness, modes, mode_counts):
@@ -402,18 +490,17 @@
     rest = jnp.pad(
         jnp.eye(PAD, dtype=jnp.float32) * (1.0 - active)[:, None], ((0, 0), (PAD, 128 - 2 * PAD))
     )
-    up, down, basis, sent = apply_stiffness(*gathered(piece), place, rest, stiff, subs)
-    image, modes_image = (down[:rows], up[:rows]), (down[rows:], up[rows:])
+    up, down, modes_image, basis, sent = apply_stiffness(gathered(piece), place, rest, stiff, subs)
     first = to_all(sent, SUB).reshape(subs * 2 * PAD, 128)
     before = moved_along(up, 1)
     after = moved_along(down, -1)
-    top = (image[0] - before[:rows]) * inner
-    bottom = (image[1] - after[:rows]) * live
+    top = (down[:rows] - before[:rows]) * inner
+    bottom = (up[:rows] - after[:rows]) * live
     own_traces = jnp.concatenate([top, bottom], 0)
     gone = jnp.zeros((PAD, rows), jnp.float32)
-    modes_top = jnp.concatenate([gone, modes_image[0], gone], 0)
+    modes_top = jnp.concatenate([gone, modes_image[:, :rows], gone], 0)
     modes_top = modes_top - jnp.concatenate([before[rows:], gone, gone], 0)
-    modes_bottom = jnp.concatenate([gone, modes_image[1], gone], 0)
+    modes_bottom = jnp.concatenate([gone, modes_image[:, rows:], gone], 0)
     modes_bottom = modes_bottom - jnp.concatenate([gone, gone, after[rows:]], 0)
     own_modes = jnp.concatenate([modes_top * inner, modes_bottom * live], 1)
 
@@ -431,48 +518,22 @@
     )
     pieces = gathered(piece)
     inverse, near, weights = coarse_inverse(sub.astype(jnp.int32)[None], first, subs, mode_count)
-    search_traces, modes_traces, sent = order_search(*pieces, place, basis, weights, subs, rows)
-    mine = (place[0] * 2 + place[1]) * (loads // lanes)
-    share = loads // lanes
+    search_traces, modes_traces, sent = order_search(pieces, place, basis, weights, subs, rows)
     second = to_all(sent, SUB)
 
-    image = dot(flex, search_traces) - dot(dot_nt(flex, modes_traces), weights)
-    own_search = own_traces - spread(own_modes, weights)
-    own_res = field - spread(own_basis[:, rows:], weights[PAD : 4 * PAD])
-    turned = jnp.concatenate([flex_modes, own_basis], 0)
-    turned = jnp.pad(turned, ((0, 128 - 6 * PAD), (0, 0))).T
+    image, own_search, own_res, turned = apply_flexibility(
+        flex, search_traces, modes_traces, weights, own_traces, own_modes, field, own_basis, flex_modes
+    )
+    second = second.reshape(subs * 2 * PAD, 128)
     low, high, direction, sums = project_direction(
-        second.reshape(subs * 2 * PAD, 128), near, turned, image, own_search, own_res, subs
+        second, near, turned, image, own_search, own_res, subs
     )
     totals = from_all(sums, ALL)
     totals = totals.sum(0)
 
     after = moved_along(low, -1)
-    near = near[PAD : 4 * PAD]
-    all_rhs = second[:, :PAD].transpose(1, 0, 2).reshape(PAD * subs, loads)
-    my_rhs = lax.dynamic_slice_in_dim(all_rhs, mine, share, 1)
-    my_weights = dot(inverse, my_rhs).reshape(PAD, subs, share).transpose(1, 0, 2)
-    my_weights = jnp.pad(my_weights, ((1, 1), (0, 0), (0, 0)))
-    my_weights = jnp.concatenate([my_weights[b : b + subs] for b in range(3)], 1)
-    tail = second[:, PAD:]
-    parts = []
-    for b in range(3):
-        start = 3 * share + b * 3 * PAD
-        product = lax.dot_general(
-            tail[:, :, start : start + 3 * PAD], my_weights, (((2,), (1,)), ((0,), (0,))),
-            precision=HIGH, preferred_element_type=jnp.float32,
-        )
-        parts.append(tail[:, :, b * share : (b + 1) * share] - product)
-    none = jnp.zeros((1, PAD, share), jnp.float32)
-    last_rhs = (
-        parts[1]
-        + jnp.concatenate([parts[0][1:], none], 0)
-        + jnp.concatenate([none, parts[2][:-1]], 0)
-    )
-    weights = dot(near, last_rhs.transpose(1, 0, 2).reshape(PAD * subs, share))
-    weights = lax.dynamic_update_slice_in_dim(
-        jnp.zeros((3 * PAD, loads), jnp.float32), weights, mine, 1
-    )
+    share = loads // lanes
+    weights = last_weights(place, second, inverse, near, subs, mode_count, share)
     weights = weights + core_swap(weights)
     return results(totals, direction, own_res, high, after, turned, live, along_x(weights))
 

time: 133 us -> 135 us (1.015)
  the two profiles are of different devices: /device:TPU:1 before, /device:TPU:160 now
where the time goes in v5:
time: 135 us
  starting transfers between devices  56.9 us (42%)
  waiting for transfers between devices  34.9 us (26%)
  Pallas kernels  26 us (19%)
  local copies, waits for them, and re-layouts  6.44 us (5%)
  other arithmetic  5.34 us (4%)
  matrix products  3.15 us (2%)
  between operations  1.8 us (1%)
    ppermute x5, starting transfers between devices, moved_along(): lax.ppermute(block, SUB, [(i - distance, i) for i in range(n) if 0 <= i -...  20.1 us
    ppermute x9, waiting for transfers between devices, along_x(): lax.ppermute(piece, 'x', [(i, (i + d) % n) for i in range(n)])  19.3 us
    all_to_all x2, starting transfers between devices, to_all(): return lax.all_to_all(values, axis, 0, 0, tiled=True)  15.1 us
    ppermute x9, starting transfers between devices, along_x(): lax.ppermute(piece, 'x', [(i, (i + d) % n) for i in range(n)])  11.2 us
    all_to_all x1, starting transfers between devices, from_all(): lax.all_to_all(jnp.broadcast_to(value[None], (count, *value.shape)), axis...  10.5 us
    ppermute x5, waiting for transfers between devices, moved_along(): lax.ppermute(block, SUB, [(i - distance, i) for i in range(n) if 0 <= i -...  10.3 us
    pallas_call x1, Pallas kernels, coarse_inverse(): pl.pallas_call(lambda *refs: inverse_kernel(subs, modes, *refs), out_shap...  5.39 us
    pallas_call x1, Pallas kernels, apply_stiffness(): pl.pallas_call(lambda *refs: stiff_kernel(rows, len(pieces) // 2, *refs),...  4.82 us
  transfers between devices with their start and end apart: 26, of which 13 were waited for; matrix products, arithmetic and copies ran while one was open for 7% of the time, Pallas kernels for 10%

profile of v5, /device:TPU:160, one launch (start us, length us, event | category | flops | bytes accessed | tf_op | source)
XLA Modules:
  0.0 134.5 jit_solution(3744496152184671009)
XLA Ops:
  2.1 5.4 %collective-permute-start.1 = (f32[8,128]{1,0:T(8,128)S(1)}, f32[8,128]{1,0:T(8,128)S(1)}, u32[]{:S(2)}, u32[]{:S(2)}) collective-permute-start(f32[8,128]{1,0:T(8,128)S(1)} %get-tuple-element.50), channel_id=1, source_target_pairs={{8,0},{16,8},{24,16},{32,24},{40,32},{48,40},{56,48},{64,56},{72,6... | collective-permute-start | bytes 12296 | tf_op jit(solution)/shard_map/ppermute | solution.py:427
  8.3 1.9 %collective-permute-start = (f32[136,128]{1,0:T(8,128)S(1)}, f32[136,128]{1,0:T(8,128)S(1)}, u32[]{:S(2)}, u32[]{:S(2)}) collective-permute-start(f32[136,128]{1,0:T(8,128)S(1)} %pad_maximum_fusion.1), channel_id=1, source_target_pairs={{0,8},{8,16},{16,24},{24,32},{32,40},{40,48},{48,56},{56,64},{64,7... | collective-permute-start | bytes 208904 | tf_op jit(solution)/shard_map/ppermute | solution.py:427
  10.3 6.3 %collective-permute-done = f32[136,128]{1,0:T(8,128)S(1)} collective-permute-done((f32[136,128]{1,0:T(8,128)S(1)}, f32[136,128]{1,0:T(8,128)S(1)}, u32[]{:S(2)}, u32[]{:S(2)}) %collective-permute-start) | collective-permute-done | bytes 69664 | tf_op jit(solution)/shard_map/ppermute | solution.py:427
  17.5 2.8 %collective-permute-start.4 = (f32[288,128]{1,0:T(8,128)S(1)}, f32[288,128]{1,0:T(8,128)S(1)}, u32[]{:S(2)}, u32[]{:S(2)}) collective-permute-start(f32[288,128]{1,0:T(8,128)S(1)} %get-tuple-element.55.refs_0_), channel_id=1, source_target_pairs={{0,6},{2,0},{4,2},{6,4},{1,7},{3,1},{5,3},{7,5},{8,14},{10,8},{12,... | collective-permute-start | bytes 442376 | tf_op jit(solution)/shard_map/ppermute | solution.py:446
  21.2 0.9 collective-permute-start.2
  22.1 3.1 %collective-permute-done.4.refs_3_ = f32[288,128]{1,0:T(8,128)S(1)} collective-permute-done((f32[288,128]{1,0:T(8,128)S(1)}, f32[288,128]{1,0:T(8,128)S(1)}, u32[]{:S(2)}, u32[]{:S(2)}) %collective-permute-start.4) | collective-permute-done | bytes 147488 | tf_op jit(solution)/shard_map/ppermute | solution.py:446
  25.2 2.2 %collective-permute-done.3.refs_2_ = f32[288,128]{1,0:T(8,128)S(1)} collective-permute-done((f32[288,128]{1,0:T(8,128)S(1)}, f32[288,128]{1,0:T(8,128)S(1)}, u32[]{:S(2)}, u32[]{:S(2)}) %collective-permute-start.3) | collective-permute-done | bytes 147488 | tf_op jit(solution)/shard_map/ppermute | solution.py:446
  27.4 1.5 %collective-permute-done.2.refs_1_ = f32[288,128]{1,0:T(8,128)S(1)} collective-permute-done((f32[288,128]{1,0:T(8,128)S(1)}, f32[288,128]{1,0:T(8,128)S(1)}, u32[]{:S(2)}, u32[]{:S(2)}) %collective-permute-start.2) | collective-permute-done | bytes 147488 | tf_op jit(solution)/shard_map/ppermute | solution.py:446
  31.0 4.8 %apply_stiffness.1 = (f32[152,128]{1,0:T(8,128)}, f32[152,128]{1,0:T(8,128)}, f32[24,256]{1,0:T(8,128)}, f32[24,2048]{1,0:T(8,128)}, f32[32,16,128]{2,1,0:T(8,128)}) custom-call(f32[288,128]{1,0:T(8,128)} %copy-done.5, f32[288,128]{1,0:T(8,128)} %copy-done.16, f32[288,128]{1,0:T(8,128)} %copy-done.15, f32[288,128]{1,0:T(8,128)} %copy-done.14, ...), custom_call_target="tpu_custom_call" | custom-call | tf_op jit(solution)/shard_map/apply_stiffness/pallas_call | solution.py:214
  35.8 7.4 %all-to-all-start = ((f32[32,16,128]{2,1,0:T(8,128)}), f32[32,16,128]{2,1,0:T(8,128)S(1)}, u32[]{:S(2)}, u32[]{:S(2)}) async-start(f32[32,16,128]{2,1,0:T(8,128)} %get-tuple-element.25), calls=%async_computation | async-start | bytes 524288 | tf_op jit(solution)/shard_map/all_to_all | solution.py:451
  43.2 5.5 %collective-permute-start.10 = (f32[152,128]{1,0:T(8,128)}, f32[152,128]{1,0:T(8,128)S(1)}, u32[]{:S(2)}, u32[]{:S(2)}) collective-permute-start(f32[152,128]{1,0:T(8,128)} %get-tuple-element.21), channel_id=1, source_target_pairs={{8,0},{16,8},{24,16},{32,24},{40,32},{48,40},{56,48},{64,56},{72,6... | collective-permute-start | bytes 233480 | tf_op jit(solution)/shard_map/ppermute | solution.py:427
  48.7 1.9 %collective-permute-start.9 = (f32[152,128]{1,0:T(8,128)}, f32[152,128]{1,0:T(8,128)S(1)}, u32[]{:S(2)}, u32[]{:S(2)}) collective-permute-start(f32[152,128]{1,0:T(8,128)} %get-tuple-element.22), channel_id=1, source_target_pairs={{0,8},{8,16},{16,24},{24,32},{32,40},{40,48},{48,56},{56,64},{64,7... | collective-permute-start | bytes 233480 | tf_op jit(solution)/shard_map/ppermute | solution.py:427
  50.7 2.7 %fusion.32.flex_modes_ref = f32[24,256]{1,0:T(8,128)S(1)} fusion(f32[24,2048]{1,0:T(8,128)} %get-tuple-element.23.refs_9_, f32[256,2048]{1,0:T(8,128)S(1)} %bitcast.28), kind=kOutput, calls=%fused_computation.64 | convolution fusion | flops 150994944 | bytes 2318336 | tf_op jit(solution)/shard_map/dot_general | solution.py:23
  53.4 3.9 %collective-permute-done.9 = f32[152,128]{1,0:T(8,128)S(1)} collective-permute-done((f32[152,128]{1,0:T(8,128)}, f32[152,128]{1,0:T(8,128)S(1)}, u32[]{:S(2)}, u32[]{:S(2)}) %collective-permute-start.9) | collective-permute-done | bytes 77856 | tf_op jit(solution)/shard_map/ppermute | solution.py:427
  60.3 5.3 %collective-permute-done.13.refs_3_ = f32[392,128]{1,0:T(8,128)S(1)} collective-permute-done((f32[392,128]{1,0:T(8,128)S(1)}, f32[392,128]{1,0:T(8,128)S(1)}, u32[]{:S(2)}, u32[]{:S(2)}) %collective-permute-start.13) | collective-permute-done | bytes 200736 | tf_op jit(solution)/shard_map/ppermute | solution.py:446
  65.6 1.8 %collective-permute-done.12.refs_2_ = f32[392,128]{1,0:T(8,128)S(1)} collective-permute-done((f32[392,128]{1,0:T(8,128)S(1)}, f32[392,128]{1,0:T(8,128)S(1)}, u32[]{:S(2)}, u32[]{:S(2)}) %collective-permute-start.12) | collective-permute-done | bytes 200736 | tf_op jit(solution)/shard_map/ppermute | solution.py:446
  67.5 2.1 %collective-permute-done.11.refs_1_ = f32[392,128]{1,0:T(8,128)S(1)} collective-permute-done((f32[392,128]{1,0:T(8,128)S(1)}, f32[392,128]{1,0:T(8,128)S(1)}, u32[]{:S(2)}, u32[]{:S(2)}) %collective-permute-start.11) | collective-permute-done | bytes 200736 | tf_op jit(solution)/shard_map/ppermute | solution.py:446
  70.4 5.4 %coarse_inverse.1 = (f32[256,256]{1,0:T(8,128)}, f32[40,256]{1,0:T(8,128)}, f32[40,128]{1,0:T(8,128)}) custom-call(s32[1]{0:T(128)} %bitcast.9.refs_0_, f32[512,128]{1,0:T(8,128)} %bitcast.32), custom_call_target="tpu_custom_call" | custom-call | tf_op jit(solution)/shard_map/coarse_inverse/pallas_call | solution.py:132
  76.6 2.9 %order_search.1 = (f32[2048,128]{1,0:T(8,128)}, f32[40,2048]{1,0:T(8,128)}, f32[32,16,128]{2,1,0:T(8,128)}) custom-call(f32[392,128]{1,0:T(8,128)} %copy-done.4, f32[392,128]{1,0:T(8,128)} %copy-done.9, f32[392,128]{1,0:T(8,128)} %copy-done.8, f32[392,128]{1,0:T(8,128)} %copy-done.7, f32[392,128]{1,0:T(8,128)} %copy-done.10, f32[392,128]{1,0:T(8,128)} %copy-done.13, ...), custom_call_target="tpu_custom_call" | custom-call | tf_op jit(solution)/shard_map/order_search/pallas_call | solution.py:267
  79.6 7.7 %all-to-all-start.1 = ((f32[32,16,128]{2,1,0:T(8,128)}), f32[32,16,128]{2,1,0:T(8,128)S(1)}, u32[]{:S(2)}, u32[]{:S(2)}) async-start(f32[32,16,128]{2,1,0:T(8,128)} %get-tuple-element.27), calls=%async_computation.1 | async-start | bytes 524288 | tf_op jit(solution)/shard_map/all_to_all | solution.py:451
  88.6 4.6 %apply_flexibility.1 = (f32[256,128]{1,0:T(8,128)}, f32[256,128]{1,0:T(8,128)}, f32[128,128]{1,0:T(8,128)}, f32[256,128]{1,0:T(8,128)}) custom-call(f32[256,2048]{1,0:T(8,128)} %bitcast.27, f32[2048,128]{1,0:T(8,128)} %get-tuple-element.29.traces_ref, f32[40,2048]{1,0:T(8,128)} %get-tuple-element.30.modes_ref, ...), custom_call_target="tpu_custom_call" | custom-call | tf_op jit(solution)/shard_map/apply_flexibility/pallas_call | solution.py:305
  93.1 3.8 %all-to-all-done.1 = f32[32,16,128]{2,1,0:T(8,128)S(1)} async-done(((f32[32,16,128]{2,1,0:T(8,128)}), f32[32,16,128]{2,1,0:T(8,128)S(1)}, u32[]{:S(2)}, u32[]{:S(2)}) %all-to-all-start.1) | async-done | bytes 262176 | tf_op jit(solution)/shard_map/all_to_all | solution.py:451
  97.6 2.3 %project_direction.1 = (f32[128,128]{1,0:T(8,128)}, f32[128,128]{1,0:T(8,128)}, f32[128,128]{1,0:T(8,128)}, f32[2,128]{1,0:T(2,128)}) custom-call(f32[512,128]{1,0:T(8,128)} %bitcast.29, f32[40,256]{1,0:T(8,128)} %get-tuple-element.28.refs_1_.refs_3_, f32[256,128]{1,0:T(8,128)} %get-tuple-element.31.refs_2_.turned_ref, ...), custom_call_target="tpu_custom_call" | custom-call | tf_op jit(solution)/shard_map/project_direction/pallas_call | solution.py:391
  100.0 1.4 %broadcast_in_dim.7 = f32[256,2,128]{2,1,0:T(2,128)} broadcast(f32[2,128]{1,0:T(2,128)} %get-tuple-element.35), dimensions={1,2} | broadcast | bytes 263168 | tf_op jit(solution)/shard_map/broadcast_in_dim | solution.py:439
  101.4 10.5 %all-to-all-start.2 = ((f32[256,2,128]{2,1,0:T(2,128)}), f32[256,2,128]{2,1,0:T(2,128)S(1)}, u32[]{:S(2)}, u32[]{:S(2)}) async-start(f32[256,2,128]{2,1,0:T(2,128)} %broadcast_in_dim.7), calls=%async_computation.2 | async-start | bytes 524288 | tf_op jit(solution)/shard_map/all_to_all | solution.py:438
  112.0 5.4 %collective-permute-start.18 = (f32[128,128]{1,0:T(8,128)}, f32[128,128]{1,0:T(8,128)S(1)}, u32[]{:S(2)}, u32[]{:S(2)}) collective-permute-start(f32[128,128]{1,0:T(8,128)} %get-tuple-element.38), channel_id=1, source_target_pairs={{8,0},{16,8},{24,16},{32,24},{40,32},{48,40},{56,48},{64,56},{72,6... | collective-permute-start | bytes 196616 | tf_op jit(solution)/shard_map/ppermute | solution.py:427
  117.4 4.1 %last_weights.1 = f32[24,128]{1,0:T(8,128)} custom-call(s32[2]{0:T(128)} %pad_add_fusion.refs_8_.refs_0_, f32[512,128]{1,0:T(8,128)} %bitcast.30, f32[256,256]{1,0:T(8,128)} %get-tuple-element.39.refs_2_, f32[40,256]{1,0:T(8,128)} %get-tuple-element.28.refs_1_.refs_3_), custom_call_target="tpu_custom_call" | custom-call | tf_op jit(solution)/shard_map/last_weights/pallas_call | solution.py:353
  121.5 1.4 %collective-permute-done.19 = f32[24,128]{1,0:T(8,128)S(1)} collective-permute-done((f32[24,128]{1,0:T(8,128)}, f32[24,128]{1,0:T(8,128)S(1)}, u32[]{:S(2)}, u32[]{:S(2)}) %collective-permute-start.19) | collective-permute-done | bytes 12320 | tf_op jit(solution)/shard_map/ppermute | solution.py:433
  123.6 2.7 %collective-permute-start.22 = (f32[24,128]{1,0:T(8,128)S(1)}, f32[24,128]{1,0:T(8,128)S(1)}, u32[]{:S(2)}, u32[]{:S(2)}) collective-permute-start(f32[24,128]{1,0:T(8,128)S(1)} %add.19.refs_0_), channel_id=1, source_target_pairs={{0,6},{2,0},{4,2},{6,4},{1,7},{3,1},{5,3},{7,5},{8,14},{10,8},{12,... | collective-permute-start | bytes 36872 | tf_op jit(solution)/shard_map/ppermute | solution.py:446
  127.1 0.9 collective-permute-start.20
  128.8 2.7 %collective-permute-done.21.refs_2_ = f32[24,128]{1,0:T(8,128)S(1)} collective-permute-done((f32[24,128]{1,0:T(8,128)S(1)}, f32[24,128]{1,0:T(8,128)S(1)}, u32[]{:S(2)}, u32[]{:S(2)}) %collective-permute-start.21) | collective-permute-done | bytes 12320 | tf_op jit(solution)/shard_map/ppermute | solution.py:446
  132.7 1.8 %results.1 = (f32[1,128,128]{2,1,0:T(8,128)}, f32[1,128,128]{2,1,0:T(8,128)}) custom-call(f32[2,128]{1,0:T(2,128)} %reduce_sum.9.totals_ref, f32[128,128]{1,0:T(8,128)} %get-tuple-element.36.direction_ref, f32[128,128]{1,0:T(8,128)} %get-tuple-element.34.refs_5_.res_ref, f32[128,128]{1,0:T(8,128)} %get-tuple-element.37.high_ref, f32[128,128]{1,0:T(8,128)} %copy-done.22, ...), custom_call_target="tpu_custom_call" | custom-call | tf_op jit(solution)/shard_map/results/pallas_call | solution.py:416
  (124 shorter events, 15.4 us)
Async XLA Ops:
  2.1 15.4 %collective-permute-start.1 = (f32[8,128]{1,0:T(8,128)S(1)}, f32[8,128]{1,0:T(8,128)S(1)}, u32[]{:S(2)}, u32[]{:S(2)}) collective-permute-start(f32[8,128]{1,0:T(8,128)S(1)} %get-tuple-element.50), channel_id=1, source_target_pairs={{8,0},{16,8},{24,16},{32,24},{40,32},{48,40},{56,48},{64,56},{72,6... | collective-permute-start | bytes 12296 | tf_op jit(solution)/shard_map/ppermute | solution.py:427
  8.3 27.5 %copy-start.3 = (f32[128,128]{1,0:T(8,128)}, f32[128,128]{1,0:T(8,128)S(1)}, u32[]{:S(2)}) copy-start(f32[128,128]{1,0:T(8,128)S(1)} %multiply_bitcast_fusion.field_ref) | copy-start | bytes 196612
  8.3 8.3 %collective-permute-start = (f32[136,128]{1,0:T(8,128)S(1)}, f32[136,128]{1,0:T(8,128)S(1)}, u32[]{:S(2)}, u32[]{:S(2)}) collective-permute-start(f32[136,128]{1,0:T(8,128)S(1)} %pad_maximum_fusion.1), channel_id=1, source_target_pairs={{0,8},{8,16},{16,24},{24,32},{32,40},{40,48},{48,56},{56,64},{64,7... | collective-permute-start | bytes 208904 | tf_op jit(solution)/shard_map/ppermute | solution.py:427
  10.3 40.4 %copy-start = (f32[1,2,128,2048]{3,2,1,0:T(8,128)S(1)}, f32[1,2,128,2048]{3,2,1,0:T(8,128)}, u32[]{:S(2)}) copy-start(f32[1,2,128,2048]{3,2,1,0:T(8,128)} %param.6) | copy-start | bytes 6291460
  17.5 7.7 %collective-permute-start.4 = (f32[288,128]{1,0:T(8,128)S(1)}, f32[288,128]{1,0:T(8,128)S(1)}, u32[]{:S(2)}, u32[]{:S(2)}) collective-permute-start(f32[288,128]{1,0:T(8,128)S(1)} %get-tuple-element.55.refs_0_), channel_id=1, source_target_pairs={{0,6},{2,0},{4,2},{6,4},{1,7},{3,1},{5,3},{7,5},{8,14},{10,8},{12,... | collective-permute-start | bytes 442376 | tf_op jit(solution)/shard_map/ppermute | solution.py:446
  20.4 7.1 %collective-permute-start.3 = (f32[288,128]{1,0:T(8,128)S(1)}, f32[288,128]{1,0:T(8,128)S(1)}, u32[]{:S(2)}, u32[]{:S(2)}) collective-permute-start(f32[288,128]{1,0:T(8,128)S(1)} %get-tuple-element.55.refs_0_), channel_id=1, source_target_pairs={{0,4},{2,6},{4,0},{6,2},{1,5},{3,7},{5,1},{7,3},{8,12},{10,14},{12... | collective-permute-start | bytes 442376 | tf_op jit(solution)/shard_map/ppermute | solution.py:446
  21.2 7.7 %collective-permute-start.2 = (f32[288,128]{1,0:T(8,128)S(1)}, f32[288,128]{1,0:T(8,128)S(1)}, u32[]{:S(2)}, u32[]{:S(2)}) collective-permute-start(f32[288,128]{1,0:T(8,128)S(1)} %get-tuple-element.55.refs_0_), channel_id=1, source_target_pairs={{0,2},{2,4},{4,6},{6,0},{1,3},{3,5},{5,7},{7,1},{8,10},{10,12},{12... | collective-permute-start | bytes 442376 | tf_op jit(solution)/shard_map/ppermute | solution.py:446
  22.1 8.0 %collective-permute-start.5 = (f32[288,128]{1,0:T(8,128)S(1)}, f32[288,128]{1,0:T(8,128)S(1)}, u32[]{:S(2)}, u32[]{:S(2)}) collective-permute-start(f32[288,128]{1,0:T(8,128)S(1)} %get-tuple-element.55.refs_0_), channel_id=1, source_target_pairs={{0,1},{1,0},{2,3},{3,2},{4,5},{5,4},{6,7},{7,6},{8,9},{9,8},{10,11... | collective-permute-start | bytes 442376 | tf_op jit(solution)/shard_map/ppermute | solution.py:433
  25.2 4.9 %collective-permute-start.8 = (f32[288,128]{1,0:T(8,128)S(1)}, f32[288,128]{1,0:T(8,128)S(1)}, u32[]{:S(2)}, u32[]{:S(2)}) collective-permute-start(f32[288,128]{1,0:T(8,128)S(1)} %collective-permute-done.4.refs_3_), channel_id=1, source_target_pairs={{0,1},{1,0},{2,3},{3,2},{4,5},{5,4},{6,7},{7,6},{8,9},{9,8},{10,11... | collective-permute-start | bytes 442376 | tf_op jit(solution)/shard_map/ppermute | solution.py:433
  27.4 2.8 %collective-permute-start.7 = (f32[288,128]{1,0:T(8,128)S(1)}, f32[288,128]{1,0:T(8,128)S(1)}, u32[]{:S(2)}, u32[]{:S(2)}) collective-permute-start(f32[288,128]{1,0:T(8,128)S(1)} %collective-permute-done.3.refs_2_), channel_id=1, source_target_pairs={{0,1},{1,0},{2,3},{3,2},{4,5},{5,4},{6,7},{7,6},{8,9},{9,8},{10,11... | collective-permute-start | bytes 442376 | tf_op jit(solution)/shard_map/ppermute | solution.py:433
  28.9 1.4 %collective-permute-start.6 = (f32[288,128]{1,0:T(8,128)S(1)}, f32[288,128]{1,0:T(8,128)S(1)}, u32[]{:S(2)}, u32[]{:S(2)}) collective-permute-start(f32[288,128]{1,0:T(8,128)S(1)} %collective-permute-done.2.refs_1_), channel_id=1, source_target_pairs={{0,1},{1,0},{2,3},{3,2},{4,5},{5,4},{6,7},{7,6},{8,9},{9,8},{10,11... | collective-permute-start | bytes 442376 | tf_op jit(solution)/shard_map/ppermute | solution.py:433
  30.1 58.5 %copy-start.21 = (f32[24,256]{1,0:T(8,128)}, f32[24,256]{1,0:T(8,128)S(1)}, u32[]{:S(2)}) copy-start(f32[24,256]{1,0:T(8,128)S(1)} %maximum_maximum_fusion.own_basis_ref) | copy-start | bytes 73732
  35.8 21.8 %copy-start.24 = (f32[152,128]{1,0:T(8,128)S(1)}, f32[152,128]{1,0:T(8,128)}, u32[]{:S(2)}) copy-start(f32[152,128]{1,0:T(8,128)} %get-tuple-element.21) | copy-start | bytes 233476
  35.8 21.9 %copy-start.23 = (f32[152,128]{1,0:T(8,128)S(1)}, f32[152,128]{1,0:T(8,128)}, u32[]{:S(2)}) copy-start(f32[152,128]{1,0:T(8,128)} %get-tuple-element.22) | copy-start | bytes 233476
  35.8 33.8 %all-to-all-start = ((f32[32,16,128]{2,1,0:T(8,128)}), f32[32,16,128]{2,1,0:T(8,128)S(1)}, u32[]{:S(2)}, u32[]{:S(2)}) async-start(f32[32,16,128]{2,1,0:T(8,128)} %get-tuple-element.25), calls=%async_computation | async-start | bytes 524288 | tf_op jit(solution)/shard_map/all_to_all | solution.py:451
  43.2 10.1 %collective-permute-start.10 = (f32[152,128]{1,0:T(8,128)}, f32[152,128]{1,0:T(8,128)S(1)}, u32[]{:S(2)}, u32[]{:S(2)}) collective-permute-start(f32[152,128]{1,0:T(8,128)} %get-tuple-element.21), channel_id=1, source_target_pairs={{8,0},{16,8},{24,16},{32,24},{40,32},{48,40},{56,48},{64,56},{72,6... | collective-permute-start | bytes 233480 | tf_op jit(solution)/shard_map/ppermute | solution.py:427
  48.7 8.6 %collective-permute-start.9 = (f32[152,128]{1,0:T(8,128)}, f32[152,128]{1,0:T(8,128)S(1)}, u32[]{:S(2)}, u32[]{:S(2)}) collective-permute-start(f32[152,128]{1,0:T(8,128)} %get-tuple-element.22), channel_id=1, source_target_pairs={{0,8},{8,16},{16,24},{24,32},{32,40},{40,48},{48,56},{56,64},{64,7... | collective-permute-start | bytes 233480 | tf_op jit(solution)/shard_map/ppermute | solution.py:427
  53.3 35.3 %copy-start.6 = (f32[24,256]{1,0:T(8,128)}, f32[24,256]{1,0:T(8,128)S(1)}, u32[]{:S(2)}) copy-start(f32[24,256]{1,0:T(8,128)S(1)} %fusion.32.flex_modes_ref) | copy-start | bytes 73732
  58.0 7.6 %collective-permute-start.13 = (f32[392,128]{1,0:T(8,128)S(1)}, f32[392,128]{1,0:T(8,128)S(1)}, u32[]{:S(2)}, u32[]{:S(2)}) collective-permute-start(f32[392,128]{1,0:T(8,128)S(1)} %constant_dynamic-update-slice_fusion.5.refs_0_), channel_id=1, source_target_pairs={{0,6},{2,0},{4,2},{6,4},{1,7},{3,1},{5,3},{7,5},{8,14},{10,8},{12,... | collective-permute-start | bytes 602120 | tf_op jit(solution)/shard_map/ppermute | solution.py:446
  58.7 8.8 %collective-permute-start.12 = (f32[392,128]{1,0:T(8,128)S(1)}, f32[392,128]{1,0:T(8,128)S(1)}, u32[]{:S(2)}, u32[]{:S(2)}) collective-permute-start(f32[392,128]{1,0:T(8,128)S(1)} %constant_dynamic-update-slice_fusion.5.refs_0_), channel_id=1, source_target_pairs={{0,4},{2,6},{4,0},{6,2},{1,5},{3,7},{5,1},{7,3},{8,12},{10,14},{12... | collective-permute-start | bytes 602120 | tf_op jit(solution)/shard_map/ppermute | solution.py:446
  59.4 10.2 %collective-permute-start.11 = (f32[392,128]{1,0:T(8,128)S(1)}, f32[392,128]{1,0:T(8,128)S(1)}, u32[]{:S(2)}, u32[]{:S(2)}) collective-permute-start(f32[392,128]{1,0:T(8,128)S(1)} %constant_dynamic-update-slice_fusion.5.refs_0_), channel_id=1, source_target_pairs={{0,2},{2,4},{4,6},{6,0},{1,3},{3,5},{5,7},{7,1},{8,10},{10,12},{12... | collective-permute-start | bytes 602120 | tf_op jit(solution)/shard_map/ppermute | solution.py:446
  60.3 15.5 %collective-permute-start.14 = (f32[392,128]{1,0:T(8,128)S(1)}, f32[392,128]{1,0:T(8,128)S(1)}, u32[]{:S(2)}, u32[]{:S(2)}) collective-permute-start(f32[392,128]{1,0:T(8,128)S(1)} %constant_dynamic-update-slice_fusion.5.refs_0_), channel_id=1, source_target_pairs={{0,1},{1,0},{2,3},{3,2},{4,5},{5,4},{6,7},{7,6},{8,9},{9,8},{10,11... | collective-permute-start | bytes 602120 | tf_op jit(solution)/shard_map/ppermute | solution.py:433
  65.6 10.2 %collective-permute-start.17 = (f32[392,128]{1,0:T(8,128)S(1)}, f32[392,128]{1,0:T(8,128)S(1)}, u32[]{:S(2)}, u32[]{:S(2)}) collective-permute-start(f32[392,128]{1,0:T(8,128)S(1)} %collective-permute-done.13.refs_3_), channel_id=1, source_target_pairs={{0,1},{1,0},{2,3},{3,2},{4,5},{5,4},{6,7},{7,6},{8,9},{9,8},{10,11... | collective-permute-start | bytes 602120 | tf_op jit(solution)/shard_map/ppermute | solution.py:433
  67.5 8.3 %collective-permute-start.16 = (f32[392,128]{1,0:T(8,128)S(1)}, f32[392,128]{1,0:T(8,128)S(1)}, u32[]{:S(2)}, u32[]{:S(2)}) collective-permute-start(f32[392,128]{1,0:T(8,128)S(1)} %collective-permute-done.12.refs_2_), channel_id=1, source_target_pairs={{0,1},{1,0},{2,3},{3,2},{4,5},{5,4},{6,7},{7,6},{8,9},{9,8},{10,11... | collective-permute-start | bytes 602120 | tf_op jit(solution)/shard_map/ppermute | solution.py:433
  69.6 6.2 %collective-permute-start.15 = (f32[392,128]{1,0:T(8,128)S(1)}, f32[392,128]{1,0:T(8,128)S(1)}, u32[]{:S(2)}, u32[]{:S(2)}) collective-permute-start(f32[392,128]{1,0:T(8,128)S(1)} %collective-permute-done.11.refs_1_), channel_id=1, source_target_pairs={{0,1},{1,0},{2,3},{3,2},{4,5},{5,4},{6,7},{7,6},{8,9},{9,8},{10,11... | collective-permute-start | bytes 602120 | tf_op jit(solution)/shard_map/ppermute | solution.py:433
  79.6 17.4 %all-to-all-start.1 = ((f32[32,16,128]{2,1,0:T(8,128)}), f32[32,16,128]{2,1,0:T(8,128)S(1)}, u32[]{:S(2)}, u32[]{:S(2)}) async-start(f32[32,16,128]{2,1,0:T(8,128)} %get-tuple-element.27), calls=%async_computation.1 | async-start | bytes 524288 | tf_op jit(solution)/shard_map/all_to_all | solution.py:451
  101.4 26.6 %all-to-all-start.2 = ((f32[256,2,128]{2,1,0:T(2,128)}), f32[256,2,128]{2,1,0:T(2,128)S(1)}, u32[]{:S(2)}, u32[]{:S(2)}) async-start(f32[256,2,128]{2,1,0:T(2,128)} %broadcast_in_dim.7), calls=%async_computation.2 | async-start | bytes 524288 | tf_op jit(solution)/shard_map/all_to_all | solution.py:438
  112.0 20.1 %collective-permute-start.18 = (f32[128,128]{1,0:T(8,128)}, f32[128,128]{1,0:T(8,128)S(1)}, u32[]{:S(2)}, u32[]{:S(2)}) collective-permute-start(f32[128,128]{1,0:T(8,128)} %get-tuple-element.38), channel_id=1, source_target_pairs={{8,0},{16,8},{24,16},{32,24},{40,32},{48,40},{56,48},{64,56},{72,6... | collective-permute-start | bytes 196616 | tf_op jit(solution)/shard_map/ppermute | solution.py:427
  121.5 1.4 %collective-permute-start.19 = (f32[24,128]{1,0:T(8,128)}, f32[24,128]{1,0:T(8,128)S(1)}, u32[]{:S(2)}, u32[]{:S(2)}) collective-permute-start(f32[24,128]{1,0:T(8,128)} %last_weights.1), channel_id=1, source_target_pairs={{0,1},{1,0},{2,3},{3,2},{4,5},{5,4},{6,7},{7,6},{8,9},{9,8},{10,11... | collective-permute-start | bytes 36872 | tf_op jit(solution)/shard_map/ppermute | solution.py:433
  123.6 5.3 %collective-permute-start.22 = (f32[24,128]{1,0:T(8,128)S(1)}, f32[24,128]{1,0:T(8,128)S(1)}, u32[]{:S(2)}, u32[]{:S(2)}) collective-permute-start(f32[24,128]{1,0:T(8,128)S(1)} %add.19.refs_0_), channel_id=1, source_target_pairs={{0,6},{2,0},{4,2},{6,4},{1,7},{3,1},{5,3},{7,5},{8,14},{10,8},{12,... | collective-permute-start | bytes 36872 | tf_op jit(solution)/shard_map/ppermute | solution.py:446
  126.3 5.2 %collective-permute-start.21 = (f32[24,128]{1,0:T(8,128)S(1)}, f32[24,128]{1,0:T(8,128)S(1)}, u32[]{:S(2)}, u32[]{:S(2)}) collective-permute-start(f32[24,128]{1,0:T(8,128)S(1)} %add.19.refs_0_), channel_id=1, source_target_pairs={{0,4},{2,6},{4,0},{6,2},{1,5},{3,7},{5,1},{7,3},{8,12},{10,14},{12... | collective-permute-start | bytes 36872 | tf_op jit(solution)/shard_map/ppermute | solution.py:446
  127.1 4.9 %collective-permute-start.20 = (f32[24,128]{1,0:T(8,128)S(1)}, f32[24,128]{1,0:T(8,128)S(1)}, u32[]{:S(2)}, u32[]{:S(2)}) collective-permute-start(f32[24,128]{1,0:T(8,128)S(1)} %add.19.refs_0_), channel_id=1, source_target_pairs={{0,2},{2,4},{4,6},{6,0},{1,3},{3,5},{5,7},{7,1},{8,10},{10,12},{12... | collective-permute-start | bytes 36872 | tf_op jit(solution)/shard_map/ppermute | solution.py:446
  (24 other events, 103.1 us)

commit v6 on v5

--- a/solution.py
+++ b/solution.py
@@ -224,62 +224,60 @@
     )(*pieces, place, rest, stiff)
 
 
-def search_kernel(rows, count, share, *refs):
-    pieces, refs = refs[: 2 * count], refs[2 * count :]
-    place_ref, basis_ref, weights_ref, traces_ref, modes_ref, sent_ref = refs
-    face = 2 * count * rows
+def search_kernel(share, *refs):
+    pieces, (place_ref, weights_ref, sent_ref) = refs[:-3], refs[-3:]
     wide = NEAR * PAD
-    head = 2 * rows
-    sums = pieces[0][head : head + 7 * PAD, :]
+    sums = pieces[0][...]
     for ref in pieces[1:]:
-        sums = sums + ref[head : head + 7 * PAD, :]
-
-    def copy(ref, at):
-        for side in range(2):
-            at_rows = pl.ds(pl.multiple_of(side * face + at * rows, rows), rows)
-            traces_ref[at_rows, :] = ref[side * rows : (side + 1) * rows, :]
-            low = head + 7 * PAD + side * wide
-            modes_ref[:, at_rows] = ref[low : low + wide, :]
-
-    each_piece(pieces, place_ref, copy)
+        sums = sums + ref[...]
     weights = jnp.concatenate([weights_ref[...], jnp.zeros((128 - wide, 128), jnp.float32)], 0)
-    change = dot(sums[3 * PAD :], weights)
-    rhs = dot(basis_ref[PAD : 2 * PAD, :], traces_ref[...]) - change[3 * PAD :]
-    flex_search = sums[: 3 * PAD] - change[: 3 * PAD]
+    rows = sums[: 4 * PAD] - dot(sums[4 * PAD :], weights)
     lane = lax.broadcasted_iota(jnp.int32, (PAD, 128), 1)
     mine = (place_ref[0] * 2 + place_ref[1]) * share
     tail = jnp.zeros((PAD, 128), jnp.float32)
     for b in range(3):
-        block = flex_search[b * PAD : (b + 1) * PAD]
+        block = rows[b * PAD : (b + 1) * PAD]
         block = pltpu.roll(block, lax.rem(128 - mine + b * share, 128), 1)
         tail = jnp.where(lane // share == b, block, tail)
     for b in range(3):
         low = 3 * share + b * 3 * PAD
-        block = pltpu.roll(sums[(3 + b) * PAD : (4 + b) * PAD], (low - wide) % 128, 1)
+        block = pltpu.roll(sums[(4 + b) * PAD : (5 + b) * PAD], (low - wide) % 128, 1)
         tail = jnp.where((lane >= low) & (lane < low + 3 * PAD), block, tail)
-    sent = jnp.concatenate([rhs, tail], 0)
+    sent = jnp.concatenate([rows[3 * PAD :], tail], 0)
     for t in range(sent_ref.shape[0]):
         sent_ref[t] = sent
 
 
-def order_search(pieces, place, basis, weights, subs, rows):
-    face = len(pieces) * rows
-    return pl.pallas_call(
-        lambda *refs: search_kernel(rows, len(pieces) // 2, 128 // len(pieces), *refs),
-        out_shape=shapes((2 * face, 128), (NEAR * PAD, 2 * face), (subs, 2 * PAD, 128)),
-        in_specs=[VMEM] * len(pieces) + [SMEM, VMEM, VMEM],
-        out_specs=[VMEM] * 3,
-        name="order_search",
-    )(*pieces, place, basis, weights)
-
-
-def flex_kernel(flex_ref, traces_ref, modes_ref, weights_ref, own_ref, own_modes_ref, field_ref, own_basis_ref,
-                flex_modes_ref, image_ref, search_ref, res_ref, turned_ref, ext_ref):
-    rows = field_ref.shape[0]
+def search_rows(pieces, place, weights, subs):
+    return pl.pallas_call(
+        lambda *refs: search_kernel(128 // len(pieces), *refs),
+        grid=(1,),
+        out_shape=shapes((subs, 2 * PAD, 128))[0],
+        in_specs=[pl.BlockSpec((8 * PAD, 128), lambda i: (0, 0))] * len(pieces)
+        + [SMEM, pl.BlockSpec(weights.shape, lambda i: (0, 0))],
+        out_specs=pl.BlockSpec((subs, 2 * PAD, 128), lambda i: (0, 0, 0)),
+        name="search_rows",
+    )(*pieces, place, weights)
+
+
+def flex_kernel(rows, count, *refs):
+    pieces, refs = refs[: 2 * count], refs[2 * count :]
+    place_ref, flex_ref, weights_ref, own_ref, own_modes_ref, field_ref, own_basis_ref, flex_modes_ref = refs[:8]
+    image_ref, search_ref, res_ref, turned_ref, ext_ref = refs[8:]
+    face = 2 * count * rows
     wide = NEAR * PAD
+    head = 8 * PAD
     weights = jnp.concatenate([weights_ref[...], jnp.zeros((128 - wide, 128), jnp.float32)], 0)
-    ext_ref[:, :128] = traces_ref[...]
-    turned_into(ext_ref, modes_ref, traces_ref.shape[0] // 128)
+    filler = jnp.zeros((128 - wide, rows), jnp.float32)
+
+    def copy(ref, at):
+        for side in range(2):
+            at_rows = pl.ds(pl.multiple_of(side * face + at * rows, rows), rows)
+            ext_ref[at_rows, :128] = ref[head + side * rows : head + (side + 1) * rows, :]
+            low = head + 2 * rows + side * wide
+            ext_ref[at_rows, 128:] = jnp.concatenate([ref[low : low + wide, :], filler], 0).T
+
+    each_piece(pieces, place_ref, copy)
     both = dot3(flex_ref[...], ext_ref[...])
     image_ref[...] = both[:, :128] - dot(both[:, 128:], weights)
     own_modes = jnp.concatenate(
@@ -300,16 +298,26 @@
     res_ref[...] = field_ref[...] - dot(turned[rows:], shifted)
 
 
-def apply_flexibility(flex, traces, modes, weights, own, own_modes, field, own_basis, flex_modes):
+def apply_flexibility(pieces, place, flex, weights, own, own_modes, field, own_basis, flex_modes):
     rows = field.shape[0]
     return pl.pallas_call(
-        flex_kernel,
+        lambda *refs: flex_kernel(rows, len(pieces) // 2, *refs),
         out_shape=shapes((2 * rows, 128), (2 * rows, 128), (rows, 128), (2 * rows, 128)),
-        in_specs=[VMEM] * 9,
+        in_specs=[VMEM] * len(pieces) + [SMEM] + [VMEM] * 7,
         out_specs=[VMEM] * 4,
-        scratch_shapes=[pltpu.VMEM((traces.shape[0], 256), jnp.float32)],
+        scratch_shapes=[pltpu.VMEM((2 * len(pieces) * rows, 256), jnp.float32)],
         name="apply_flexibility",
-    )(flex, traces, modes, weights, own, own_modes, field, own_basis, flex_modes)
+    )(*pieces, place, flex, weights, own, own_modes, field, own_basis, flex_modes)
+
+
+def chosen(a, choice):
+    total = None
+    for _ in range(3):
+        part = a.astype(jnp.bfloat16)
+        a = a - part.astype(jnp.float32)
+        term = jnp.dot(part, choice, preferred_element_type=jnp.float32)
+        total = term if total is None else total + term
+    return total
 
 
 def last_kernel(subs, modes, share, place_ref, second_ref, inverse_ref, near_ref, out_ref):
@@ -327,22 +335,42 @@
     def later(x):
         return jnp.where(row == subs - 1, 0.0, pltpu.roll(x, subs - 1, 0))
 
-    near = []
+    here = jnp.zeros((subs, 128), jnp.float32)
     for k in range(modes):
-        here = weights[k * subs : (k + 1) * subs]
-        near.append((earlier(here), here, later(here)))
+        block = weights[k * subs : (k + 1) * subs]
+        here = jnp.where(lane // share == k, pltpu.roll(block, k * share, 1), here)
+    near = (earlier(here), here, later(here))
+    tails = jnp.concatenate(
+        [second_ref[pl.ds(PAD + i, subs, stride=2 * PAD), :] for i in range(PAD)], axis=0
+    )
+    source = lax.broadcasted_iota(jnp.int32, (128, 9 * 128), 0)
+    target = lax.broadcasted_iota(jnp.int32, (128, 9 * 128), 1)
+    wanted = 3 * share + (target // 128) * PAD + (target % 128) // share
+    factors = chosen(tails, (source == wanted).astype(jnp.float32).astype(jnp.bfloat16))
+    products = []
+    for b in range(3):
+        strips = []
+        for i in range(PAD):
+            strip = jnp.zeros((subs, 128), jnp.float32)
+            for c in range(3):
+                at = (b * 3 + c) * 128
+                strip = strip + factors[i * subs : (i + 1) * subs, at : at + 128] * near[c]
+            strips.append(strip)
+        products.append(jnp.concatenate(strips, 0))
+    source = lax.broadcasted_iota(jnp.int32, (128, 128), 0)
+    target = lax.broadcasted_iota(jnp.int32, (128, 128), 1)
+    added = chosen(
+        jnp.concatenate(products, 0),
+        ((source % share == target) & (source < modes * share)).astype(jnp.float32).astype(jnp.bfloat16),
+    )
     out = []
     for i in range(PAD):
-        tail = second_ref[pl.ds(PAD + i, subs, stride=2 * PAD), :]
         parts = []
         for b in range(3):
-            part = tail if b == 0 else pltpu.roll(tail, 128 - b * share, 1)
-            if i < modes:
-                for c in range(3):
-                    for k in range(modes):
-                        at = 3 * share + b * 3 * PAD + c * PAD + k
-                        part = part - tail[:, at : at + 1] * near[k][c]
-            parts.append(part)
+            tail = tails[i * subs : (i + 1) * subs]
+            tail = tail if b == 0 else pltpu.roll(tail, 128 - b * share, 1)
+            start = (b * PAD + i) * subs
+            parts.append(tail - added[start : start + subs])
         total = parts[1] + later(parts[0]) + earlier(parts[2])
         out.append(jnp.where(lane < share, total, 0.0))
     last = dot(near_ref[PAD : 4 * PAD, :], jnp.concatenate(out, 0))
@@ -383,14 +411,14 @@
     direction_ref[...] = direction[rows:]
     first = jnp.sum(res_ref[...] * search_ref[rows:, :], axis=0, keepdims=True)
     second = jnp.sum(direction * image, axis=0, keepdims=True)
-    sums_ref[...] = jnp.concatenate([first, second], 0)
-
-
-def project_direction(second, near, turned, image, search, res, subs):
+    sums_ref[...] = jnp.broadcast_to(jnp.concatenate([first, second], 0)[None], sums_ref.shape)
+
+
+def project_direction(second, near, turned, image, search, res, subs, devices):
     rows = res.shape[0]
     return pl.pallas_call(
         lambda *refs: direction_kernel(subs, *refs),
-        out_shape=shapes((rows, 128), (rows, 128), (rows, 128), (2, 128)),
+        out_shape=shapes((rows, 128), (rows, 128), (rows, 128), (devices, 2, 128)),
         in_specs=[VMEM] * 6,
         out_specs=[VMEM] * 4,
         name="project_direction",
@@ -433,13 +461,6 @@
     return lax.ppermute(block, "c", [(0, 1), (1, 0)])
 
 
-def from_all(value, axis):
-    count = lax.axis_size(axis)
-    return lax.all_to_all(
-        jnp.broadcast_to(value[None], (count, *value.shape)), axis, 0, 0, tiled=True
-    )
-
-
 def along_x(piece):
     n = lax.axis_size("x")
     return [piece] + [
@@ -505,36 +526,35 @@
     own_modes = jnp.concatenate([modes_top * inner, modes_bottom * live], 1)
 
     flex_modes = dot_nt(basis, flex)
-    small = dot_nt(flex_modes, jnp.concatenate([own_modes, own_basis], 0))
-    cross = dot_nt(own_basis[PAD : 2 * PAD], own_modes)
-    small = jnp.pad(small, ((0, 0), (0, 128 - small.shape[1])))
-    cross = jnp.pad(cross, ((0, 0), (0, 128 - cross.shape[1])))
+    tests = jnp.concatenate([flex_modes, own_basis[PAD : 2 * PAD]], 0)
+    small = dot_nt(tests, jnp.concatenate([own_modes, own_basis], 0))
     piece = jnp.concatenate(
         [
-            own_traces, dot(flex_modes, own_traces), small, cross, own_modes[:, :rows],
-            own_modes[:, rows:],
+            dot(tests, own_traces), jnp.pad(small, ((0, 0), (0, 128 - small.shape[1]))), own_traces,
+            own_modes[:, :rows], own_modes[:, rows:],
         ],
         0,
     )
     pieces = gathered(piece)
     inverse, near, weights = coarse_inverse(sub.astype(jnp.int32)[None], first, subs, mode_count)
-    search_traces, modes_traces, sent = order_search(pieces, place, basis, weights, subs, rows)
+    sent = search_rows(pieces, place, weights, subs)
     second = to_all(sent, SUB)
 
     image, own_search, own_res, turned = apply_flexibility(
-        flex, search_traces, modes_traces, weights, own_traces, own_modes, field, own_basis, flex_modes
+        pieces, place, flex, weights, own_traces, own_modes, field, own_basis, flex_modes
     )
     second = second.reshape(subs * 2 * PAD, 128)
     low, high, direction, sums = project_direction(
-        second, near, turned, image, own_search, own_res, subs
-    )
-    totals = from_all(sums, ALL)
+        second, near, turned, image, own_search, own_res, subs, lax.axis_size(ALL)
+    )
+    totals = to_all(sums, ALL)
     totals = totals.sum(0)
 
     after = moved_along(low, -1)
     share = loads // lanes
     weights = last_weights(place, second, inverse, near, subs, mode_count, share)
-    weights = weights + core_swap(weights)
+    swapped = core_swap(weights)
+    weights = weights + swapped
     return results(totals, direction, own_res, high, after, turned, live, along_x(weights))
 
 

time: 135 us -> 132 us (0.978)
  the two profiles are of different devices: /device:TPU:160 before, /device:TPU:1 now
where the time goes in v6:
time: 132 us; the launch traced here: 130 us
  starting transfers between devices  72.1 us (55%)
  Pallas kernels  24.8 us (19%)
  waiting for transfers between devices  18.1 us (14%)
  other arithmetic  5.4 us (4%)
  local copies, waits for them, and re-layouts  5.04 us (4%)
  matrix products  3.05 us (2%)
  between operations  1.89 us (1%)
    all_to_all x3, starting transfers between devices, to_all(): return lax.all_to_all(values, axis, 0, 0, tiled=True)  33.5 us
    ppermute x9, starting transfers between devices, core_swap(): return lax.ppermute(block, 'c', [(0, 1), (1, 0)])  18.9 us
    ppermute x5, starting transfers between devices, moved_along(): lax.ppermute(block, SUB, [(i - distance, i) for i in range(n) if 0 <= i -...  12.5 us
    all_to_all x3, waiting for transfers between devices, to_all(): return lax.all_to_all(values, axis, 0, 0, tiled=True)  10.4 us
    ppermute x9, starting transfers between devices, along_x(): lax.ppermute(piece, 'x', [(i, (i + d) % n) for i in range(n)])  7.24 us
    pallas_call x1, Pallas kernels, coarse_inverse(): pl.pallas_call(lambda *refs: inverse_kernel(subs, modes, *refs), out_shap...  5.39 us
    ppermute x9, waiting for transfers between devices, along_x(): lax.ppermute(piece, 'x', [(i, (i + d) % n) for i in range(n)])  5.32 us
    pallas_call x1, Pallas kernels, apply_flexibility(): pl.pallas_call(lambda *refs: flex_kernel(rows, len(pieces) // 2, *refs),...  5.13 us
  transfers between devices with their start and end apart: 26, of which 7 were waited for; matrix products, arithmetic and copies ran while one was open for 7% of the time, Pallas kernels for 11%

profile of v6, /device:TPU:1, one launch (start us, length us, event | category | flops | bytes accessed | tf_op | source)
XLA Modules:
  0.0 130.4 jit_solution(8426515971297825650)
XLA Ops:
  2.1 1.3 collective-permute-start.1
  4.2 4.7 %collective-permute-start = (f32[136,128]{1,0:T(8,128)S(1)}, f32[136,128]{1,0:T(8,128)S(1)}, u32[]{:S(2)}, u32[]{:S(2)}) collective-permute-start(f32[136,128]{1,0:T(8,128)S(1)} %pad_maximum_fusion.1), channel_id=1, source_target_pairs={{0,8},{8,16},{16,24},{24,32},{32,40},{40,48},{48,56},{56,64},{64,7... | collective-permute-start | bytes 208904 | tf_op jit(solution)/shard_map/ppermute | solution.py:455
  8.9 1.3 %collective-permute-done = f32[136,128]{1,0:T(8,128)S(1)} collective-permute-done((f32[136,128]{1,0:T(8,128)S(1)}, f32[136,128]{1,0:T(8,128)S(1)}, u32[]{:S(2)}, u32[]{:S(2)}) %collective-permute-start) | collective-permute-done | bytes 69664 | tf_op jit(solution)/shard_map/ppermute | solution.py:455
  11.1 2.7 %collective-permute-start.4 = (f32[288,128]{1,0:T(8,128)S(1)}, f32[288,128]{1,0:T(8,128)S(1)}, u32[]{:S(2)}, u32[]{:S(2)}) collective-permute-start(f32[288,128]{1,0:T(8,128)S(1)} %get-tuple-element.44.refs_0_), channel_id=1, source_target_pairs={{0,6},{2,0},{4,2},{6,4},{1,7},{3,1},{5,3},{7,5},{8,14},{10,8},{12,... | collective-permute-start | bytes 442376 | tf_op jit(solution)/shard_map/ppermute | solution.py:467
  15.1 2.6 %collective-permute-start.5 = (f32[288,128]{1,0:T(8,128)S(1)}, f32[288,128]{1,0:T(8,128)S(1)}, u32[]{:S(2)}, u32[]{:S(2)}) collective-permute-start(f32[288,128]{1,0:T(8,128)S(1)} %get-tuple-element.44.refs_0_), channel_id=1, source_target_pairs={{0,1},{1,0},{2,3},{3,2},{4,5},{5,4},{6,7},{7,6},{8,9},{9,8},{10,11... | collective-permute-start | bytes 442376 | tf_op jit(solution)/shard_map/ppermute | solution.py:461
  18.0 3.1 %collective-permute-start.8 = (f32[288,128]{1,0:T(8,128)S(1)}, f32[288,128]{1,0:T(8,128)S(1)}, u32[]{:S(2)}, u32[]{:S(2)}) collective-permute-start(f32[288,128]{1,0:T(8,128)S(1)} %collective-permute-done.4.refs_3_), channel_id=1, source_target_pairs={{0,1},{1,0},{2,3},{3,2},{4,5},{5,4},{6,7},{7,6},{8,9},{9,8},{10,11... | collective-permute-start | bytes 442376 | tf_op jit(solution)/shard_map/ppermute | solution.py:461
  21.1 2.1 %collective-permute-start.7 = (f32[288,128]{1,0:T(8,128)S(1)}, f32[288,128]{1,0:T(8,128)S(1)}, u32[]{:S(2)}, u32[]{:S(2)}) collective-permute-start(f32[288,128]{1,0:T(8,128)S(1)} %collective-permute-done.3.refs_2_), channel_id=1, source_target_pairs={{0,1},{1,0},{2,3},{3,2},{4,5},{5,4},{6,7},{7,6},{8,9},{9,8},{10,11... | collective-permute-start | bytes 442376 | tf_op jit(solution)/shard_map/ppermute | solution.py:461
  23.2 1.6 %collective-permute-start.6 = (f32[288,128]{1,0:T(8,128)S(1)}, f32[288,128]{1,0:T(8,128)S(1)}, u32[]{:S(2)}, u32[]{:S(2)}) collective-permute-start(f32[288,128]{1,0:T(8,128)S(1)} %collective-permute-done.2.refs_1_), channel_id=1, source_target_pairs={{0,1},{1,0},{2,3},{3,2},{4,5},{5,4},{6,7},{7,6},{8,9},{9,8},{10,11... | collective-permute-start | bytes 442376 | tf_op jit(solution)/shard_map/ppermute | solution.py:461
  26.9 4.9 %apply_stiffness.1 = (f32[152,128]{1,0:T(8,128)}, f32[152,128]{1,0:T(8,128)}, f32[24,256]{1,0:T(8,128)}, f32[24,2048]{1,0:T(8,128)}, f32[32,16,128]{2,1,0:T(8,128)}) custom-call(f32[288,128]{1,0:T(8,128)} %copy-done.12, f32[288,128]{1,0:T(8,128)} %copy-done.16, f32[288,128]{1,0:T(8,128)} %copy-done.15, f32[288,128]{1,0:T(8,128)} %copy-done.14, ...), custom_call_target="tpu_custom_call" | custom-call | tf_op jit(solution)/shard_map/apply_stiffness/pallas_call | solution.py:214
  31.8 14.6 %all-to-all-start = ((f32[32,16,128]{2,1,0:T(8,128)}), f32[32,16,128]{2,1,0:T(8,128)S(1)}, u32[]{:S(2)}, u32[]{:S(2)}) async-start(f32[32,16,128]{2,1,0:T(8,128)} %get-tuple-element.22), calls=%async_computation | async-start | bytes 524288 | tf_op jit(solution)/shard_map/all_to_all | solution.py:472
  46.5 1.3 collective-permute-start.10
  47.8 4.0 %collective-permute-start.9 = (f32[152,128]{1,0:T(8,128)}, f32[152,128]{1,0:T(8,128)S(1)}, u32[]{:S(2)}, u32[]{:S(2)}) collective-permute-start(f32[152,128]{1,0:T(8,128)} %get-tuple-element.20), channel_id=1, source_target_pairs={{0,8},{8,16},{16,24},{24,32},{32,40},{40,48},{48,56},{56,64},{64,7... | collective-permute-start | bytes 233480 | tf_op jit(solution)/shard_map/ppermute | solution.py:455
  51.8 2.7 %fusion.28.refs_15_ = f32[24,256]{1,0:T(8,128)S(1)} fusion(f32[24,2048]{1,0:T(8,128)} %get-tuple-element.18, f32[256,2048]{1,0:T(8,128)S(1)} %bitcast.26), kind=kOutput, calls=%fused_computation.62 | convolution fusion | flops 150994944 | bytes 2318336 | tf_op jit(solution)/shard_map/dot_general | solution.py:23
  56.6 1.6 %collective-permute-start.14 = (f32[400,128]{1,0:T(8,128)S(1)}, f32[400,128]{1,0:T(8,128)S(1)}, u32[]{:S(2)}, u32[]{:S(2)}) collective-permute-start(f32[400,128]{1,0:T(8,128)S(1)} %constant_dynamic-update-slice_fusion.5.refs_0_), channel_id=1, source_target_pairs={{0,1},{1,0},{2,3},{3,2},{4,5},{5,4},{6,7},{7,6},{8,9},{9,8},{10,11... | collective-permute-start | bytes 614408 | tf_op jit(solution)/shard_map/ppermute | solution.py:461
  58.2 2.7 %collective-permute-done.13.refs_3_ = f32[400,128]{1,0:T(8,128)S(1)} collective-permute-done((f32[400,128]{1,0:T(8,128)S(1)}, f32[400,128]{1,0:T(8,128)S(1)}, u32[]{:S(2)}, u32[]{:S(2)}) %collective-permute-start.13) | collective-permute-done | bytes 204832 | tf_op jit(solution)/shard_map/ppermute | solution.py:467
  60.9 3.0 %collective-permute-start.17 = (f32[400,128]{1,0:T(8,128)S(1)}, f32[400,128]{1,0:T(8,128)S(1)}, u32[]{:S(2)}, u32[]{:S(2)}) collective-permute-start(f32[400,128]{1,0:T(8,128)S(1)} %collective-permute-done.13.refs_3_), channel_id=1, source_target_pairs={{0,1},{1,0},{2,3},{3,2},{4,5},{5,4},{6,7},{7,6},{8,9},{9,8},{10,11... | collective-permute-start | bytes 614408 | tf_op jit(solution)/shard_map/ppermute | solution.py:461
  63.9 2.2 %collective-permute-start.16 = (f32[400,128]{1,0:T(8,128)S(1)}, f32[400,128]{1,0:T(8,128)S(1)}, u32[]{:S(2)}, u32[]{:S(2)}) collective-permute-start(f32[400,128]{1,0:T(8,128)S(1)} %collective-permute-done.12.refs_2_), channel_id=1, source_target_pairs={{0,1},{1,0},{2,3},{3,2},{4,5},{5,4},{6,7},{7,6},{8,9},{9,8},{10,11... | collective-permute-start | bytes 614408 | tf_op jit(solution)/shard_map/ppermute | solution.py:461
  66.1 2.3 %collective-permute-done.11.refs_1_ = f32[400,128]{1,0:T(8,128)S(1)} collective-permute-done((f32[400,128]{1,0:T(8,128)S(1)}, f32[400,128]{1,0:T(8,128)S(1)}, u32[]{:S(2)}, u32[]{:S(2)}) %collective-permute-start.11) | collective-permute-done | bytes 204832 | tf_op jit(solution)/shard_map/ppermute | solution.py:467
  69.6 5.4 %coarse_inverse.1 = (f32[256,256]{1,0:T(8,128)}, f32[40,256]{1,0:T(8,128)}, f32[40,128]{1,0:T(8,128)}) custom-call(s32[1]{0:T(128)} %bitcast.9.refs_0_, f32[512,128]{1,0:T(8,128)} %bitcast.30), custom_call_target="tpu_custom_call" | custom-call | tf_op jit(solution)/shard_map/coarse_inverse/pallas_call | solution.py:132
  75.9 1.8 %search_rows.1 = f32[32,16,128]{2,1,0:T(8,128)} custom-call(f32[400,128]{1,0:T(8,128)} %copy-done.3, f32[400,128]{1,0:T(8,128)} %copy-done.6, f32[400,128]{1,0:T(8,128)} %copy-done.5, f32[400,128]{1,0:T(8,128)} %copy-done.4, f32[400,128]{1,0:T(8,128)} %copy-done.7, f32[400,128]{1,0:T(8,128)} %copy-done.10, f32[400,128]{1,0:T(8,128)} %copy-done.9, ...), custom_call_target="tpu_custom_call" | custom-call | tf_op jit(solution)/shard_map/search_rows/pallas_call | solution.py:252
  77.7 11.7 %all-to-all-start.1 = ((f32[32,16,128]{2,1,0:T(8,128)}), f32[32,16,128]{2,1,0:T(8,128)S(1)}, u32[]{:S(2)}, u32[]{:S(2)}) async-start(f32[32,16,128]{2,1,0:T(8,128)} %search_rows.1), calls=%async_computation.1 | async-start | bytes 524288 | tf_op jit(solution)/shard_map/all_to_all | solution.py:472
  90.7 5.1 %apply_flexibility.1 = (f32[256,128]{1,0:T(8,128)}, f32[256,128]{1,0:T(8,128)}, f32[128,128]{1,0:T(8,128)}, f32[256,128]{1,0:T(8,128)}) custom-call(f32[400,128]{1,0:T(8,128)} %copy-done.3, f32[400,128]{1,0:T(8,128)} %copy-done.6, f32[400,128]{1,0:T(8,128)} %copy-done.5, f32[400,128]{1,0:T(8,128)} %copy-done.4, f32[400,128]{1,0:T(8,128)} %copy-done.7, ...), custom_call_target="tpu_custom_call" | custom-call | tf_op jit(solution)/shard_map/apply_flexibility/pallas_call | solution.py:303
  95.9 5.5 %all-to-all-done.1 = f32[32,16,128]{2,1,0:T(8,128)S(1)} async-done(((f32[32,16,128]{2,1,0:T(8,128)}), f32[32,16,128]{2,1,0:T(8,128)S(1)}, u32[]{:S(2)}, u32[]{:S(2)}) %all-to-all-start.1) | async-done | bytes 262176 | tf_op jit(solution)/shard_map/all_to_all | solution.py:472
  102.0 2.5 %project_direction.1 = (f32[128,128]{1,0:T(8,128)}, f32[128,128]{1,0:T(8,128)}, f32[128,128]{1,0:T(8,128)}, f32[256,2,128]{2,1,0:T(2,128)}) custom-call(f32[512,128]{1,0:T(8,128)} %bitcast.27, f32[40,256]{1,0:T(8,128)} %get-tuple-element.24.refs_1_.refs_3_, f32[256,128]{1,0:T(8,128)} %get-tuple-element.25.refs_2_.turned_ref, ...), custom_call_target="tpu_custom_call" | custom-call | tf_op jit(solution)/shard_map/project_direction/pallas_call | solution.py:419
  104.5 7.1 %all-to-all-start.2 = ((f32[256,2,128]{2,1,0:T(2,128)}), f32[256,2,128]{2,1,0:T(2,128)S(1)}, u32[]{:S(2)}, u32[]{:S(2)}) async-start(f32[256,2,128]{2,1,0:T(2,128)} %get-tuple-element.29), calls=%async_computation.2 | async-start | bytes 524288 | tf_op jit(solution)/shard_map/all_to_all | solution.py:472
  111.6 1.3 collective-permute-start.18
  112.9 3.3 %last_weights.1 = f32[24,128]{1,0:T(8,128)} custom-call(s32[2]{0:T(128)} %pad_add_fusion.refs_8_.refs_0_, f32[512,128]{1,0:T(8,128)} %bitcast.28, f32[256,256]{1,0:T(8,128)} %get-tuple-element.33.refs_2_, f32[40,256]{1,0:T(8,128)} %get-tuple-element.24.refs_1_.refs_3_), custom_call_target="tpu_custom_call" | custom-call | tf_op jit(solution)/shard_map/last_weights/pallas_call | solution.py:381
  116.2 2.3 %collective-permute-start.19 = (f32[24,128]{1,0:T(8,128)}, f32[24,128]{1,0:T(8,128)S(1)}, u32[]{:S(2)}, u32[]{:S(2)}) collective-permute-start(f32[24,128]{1,0:T(8,128)} %last_weights.1), channel_id=1, source_target_pairs={{0,1},{1,0},{2,3},{3,2},{4,5},{5,4},{6,7},{7,6},{8,9},{9,8},{10,11... | collective-permute-start | bytes 36872 | tf_op jit(solution)/shard_map/ppermute | solution.py:461
  118.5 1.0 collective-permute-done.19
  122.1 4.9 %all-to-all-done.2 = f32[256,2,128]{2,1,0:T(2,128)S(1)} async-done(((f32[256,2,128]{2,1,0:T(2,128)}), f32[256,2,128]{2,1,0:T(2,128)S(1)}, u32[]{:S(2)}, u32[]{:S(2)}) %all-to-all-start.2) | async-done | bytes 262176 | tf_op jit(solution)/shard_map/all_to_all | solution.py:472
  127.0 0.9 reduce_sum.9.totals_ref
  128.6 1.8 %results.1 = (f32[1,128,128]{2,1,0:T(8,128)}, f32[1,128,128]{2,1,0:T(8,128)}) custom-call(f32[2,128]{1,0:T(2,128)} %reduce_sum.9.totals_ref, f32[128,128]{1,0:T(8,128)} %get-tuple-element.30.direction_ref, f32[128,128]{1,0:T(8,128)} %get-tuple-element.28.refs_5_.res_ref, f32[128,128]{1,0:T(8,128)} %get-tuple-element.31.high_ref, f32[128,128]{1,0:T(8,128)} %copy-done.22, ...), custom_call_target="tpu_custom_call" | custom-call | tf_op jit(solution)/shard_map/results/pallas_call | solution.py:444
  (124 shorter events, 15.3 us)
Async XLA Ops:
  2.1 9.0 %collective-permute-start.1 = (f32[8,128]{1,0:T(8,128)S(1)}, f32[8,128]{1,0:T(8,128)S(1)}, u32[]{:S(2)}, u32[]{:S(2)}) collective-permute-start(f32[8,128]{1,0:T(8,128)S(1)} %get-tuple-element.41), channel_id=1, source_target_pairs={{8,0},{16,8},{24,16},{32,24},{40,32},{48,40},{56,48},{64,56},{72,6... | collective-permute-start | bytes 12296 | tf_op jit(solution)/shard_map/ppermute | solution.py:455
  4.2 27.6 %copy-start.11 = (f32[128,128]{1,0:T(8,128)}, f32[128,128]{1,0:T(8,128)S(1)}, u32[]{:S(2)}) copy-start(f32[128,128]{1,0:T(8,128)S(1)} %multiply_bitcast_fusion.refs_13_) | copy-start | bytes 196612
  4.2 6.0 %collective-permute-start = (f32[136,128]{1,0:T(8,128)S(1)}, f32[136,128]{1,0:T(8,128)S(1)}, u32[]{:S(2)}, u32[]{:S(2)}) collective-permute-start(f32[136,128]{1,0:T(8,128)S(1)} %pad_maximum_fusion.1), channel_id=1, source_target_pairs={{0,8},{8,16},{16,24},{24,32},{32,40},{40,48},{48,56},{56,64},{64,7... | collective-permute-start | bytes 208904 | tf_op jit(solution)/shard_map/ppermute | solution.py:455
  8.9 42.9 %copy-start = (f32[1,2,128,2048]{3,2,1,0:T(8,128)S(1)}, f32[1,2,128,2048]{3,2,1,0:T(8,128)}, u32[]{:S(2)}) copy-start(f32[1,2,128,2048]{3,2,1,0:T(8,128)} %param.6) | copy-start | bytes 6291460
  11.1 6.9 %collective-permute-start.4 = (f32[288,128]{1,0:T(8,128)S(1)}, f32[288,128]{1,0:T(8,128)S(1)}, u32[]{:S(2)}, u32[]{:S(2)}) collective-permute-start(f32[288,128]{1,0:T(8,128)S(1)} %get-tuple-element.44.refs_0_), channel_id=1, source_target_pairs={{0,6},{2,0},{4,2},{6,4},{1,7},{3,1},{5,3},{7,5},{8,14},{10,8},{12,... | collective-permute-start | bytes 442376 | tf_op jit(solution)/shard_map/ppermute | solution.py:467
  13.9 7.3 %collective-permute-start.3 = (f32[288,128]{1,0:T(8,128)S(1)}, f32[288,128]{1,0:T(8,128)S(1)}, u32[]{:S(2)}, u32[]{:S(2)}) collective-permute-start(f32[288,128]{1,0:T(8,128)S(1)} %get-tuple-element.44.refs_0_), channel_id=1, source_target_pairs={{0,4},{2,6},{4,0},{6,2},{1,5},{3,7},{5,1},{7,3},{8,12},{10,14},{12... | collective-permute-start | bytes 442376 | tf_op jit(solution)/shard_map/ppermute | solution.py:467
  14.4 8.8 %collective-permute-start.2 = (f32[288,128]{1,0:T(8,128)S(1)}, f32[288,128]{1,0:T(8,128)S(1)}, u32[]{:S(2)}, u32[]{:S(2)}) collective-permute-start(f32[288,128]{1,0:T(8,128)S(1)} %get-tuple-element.44.refs_0_), channel_id=1, source_target_pairs={{0,2},{2,4},{4,6},{6,0},{1,3},{3,5},{5,7},{7,1},{8,10},{10,12},{12... | collective-permute-start | bytes 442376 | tf_op jit(solution)/shard_map/ppermute | solution.py:467
  15.1 11.0 %collective-permute-start.5 = (f32[288,128]{1,0:T(8,128)S(1)}, f32[288,128]{1,0:T(8,128)S(1)}, u32[]{:S(2)}, u32[]{:S(2)}) collective-permute-start(f32[288,128]{1,0:T(8,128)S(1)} %get-tuple-element.44.refs_0_), channel_id=1, source_target_pairs={{0,1},{1,0},{2,3},{3,2},{4,5},{5,4},{6,7},{7,6},{8,9},{9,8},{10,11... | collective-permute-start | bytes 442376 | tf_op jit(solution)/shard_map/ppermute | solution.py:461
  18.0 8.1 %collective-permute-start.8 = (f32[288,128]{1,0:T(8,128)S(1)}, f32[288,128]{1,0:T(8,128)S(1)}, u32[]{:S(2)}, u32[]{:S(2)}) collective-permute-start(f32[288,128]{1,0:T(8,128)S(1)} %collective-permute-done.4.refs_3_), channel_id=1, source_target_pairs={{0,1},{1,0},{2,3},{3,2},{4,5},{5,4},{6,7},{7,6},{8,9},{9,8},{10,11... | collective-permute-start | bytes 442376 | tf_op jit(solution)/shard_map/ppermute | solution.py:461
  21.1 5.0 %collective-permute-start.7 = (f32[288,128]{1,0:T(8,128)S(1)}, f32[288,128]{1,0:T(8,128)S(1)}, u32[]{:S(2)}, u32[]{:S(2)}) collective-permute-start(f32[288,128]{1,0:T(8,128)S(1)} %collective-permute-done.3.refs_2_), channel_id=1, source_target_pairs={{0,1},{1,0},{2,3},{3,2},{4,5},{5,4},{6,7},{7,6},{8,9},{9,8},{10,11... | collective-permute-start | bytes 442376 | tf_op jit(solution)/shard_map/ppermute | solution.py:461
  23.2 2.9 %collective-permute-start.6 = (f32[288,128]{1,0:T(8,128)S(1)}, f32[288,128]{1,0:T(8,128)S(1)}, u32[]{:S(2)}, u32[]{:S(2)}) collective-permute-start(f32[288,128]{1,0:T(8,128)S(1)} %collective-permute-done.2.refs_1_), channel_id=1, source_target_pairs={{0,1},{1,0},{2,3},{3,2},{4,5},{5,4},{6,7},{7,6},{8,9},{9,8},{10,11... | collective-permute-start | bytes 442376 | tf_op jit(solution)/shard_map/ppermute | solution.py:461
  26.1 64.7 %copy-start.21 = (f32[24,256]{1,0:T(8,128)}, f32[24,256]{1,0:T(8,128)S(1)}, u32[]{:S(2)}) copy-start(f32[24,256]{1,0:T(8,128)S(1)} %maximum_maximum_fusion.refs_14_) | copy-start | bytes 73732
  31.8 23.0 %copy-start.24 = (f32[152,128]{1,0:T(8,128)S(1)}, f32[152,128]{1,0:T(8,128)}, u32[]{:S(2)}) copy-start(f32[152,128]{1,0:T(8,128)} %get-tuple-element.20) | copy-start | bytes 233476
  31.8 23.0 %copy-start.23 = (f32[152,128]{1,0:T(8,128)S(1)}, f32[152,128]{1,0:T(8,128)}, u32[]{:S(2)}) copy-start(f32[152,128]{1,0:T(8,128)} %get-tuple-element.19) | copy-start | bytes 233476
  31.8 37.1 %all-to-all-start = ((f32[32,16,128]{2,1,0:T(8,128)}), f32[32,16,128]{2,1,0:T(8,128)S(1)}, u32[]{:S(2)}, u32[]{:S(2)}) async-start(f32[32,16,128]{2,1,0:T(8,128)} %get-tuple-element.22), calls=%async_computation | async-start | bytes 524288 | tf_op jit(solution)/shard_map/all_to_all | solution.py:472
  46.5 8.0 %collective-permute-start.10 = (f32[152,128]{1,0:T(8,128)}, f32[152,128]{1,0:T(8,128)S(1)}, u32[]{:S(2)}, u32[]{:S(2)}) collective-permute-start(f32[152,128]{1,0:T(8,128)} %get-tuple-element.19), channel_id=1, source_target_pairs={{8,0},{16,8},{24,16},{32,24},{40,32},{48,40},{56,48},{64,56},{72,6... | collective-permute-start | bytes 233480 | tf_op jit(solution)/shard_map/ppermute | solution.py:455
  47.8 6.7 %collective-permute-start.9 = (f32[152,128]{1,0:T(8,128)}, f32[152,128]{1,0:T(8,128)S(1)}, u32[]{:S(2)}, u32[]{:S(2)}) collective-permute-start(f32[152,128]{1,0:T(8,128)} %get-tuple-element.20), channel_id=1, source_target_pairs={{0,8},{8,16},{16,24},{24,32},{32,40},{40,48},{48,56},{56,64},{64,7... | collective-permute-start | bytes 233480 | tf_op jit(solution)/shard_map/ppermute | solution.py:455
  54.5 35.6 %copy-start.13 = (f32[24,256]{1,0:T(8,128)}, f32[24,256]{1,0:T(8,128)S(1)}, u32[]{:S(2)}) copy-start(f32[24,256]{1,0:T(8,128)S(1)} %fusion.28.refs_15_) | copy-start | bytes 73732
  55.1 5.9 %collective-permute-start.13 = (f32[400,128]{1,0:T(8,128)S(1)}, f32[400,128]{1,0:T(8,128)S(1)}, u32[]{:S(2)}, u32[]{:S(2)}) collective-permute-start(f32[400,128]{1,0:T(8,128)S(1)} %constant_dynamic-update-slice_fusion.5.refs_0_), channel_id=1, source_target_pairs={{0,6},{2,0},{4,2},{6,4},{1,7},{3,1},{5,3},{7,5},{8,14},{10,8},{12,... | collective-permute-start | bytes 614408 | tf_op jit(solution)/shard_map/ppermute | solution.py:467
  55.5 8.5 %collective-permute-start.12 = (f32[400,128]{1,0:T(8,128)S(1)}, f32[400,128]{1,0:T(8,128)S(1)}, u32[]{:S(2)}, u32[]{:S(2)}) collective-permute-start(f32[400,128]{1,0:T(8,128)S(1)} %constant_dynamic-update-slice_fusion.5.refs_0_), channel_id=1, source_target_pairs={{0,4},{2,6},{4,0},{6,2},{1,5},{3,7},{5,1},{7,3},{8,12},{10,14},{12... | collective-permute-start | bytes 614408 | tf_op jit(solution)/shard_map/ppermute | solution.py:467
  56.0 12.4 %collective-permute-start.11 = (f32[400,128]{1,0:T(8,128)S(1)}, f32[400,128]{1,0:T(8,128)S(1)}, u32[]{:S(2)}, u32[]{:S(2)}) collective-permute-start(f32[400,128]{1,0:T(8,128)S(1)} %constant_dynamic-update-slice_fusion.5.refs_0_), channel_id=1, source_target_pairs={{0,2},{2,4},{4,6},{6,0},{1,3},{3,5},{5,7},{7,1},{8,10},{10,12},{12... | collective-permute-start | bytes 614408 | tf_op jit(solution)/shard_map/ppermute | solution.py:467
  56.6 18.3 %collective-permute-start.14 = (f32[400,128]{1,0:T(8,128)S(1)}, f32[400,128]{1,0:T(8,128)S(1)}, u32[]{:S(2)}, u32[]{:S(2)}) collective-permute-start(f32[400,128]{1,0:T(8,128)S(1)} %constant_dynamic-update-slice_fusion.5.refs_0_), channel_id=1, source_target_pairs={{0,1},{1,0},{2,3},{3,2},{4,5},{5,4},{6,7},{7,6},{8,9},{9,8},{10,11... | collective-permute-start | bytes 614408 | tf_op jit(solution)/shard_map/ppermute | solution.py:461
  60.9 14.0 %collective-permute-start.17 = (f32[400,128]{1,0:T(8,128)S(1)}, f32[400,128]{1,0:T(8,128)S(1)}, u32[]{:S(2)}, u32[]{:S(2)}) collective-permute-start(f32[400,128]{1,0:T(8,128)S(1)} %collective-permute-done.13.refs_3_), channel_id=1, source_target_pairs={{0,1},{1,0},{2,3},{3,2},{4,5},{5,4},{6,7},{7,6},{8,9},{9,8},{10,11... | collective-permute-start | bytes 614408 | tf_op jit(solution)/shard_map/ppermute | solution.py:461
  63.9 11.0 %collective-permute-start.16 = (f32[400,128]{1,0:T(8,128)S(1)}, f32[400,128]{1,0:T(8,128)S(1)}, u32[]{:S(2)}, u32[]{:S(2)}) collective-permute-start(f32[400,128]{1,0:T(8,128)S(1)} %collective-permute-done.12.refs_2_), channel_id=1, source_target_pairs={{0,1},{1,0},{2,3},{3,2},{4,5},{5,4},{6,7},{7,6},{8,9},{9,8},{10,11... | collective-permute-start | bytes 614408 | tf_op jit(solution)/shard_map/ppermute | solution.py:461
  68.4 6.6 %collective-permute-start.15 = (f32[400,128]{1,0:T(8,128)S(1)}, f32[400,128]{1,0:T(8,128)S(1)}, u32[]{:S(2)}, u32[]{:S(2)}) collective-permute-start(f32[400,128]{1,0:T(8,128)S(1)} %collective-permute-done.11.refs_1_), channel_id=1, source_target_pairs={{0,1},{1,0},{2,3},{3,2},{4,5},{5,4},{6,7},{7,6},{8,9},{9,8},{10,11... | collective-permute-start | bytes 614408 | tf_op jit(solution)/shard_map/ppermute | solution.py:461
  77.7 23.6 %all-to-all-start.1 = ((f32[32,16,128]{2,1,0:T(8,128)}), f32[32,16,128]{2,1,0:T(8,128)S(1)}, u32[]{:S(2)}, u32[]{:S(2)}) async-start(f32[32,16,128]{2,1,0:T(8,128)} %search_rows.1), calls=%async_computation.1 | async-start | bytes 524288 | tf_op jit(solution)/shard_map/all_to_all | solution.py:472
  104.5 22.5 %all-to-all-start.2 = ((f32[256,2,128]{2,1,0:T(2,128)}), f32[256,2,128]{2,1,0:T(2,128)S(1)}, u32[]{:S(2)}, u32[]{:S(2)}) async-start(f32[256,2,128]{2,1,0:T(2,128)} %get-tuple-element.29), calls=%async_computation.2 | async-start | bytes 524288 | tf_op jit(solution)/shard_map/all_to_all | solution.py:472
  111.6 16.3 %collective-permute-start.18 = (f32[128,128]{1,0:T(8,128)}, f32[128,128]{1,0:T(8,128)S(1)}, u32[]{:S(2)}, u32[]{:S(2)}) collective-permute-start(f32[128,128]{1,0:T(8,128)} %get-tuple-element.32), channel_id=1, source_target_pairs={{8,0},{16,8},{24,16},{32,24},{40,32},{48,40},{56,48},{64,56},{72,6... | collective-permute-start | bytes 196616 | tf_op jit(solution)/shard_map/ppermute | solution.py:455
  116.2 3.3 %collective-permute-start.19 = (f32[24,128]{1,0:T(8,128)}, f32[24,128]{1,0:T(8,128)S(1)}, u32[]{:S(2)}, u32[]{:S(2)}) collective-permute-start(f32[24,128]{1,0:T(8,128)} %last_weights.1), channel_id=1, source_target_pairs={{0,1},{1,0},{2,3},{3,2},{4,5},{5,4},{6,7},{7,6},{8,9},{9,8},{10,11... | collective-permute-start | bytes 36872 | tf_op jit(solution)/shard_map/ppermute | solution.py:461
  120.3 7.6 %collective-permute-start.22 = (f32[24,128]{1,0:T(8,128)S(1)}, f32[24,128]{1,0:T(8,128)S(1)}, u32[]{:S(2)}, u32[]{:S(2)}) collective-permute-start(f32[24,128]{1,0:T(8,128)S(1)} %add.17.refs_0_), channel_id=1, source_target_pairs={{0,6},{2,0},{4,2},{6,4},{1,7},{3,1},{5,3},{7,5},{8,14},{10,8},{12,... | collective-permute-start | bytes 36872 | tf_op jit(solution)/shard_map/ppermute | solution.py:467
  121.0 6.9 %collective-permute-start.21 = (f32[24,128]{1,0:T(8,128)S(1)}, f32[24,128]{1,0:T(8,128)S(1)}, u32[]{:S(2)}, u32[]{:S(2)}) collective-permute-start(f32[24,128]{1,0:T(8,128)S(1)} %add.17.refs_0_), channel_id=1, source_target_pairs={{0,4},{2,6},{4,0},{6,2},{1,5},{3,7},{5,1},{7,3},{8,12},{10,14},{12... | collective-permute-start | bytes 36872 | tf_op jit(solution)/shard_map/ppermute | solution.py:467
  121.5 6.4 %collective-permute-start.20 = (f32[24,128]{1,0:T(8,128)S(1)}, f32[24,128]{1,0:T(8,128)S(1)}, u32[]{:S(2)}, u32[]{:S(2)}) collective-permute-start(f32[24,128]{1,0:T(8,128)S(1)} %add.17.refs_0_), channel_id=1, source_target_pairs={{0,2},{2,4},{4,6},{6,0},{1,3},{3,5},{5,7},{7,1},{8,10},{10,12},{12... | collective-permute-start | bytes 36872 | tf_op jit(solution)/shard_map/ppermute | solution.py:467
  (24 other events, 123.3 us)

commit v7 on v6

--- a/solution.py
+++ b/solution.py
@@ -128,19 +128,11 @@
 
 def coarse_inverse(sub, sent, subs, modes):
     size = subs * PAD
-    vmem = pl.BlockSpec(memory_space=pltpu.VMEM)
-    return pl.pallas_call(
+    return local_call(
         lambda *refs: inverse_kernel(subs, modes, *refs),
-        out_shape=[
-            jax.ShapeDtypeStruct((size, size), jnp.float32),
-            jax.ShapeDtypeStruct((NEAR * PAD, size), jnp.float32),
-            jax.ShapeDtypeStruct((NEAR * PAD, 128), jnp.float32),
-        ],
-        in_specs=[pl.BlockSpec(memory_space=pltpu.SMEM), vmem],
-        out_specs=[vmem] * 3,
-        scratch_shapes=[pltpu.VMEM((3 * PAD * PAD, 128), jnp.float32)],
-        name="coarse_inverse",
-    )(sub, sent)
+        [(size, size), (NEAR * PAD, size), (NEAR * PAD, 128)], 3, [sent], [sub],
+        [(3 * PAD * PAD, 128)],
+    )
 
 
 def each_piece(pieces, place_ref, copy):
@@ -173,13 +165,29 @@
 SMEM = pl.BlockSpec(memory_space=pltpu.SMEM)
 
 
-def shapes(*dims):
-    return [jax.ShapeDtypeStruct(d, jnp.float32) for d in dims]
-
-
-def stiff_kernel(rows, count, *refs):
+KERNEL_BYTES = 24 << 20
+
+
+def local_call(kernel, outs, kept, arrays, scalars=(), scratch=(), large=None):
+    return pl.pallas_call(
+        kernel,
+        out_shape=[
+            pltpu.VMEM(d, jnp.float32) if k < kept else jax.ShapeDtypeStruct(d, jnp.float32)
+            for k, d in enumerate(outs)
+        ],
+        in_specs=[SMEM] * len(scalars) + [VMEM] * len(arrays),
+        out_specs=[VMEM] * len(outs),
+        scratch_shapes=[pltpu.VMEM(d, jnp.float32) for d in scratch],
+        compiler_params=pltpu.CompilerParams(vmem_limit_bytes=KERNEL_BYTES),
+    )(*scalars, *[
+        a if k == large else pltpu.with_memory_space_constraint(a, pltpu.VMEM)
+        for k, a in enumerate(arrays)
+    ])
+
+
+def stiff_kernel(rows, count, place_ref, *refs):
     pieces, refs = refs[: 2 * count], refs[2 * count :]
-    place_ref, rest_ref, stiff_ref, up_ref, down_ref, image_ref, basis_ref, sent_ref, ext_ref = refs
+    rest_ref, stiff_ref, up_ref, down_ref, image_ref, basis_ref, sent_ref, ext_ref = refs
     face = 2 * count * rows
     basis_ref[2 * PAD :, :face] = jnp.zeros((PAD, face), jnp.float32)
     basis_ref[:PAD, face:] = jnp.zeros((PAD, face), jnp.float32)
@@ -211,25 +219,22 @@
 
 def apply_stiffness(pieces, place, rest, stiff, subs):
     rows, face = stiff.shape[0] // 2, stiff.shape[1] // 2
-    return pl.pallas_call(
+    return local_call(
         lambda *refs: stiff_kernel(rows, len(pieces) // 2, *refs),
-        out_shape=shapes(
+        [
             (rows + 3 * PAD, 128), (rows + 3 * PAD, 128), (3 * PAD, 2 * rows), (3 * PAD, 2 * face),
             (subs, 2 * PAD, 128),
-        ),
-        in_specs=[VMEM] * len(pieces) + [SMEM, VMEM, VMEM],
-        out_specs=[VMEM] * 5,
-        scratch_shapes=[pltpu.VMEM((2 * face, 256), jnp.float32)],
-        name="apply_stiffness",
-    )(*pieces, place, rest, stiff)
-
-
-def search_kernel(share, *refs):
-    pieces, (place_ref, weights_ref, sent_ref) = refs[:-3], refs[-3:]
+        ],
+        4, [*pieces, rest, stiff], [place], [(2 * face, 256)],
+    )
+
+
+def search_kernel(share, place_ref, *refs):
+    pieces, (weights_ref, sent_ref) = refs[:-2], refs[-2:]
     wide = NEAR * PAD
-    sums = pieces[0][...]
+    sums = pieces[0][: 8 * PAD, :]
     for ref in pieces[1:]:
-        sums = sums + ref[...]
+        sums = sums + ref[: 8 * PAD, :]
     weights = jnp.concatenate([weights_ref[...], jnp.zeros((128 - wide, 128), jnp.float32)], 0)
     rows = sums[: 4 * PAD] - dot(sums[4 * PAD :], weights)
     lane = lax.broadcasted_iota(jnp.int32, (PAD, 128), 1)
@@ -249,21 +254,16 @@
 
 
 def search_rows(pieces, place, weights, subs):
-    return pl.pallas_call(
+    return local_call(
         lambda *refs: search_kernel(128 // len(pieces), *refs),
-        grid=(1,),
-        out_shape=shapes((subs, 2 * PAD, 128))[0],
-        in_specs=[pl.BlockSpec((8 * PAD, 128), lambda i: (0, 0))] * len(pieces)
-        + [SMEM, pl.BlockSpec(weights.shape, lambda i: (0, 0))],
-        out_specs=pl.BlockSpec((subs, 2 * PAD, 128), lambda i: (0, 0, 0)),
-        name="search_rows",
-    )(*pieces, place, weights)
-
-
-def flex_kernel(rows, count, *refs):
+        [(subs, 2 * PAD, 128)], 0, [*pieces, weights], [place],
+    )[0]
+
+
+def flex_kernel(rows, count, place_ref, *refs):
     pieces, refs = refs[: 2 * count], refs[2 * count :]
-    place_ref, flex_ref, weights_ref, own_ref, own_modes_ref, field_ref, own_basis_ref, flex_modes_ref = refs[:8]
-    image_ref, search_ref, res_ref, turned_ref, ext_ref = refs[8:]
+    flex_ref, weights_ref, own_ref, own_modes_ref, field_ref, own_basis_ref, flex_modes_ref = refs[:7]
+    image_ref, search_ref, res_ref, turned_ref, ext_ref = refs[7:]
     face = 2 * count * rows
     wide = NEAR * PAD
     head = 8 * PAD
@@ -298,16 +298,13 @@
     res_ref[...] = field_ref[...] - dot(turned[rows:], shifted)
 
 
-def apply_flexibility(pieces, place, flex, weights, own, own_modes, field, own_basis, flex_modes):
-    rows = field.shape[0]
-    return pl.pallas_call(
+def apply_flexibility(pieces, place, *arrays):
+    rows = arrays[0].shape[0] // 2
+    return local_call(
         lambda *refs: flex_kernel(rows, len(pieces) // 2, *refs),
-        out_shape=shapes((2 * rows, 128), (2 * rows, 128), (rows, 128), (2 * rows, 128)),
-        in_specs=[VMEM] * len(pieces) + [SMEM] + [VMEM] * 7,
-        out_specs=[VMEM] * 4,
-        scratch_shapes=[pltpu.VMEM((2 * len(pieces) * rows, 256), jnp.float32)],
-        name="apply_flexibility",
-    )(*pieces, place, flex, weights, own, own_modes, field, own_basis, flex_modes)
+        [(2 * rows, 128), (2 * rows, 128), (rows, 128), (2 * rows, 128)], 4, [*pieces, *arrays],
+        [place], [(2 * len(pieces) * rows, 256)], len(pieces),
+    )
 
 
 def chosen(a, choice):
@@ -378,13 +375,10 @@
 
 
 def last_weights(place, second, inverse, near, subs, modes, share):
-    return pl.pallas_call(
+    return local_call(
         lambda *refs: last_kernel(subs, modes, share, *refs),
-        out_shape=shapes((3 * PAD, 128))[0],
-        in_specs=[SMEM] + [VMEM] * 3,
-        out_specs=VMEM,
-        name="last_weights",
-    )(place, second, inverse, near)
+        [(3 * PAD, 128)], 1, [second, inverse, near], [place],
+    )[0]
 
 
 def direction_kernel(subs, second_ref, near_ref, turned_ref, image_ref, search_ref, res_ref, low_ref, high_ref,
@@ -416,16 +410,14 @@
 
 def project_direction(second, near, turned, image, search, res, subs, devices):
     rows = res.shape[0]
-    return pl.pallas_call(
+    return local_call(
         lambda *refs: direction_kernel(subs, *refs),
-        out_shape=shapes((rows, 128), (rows, 128), (rows, 128), (devices, 2, 128)),
-        in_specs=[VMEM] * 6,
-        out_specs=[VMEM] * 4,
-        name="project_direction",
-    )(second, near, turned, image, search, res)
-
-
-def result_kernel(totals_ref, direction_ref, res_ref, high_ref, after_ref, turned_ref, live_ref, *refs):
+        [(rows, 128), (rows, 128), (rows, 128), (devices, 2, 128)], 3,
+        [second, near, turned, image, search, res],
+    )
+
+
+def result_kernel(live_ref, totals_ref, direction_ref, res_ref, high_ref, after_ref, turned_ref, *refs):
     parts, (multipliers_ref, residual_ref) = refs[:-2], refs[-2:]
     weights = parts[0][...]
     for part in parts[1:]:
@@ -441,13 +433,10 @@
 
 
 def results(totals, direction, res, high, after, turned, live, parts):
-    return pl.pallas_call(
-        result_kernel,
-        out_shape=shapes((1, *res.shape), (1, *res.shape)),
-        in_specs=[VMEM] * 6 + [SMEM] + [VMEM] * len(parts),
-        out_specs=[VMEM] * 2,
-        name="results",
-    )(totals, direction, res, high, after, turned, live[None], *parts)
+    return local_call(
+        result_kernel, [(1, *res.shape)] * 2, 0,
+        [totals, direction, res, high, after, turned, *parts], [live[None]],
+    )
 
 
 def moved_along(block, distance):

time: 132 us -> 129 us (0.977)
  Pallas kernels: 24.8 us -> 16.9 us
  local copies, waits for them, and re-layouts: 5.04 us -> 12.1 us
  waiting for transfers between devices: 18.1 us -> 15.2 us
  starting transfers between devices: 72.1 us -> 74.8 us
  other arithmetic: 5.4 us -> 3.91 us
    pallas_call x7, Pallas kernels: 24.8 us -> 16.9 us  [local_call(): pl.pallas_call(kernel, out_shape=[pltpu.VMEM(d, jnp.float32) if k < kept...]
    unnamed x66 -> x50, local copies, waits for them, and re-layouts: 4.36 us -> 12 us
    ppermute x9, waiting for transfers between devices: 5.32 us -> 3.57 us  [along_x(): lax.ppermute(piece, 'x', [(i, (i + d) % n) for i in range(n)])]
    all_to_all x3, waiting for transfers between devices: 10.4 us -> 8.64 us  [to_all(): return lax.all_to_all(values, axis, 0, 0, tiled=True)]
    ppermute x9, starting transfers between devices: 18.9 us -> 20.6 us  [core_swap(): return lax.ppermute(block, 'c', [(0, 1), (1, 0)])]
  transfers between devices with their start and end apart: 26 -> 26, of which waited for: 7 -> 8; matrix products, arithmetic and copies ran while one was open for 7% -> 5% of each run, Pallas kernels for 11% -> 7%
where the time goes in v7:
time: 129 us; the launch traced here: 127 us
  starting transfers between devices  74.8 us (58%)
  Pallas kernels  16.9 us (13%)
  waiting for transfers between devices  15.2 us (12%)
  local copies, waits for them, and re-layouts  12.1 us (9%)
  other arithmetic  3.91 us (3%)
  matrix products  2.12 us (2%)
  between operations  1.75 us (1%)
    all_to_all x3, starting transfers between devices, to_all(): return lax.all_to_all(values, axis, 0, 0, tiled=True)  34.5 us
    ppermute x9, starting transfers between devices, core_swap(): return lax.ppermute(block, 'c', [(0, 1), (1, 0)])  20.6 us
    pallas_call x7, Pallas kernels, local_call(): pl.pallas_call(kernel, out_shape=[pltpu.VMEM(d, jnp.float32) if k < kept...  16.9 us
    ppermute x5, starting transfers between devices, moved_along(): lax.ppermute(block, SUB, [(i - distance, i) for i in range(n) if 0 <= i -...  12.5 us
    unnamed x50, local copies, waits for them, and re-layouts  12 us
    all_to_all x3, waiting for transfers between devices, to_all(): return lax.all_to_all(values, axis, 0, 0, tiled=True)  8.64 us
    ppermute x9, starting transfers between devices, along_x(): lax.ppermute(piece, 'x', [(i, (i + d) % n) for i in range(n)])  7.27 us
    ppermute x9, waiting for transfers between devices, along_x(): lax.ppermute(piece, 'x', [(i, (i + d) % n) for i in range(n)])  3.57 us
  transfers between devices with their start and end apart: 26, of which 8 were waited for; matrix products, arithmetic and copies ran while one was open for 5% of the time, Pallas kernels for 7%

profile of v7, /device:TPU:1, one launch (start us, length us, event | category | flops | bytes accessed | tf_op | source)
XLA Modules:
  0.0 126.8 jit_solution(837007236377119158)
XLA Ops:
  2.1 1.3 %collective-permute-start.1 = (f32[8,128]{1,0:T(8,128)S(1)}, f32[8,128]{1,0:T(8,128)S(1)}, u32[]{:S(2)}, u32[]{:S(2)}) collective-permute-start(f32[8,128]{1,0:T(8,128)S(1)} %get-tuple-element.41), channel_id=1, source_target_pairs={{8,0},{16,8},{24,16},{32,24},{40,32},{48,40},{56,48},{64,56},{72,6... | collective-permute-start | bytes 12296 | tf_op jit(solution)/shard_map/ppermute | solution.py:444
  4.2 4.7 %collective-permute-start = (f32[136,128]{1,0:T(8,128)S(1)}, f32[136,128]{1,0:T(8,128)S(1)}, u32[]{:S(2)}, u32[]{:S(2)}) collective-permute-start(f32[136,128]{1,0:T(8,128)S(1)} %pad_maximum_fusion.1), channel_id=1, source_target_pairs={{0,8},{8,16},{16,24},{24,32},{32,40},{40,48},{48,56},{56,64},{64,7... | collective-permute-start | bytes 208904 | tf_op jit(solution)/shard_map/ppermute | solution.py:444
  8.9 1.3 %collective-permute-done = f32[136,128]{1,0:T(8,128)S(1)} collective-permute-done((f32[136,128]{1,0:T(8,128)S(1)}, f32[136,128]{1,0:T(8,128)S(1)}, u32[]{:S(2)}, u32[]{:S(2)}) %collective-permute-start) | collective-permute-done | bytes 69664 | tf_op jit(solution)/shard_map/ppermute | solution.py:444
  11.1 2.7 %collective-permute-start.4 = (f32[288,128]{1,0:T(8,128)S(1)}, f32[288,128]{1,0:T(8,128)S(1)}, u32[]{:S(2)}, u32[]{:S(2)}) collective-permute-start(f32[288,128]{1,0:T(8,128)S(1)} %get-tuple-element.44.refs_1_), channel_id=1, source_target_pairs={{0,6},{2,0},{4,2},{6,4},{1,7},{3,1},{5,3},{7,5},{8,14},{10,8},{12,... | collective-permute-start | bytes 442376 | tf_op jit(solution)/shard_map/ppermute | solution.py:456
  15.0 2.6 %collective-permute-start.5 = (f32[288,128]{1,0:T(8,128)S(1)}, f32[288,128]{1,0:T(8,128)S(1)}, u32[]{:S(2)}, u32[]{:S(2)}) collective-permute-start(f32[288,128]{1,0:T(8,128)S(1)} %get-tuple-element.44.refs_1_), channel_id=1, source_target_pairs={{0,1},{1,0},{2,3},{3,2},{4,5},{5,4},{6,7},{7,6},{8,9},{9,8},{10,11... | collective-permute-start | bytes 442376 | tf_op jit(solution)/shard_map/ppermute | solution.py:450
  18.0 3.1 %collective-permute-start.8 = (f32[288,128]{1,0:T(8,128)S(1)}, f32[288,128]{1,0:T(8,128)S(1)}, u32[]{:S(2)}, u32[]{:S(2)}) collective-permute-start(f32[288,128]{1,0:T(8,128)S(1)} %collective-permute-done.4.refs_4_), channel_id=1, source_target_pairs={{0,1},{1,0},{2,3},{3,2},{4,5},{5,4},{6,7},{7,6},{8,9},{9,8},{10,11... | collective-permute-start | bytes 442376 | tf_op jit(solution)/shard_map/ppermute | solution.py:450
  21.1 2.1 %collective-permute-start.7 = (f32[288,128]{1,0:T(8,128)S(1)}, f32[288,128]{1,0:T(8,128)S(1)}, u32[]{:S(2)}, u32[]{:S(2)}) collective-permute-start(f32[288,128]{1,0:T(8,128)S(1)} %collective-permute-done.3.refs_3_), channel_id=1, source_target_pairs={{0,1},{1,0},{2,3},{3,2},{4,5},{5,4},{6,7},{7,6},{8,9},{9,8},{10,11... | collective-permute-start | bytes 442376 | tf_op jit(solution)/shard_map/ppermute | solution.py:450
  23.2 1.6 %collective-permute-start.6 = (f32[288,128]{1,0:T(8,128)S(1)}, f32[288,128]{1,0:T(8,128)S(1)}, u32[]{:S(2)}, u32[]{:S(2)}) collective-permute-start(f32[288,128]{1,0:T(8,128)S(1)} %collective-permute-done.2.refs_2_), channel_id=1, source_target_pairs={{0,1},{1,0},{2,3},{3,2},{4,5},{5,4},{6,7},{7,6},{8,9},{9,8},{10,11... | collective-permute-start | bytes 442376 | tf_op jit(solution)/shard_map/ppermute | solution.py:450
  25.8 1.6 %copy-done.1 = f32[1,2,128,2048]{3,2,1,0:T(8,128)S(1)} copy-done((f32[1,2,128,2048]{3,2,1,0:T(8,128)S(1)}, f32[1,2,128,2048]{3,2,1,0:T(8,128)}, u32[]{:S(2)}) %copy-start.1) | copy-done | bytes 2097176
  27.4 3.3 %shard_map.68 = (f32[152,128]{1,0:T(8,128)S(1)}, f32[152,128]{1,0:T(8,128)S(1)}, f32[24,256]{1,0:T(8,128)S(1)}, f32[24,2048]{1,0:T(8,128)S(1)}, f32[32,16,128]{2,1,0:T(8,128)}) custom-call(s32[2]{0:T(128)S(1)} %pad_add_fusion.refs_0_, f32[288,128]{1,0:T(8,128)S(1)} %get-tuple-element.44.refs_1_, f32[288,128]{1,0:T(8,128)S(1)} %collective-permute-done.2.refs_2_, ...), custom_call_target="tpu_custom_call" | custom-call | tf_op jit(solution)/shard_map/pallas_call | solution.py:172
  30.7 14.5 %all-to-all-start = ((f32[32,16,128]{2,1,0:T(8,128)}), f32[32,16,128]{2,1,0:T(8,128)S(1)}, u32[]{:S(2)}, u32[]{:S(2)}) async-start(f32[32,16,128]{2,1,0:T(8,128)} %get-tuple-element.22), calls=%async_computation | async-start | bytes 524288 | tf_op jit(solution)/shard_map/all_to_all | solution.py:461
  45.2 1.3 %collective-permute-start.10 = (f32[152,128]{1,0:T(8,128)S(1)}, f32[152,128]{1,0:T(8,128)S(1)}, u32[]{:S(2)}, u32[]{:S(2)}) collective-permute-start(f32[152,128]{1,0:T(8,128)S(1)} %get-tuple-element.19), channel_id=1, source_target_pairs={{8,0},{16,8},{24,16},{32,24},{40,32},{48,40},{56,48},{64,56},{72,6... | collective-permute-start | bytes 233480 | tf_op jit(solution)/shard_map/ppermute | solution.py:444
  46.5 4.0 %collective-permute-start.9 = (f32[152,128]{1,0:T(8,128)S(1)}, f32[152,128]{1,0:T(8,128)S(1)}, u32[]{:S(2)}, u32[]{:S(2)}) collective-permute-start(f32[152,128]{1,0:T(8,128)S(1)} %get-tuple-element.20), channel_id=1, source_target_pairs={{0,8},{8,16},{16,24},{24,32},{32,40},{40,48},{48,56},{56,64},{64,7... | collective-permute-start | bytes 233480 | tf_op jit(solution)/shard_map/ppermute | solution.py:444
  50.5 1.7 %fusion.28.refs_15_ = f32[24,256]{1,0:T(8,128)S(1)} fusion(f32[24,2048]{1,0:T(8,128)S(1)} %get-tuple-element.18, f32[256,2048]{1,0:T(8,128)S(1)} %bitcast.25), kind=kOutput, calls=%fused_computation.62 | convolution fusion | flops 150994944 | bytes 2318336 | tf_op jit(solution)/shard_map/dot_general | solution.py:23
  54.7 2.1 %collective-permute-start.14 = (f32[400,128]{1,0:T(8,128)S(1)}, f32[400,128]{1,0:T(8,128)S(1)}, u32[]{:S(2)}, u32[]{:S(2)}) collective-permute-start(f32[400,128]{1,0:T(8,128)S(1)} %constant_dynamic-update-slice_fusion.5.refs_1_), channel_id=1, source_target_pairs={{0,1},{1,0},{2,3},{3,2},{4,5},{5,4},{6,7},{7,6},{8,9},{9,8},{10,11... | collective-permute-start | bytes 614408 | tf_op jit(solution)/shard_map/ppermute | solution.py:450
  56.8 1.6 %collective-permute-done.13.refs_4_ = f32[400,128]{1,0:T(8,128)S(1)} collective-permute-done((f32[400,128]{1,0:T(8,128)S(1)}, f32[400,128]{1,0:T(8,128)S(1)}, u32[]{:S(2)}, u32[]{:S(2)}) %collective-permute-start.13) | collective-permute-done | bytes 204832 | tf_op jit(solution)/shard_map/ppermute | solution.py:456
  58.4 4.1 %collective-permute-start.17 = (f32[400,128]{1,0:T(8,128)S(1)}, f32[400,128]{1,0:T(8,128)}, u32[]{:S(2)}, u32[]{:S(2)}) collective-permute-start(f32[400,128]{1,0:T(8,128)S(1)} %collective-permute-done.13.refs_4_), channel_id=1, source_target_pairs={{0,1},{1,0},{2,3},{3,2},{4,5},{5,4},{6,7},{7,6},{8,9},{9,8},{10,11... | collective-permute-start | bytes 614408 | tf_op jit(solution)/shard_map/ppermute | solution.py:450
  62.5 2.1 %collective-permute-start.16 = (f32[400,128]{1,0:T(8,128)S(1)}, f32[400,128]{1,0:T(8,128)}, u32[]{:S(2)}, u32[]{:S(2)}) collective-permute-start(f32[400,128]{1,0:T(8,128)S(1)} %collective-permute-done.12.refs_3_), channel_id=1, source_target_pairs={{0,1},{1,0},{2,3},{3,2},{4,5},{5,4},{6,7},{7,6},{8,9},{9,8},{10,11... | collective-permute-start | bytes 614408 | tf_op jit(solution)/shard_map/ppermute | solution.py:450
  64.7 1.6 %collective-permute-done.11.refs_2_ = f32[400,128]{1,0:T(8,128)S(1)} collective-permute-done((f32[400,128]{1,0:T(8,128)S(1)}, f32[400,128]{1,0:T(8,128)S(1)}, u32[]{:S(2)}, u32[]{:S(2)}) %collective-permute-start.11) | collective-permute-done | bytes 204832 | tf_op jit(solution)/shard_map/ppermute | solution.py:456
  66.9 3.8 %shard_map.69 = (f32[256,256]{1,0:T(8,128)S(1)}, f32[40,256]{1,0:T(8,128)S(1)}, f32[40,128]{1,0:T(8,128)S(1)}) custom-call(s32[1]{0:T(128)} %bitcast.10.refs_0_, f32[512,128]{1,0:T(8,128)S(1)} %bitcast.30), custom_call_target="tpu_custom_call" | custom-call | tf_op jit(solution)/shard_map/pallas_call | solution.py:172
  71.5 2.1 %shard_map.70 = f32[32,16,128]{2,1,0:T(8,128)} custom-call(s32[2]{0:T(128)S(1)} %pad_add_fusion.refs_0_, f32[400,128]{1,0:T(8,128)S(1)} %constant_dynamic-update-slice_fusion.5.refs_1_, f32[400,128]{1,0:T(8,128)S(1)} %collective-permute-done.11.refs_2_, f32[400,128]{1,0:T(8,128)S(1)} %collective-permute-done.12.refs_3_, ...), custom_call_target="tpu_custom_call" | custom-call | tf_op jit(solution)/shard_map/pallas_call | solution.py:172
  73.6 12.5 %all-to-all-start.1 = ((f32[32,16,128]{2,1,0:T(8,128)}), f32[32,16,128]{2,1,0:T(8,128)S(1)}, u32[]{:S(2)}, u32[]{:S(2)}) async-start(f32[32,16,128]{2,1,0:T(8,128)} %shard_map.70), calls=%async_computation.1 | async-start | bytes 524288 | tf_op jit(solution)/shard_map/all_to_all | solution.py:461
  89.1 3.3 %shard_map.71 = (f32[256,128]{1,0:T(8,128)S(1)}, f32[256,128]{1,0:T(8,128)S(1)}, f32[128,128]{1,0:T(8,128)S(1)}, f32[256,128]{1,0:T(8,128)S(1)}) custom-call(s32[2]{0:T(128)S(1)} %pad_add_fusion.refs_0_, f32[400,128]{1,0:T(8,128)S(1)} %constant_dynamic-update-slice_fusion.5.refs_1_, f32[400,128]{1,0:T(8,128)S(1)} %collective-permute-done.11.refs_2_, ...), custom_call_target="tpu_custom_call" | custom-call | tf_op jit(solution)/shard_map/pallas_call | solution.py:172
  94.4 3.5 %all-to-all-done.1 = f32[32,16,128]{2,1,0:T(8,128)S(1)} async-done(((f32[32,16,128]{2,1,0:T(8,128)}), f32[32,16,128]{2,1,0:T(8,128)S(1)}, u32[]{:S(2)}, u32[]{:S(2)}) %all-to-all-start.1) | async-done | bytes 262176 | tf_op jit(solution)/shard_map/all_to_all | solution.py:461
  98.0 0.9 copy-done.3
  101.5 1.3 %shard_map.72 = (f32[128,128]{1,0:T(8,128)S(1)}, f32[128,128]{1,0:T(8,128)S(1)}, f32[128,128]{1,0:T(8,128)S(1)}, f32[256,2,128]{2,1,0:T(2,128)}) custom-call(f32[512,128]{1,0:T(8,128)S(1)} %bitcast.27, f32[40,256]{1,0:T(8,128)S(1)} %copy-done.8, f32[256,128]{1,0:T(8,128)S(1)} %copy-done.3, f32[256,128]{1,0:T(8,128)S(1)} %copy-done.13, ...), custom_call_target="tpu_custom_call" | custom-call | tf_op jit(solution)/shard_map/pallas_call | solution.py:172
  102.8 7.5 %all-to-all-start.2 = ((f32[256,2,128]{2,1,0:T(2,128)}), f32[256,2,128]{2,1,0:T(2,128)S(1)}, u32[]{:S(2)}, u32[]{:S(2)}) async-start(f32[256,2,128]{2,1,0:T(2,128)} %get-tuple-element.29), calls=%async_computation.2 | async-start | bytes 524288 | tf_op jit(solution)/shard_map/all_to_all | solution.py:461
  110.3 1.3 %collective-permute-start.18 = (f32[128,128]{1,0:T(8,128)S(1)}, f32[128,128]{1,0:T(8,128)S(1)}, u32[]{:S(2)}, u32[]{:S(2)}) collective-permute-start(f32[128,128]{1,0:T(8,128)S(1)} %get-tuple-element.32), channel_id=1, source_target_pairs={{8,0},{16,8},{24,16},{32,24},{40,32},{48,40},{56,48},{64,56},{72,6... | collective-permute-start | bytes 196616 | tf_op jit(solution)/shard_map/ppermute | solution.py:444
  111.6 0.9 copy-done.6
  113.4 2.2 %shard_map.73 = f32[24,128]{1,0:T(8,128)S(1)} custom-call(s32[2]{0:T(128)S(1)} %pad_add_fusion.refs_0_, f32[512,128]{1,0:T(8,128)S(1)} %bitcast.28, f32[256,256]{1,0:T(8,128)S(1)} %copy-done.6, f32[40,256]{1,0:T(8,128)S(1)} %copy-done.9), custom_call_target="tpu_custom_call" | custom-call | tf_op jit(solution)/shard_map/pallas_call | solution.py:172
  115.5 2.2 %collective-permute-start.19 = (f32[24,128]{1,0:T(8,128)S(1)}, f32[24,128]{1,0:T(8,128)S(1)}, u32[]{:S(2)}, u32[]{:S(2)}) collective-permute-start(f32[24,128]{1,0:T(8,128)S(1)} %shard_map.73), channel_id=1, source_target_pairs={{0,1},{1,0},{2,3},{3,2},{4,5},{5,4},{6,7},{7,6},{8,9},{9,8},{10,11... | collective-permute-start | bytes 36872 | tf_op jit(solution)/shard_map/ppermute | solution.py:450
  120.5 5.1 %all-to-all-done.2 = f32[256,2,128]{2,1,0:T(2,128)S(1)} async-done(((f32[256,2,128]{2,1,0:T(2,128)}), f32[256,2,128]{2,1,0:T(2,128)S(1)}, u32[]{:S(2)}, u32[]{:S(2)}) %all-to-all-start.2) | async-done | bytes 262176 | tf_op jit(solution)/shard_map/all_to_all | solution.py:461
  (108 shorter events, 21.0 us)
Async XLA Ops:
  2.1 9.0 %collective-permute-start.1 = (f32[8,128]{1,0:T(8,128)S(1)}, f32[8,128]{1,0:T(8,128)S(1)}, u32[]{:S(2)}, u32[]{:S(2)}) collective-permute-start(f32[8,128]{1,0:T(8,128)S(1)} %get-tuple-element.41), channel_id=1, source_target_pairs={{8,0},{16,8},{24,16},{32,24},{40,32},{48,40},{56,48},{64,56},{72,6... | collective-permute-start | bytes 12296 | tf_op jit(solution)/shard_map/ppermute | solution.py:444
  4.2 6.0 %collective-permute-start = (f32[136,128]{1,0:T(8,128)S(1)}, f32[136,128]{1,0:T(8,128)S(1)}, u32[]{:S(2)}, u32[]{:S(2)}) collective-permute-start(f32[136,128]{1,0:T(8,128)S(1)} %pad_maximum_fusion.1), channel_id=1, source_target_pairs={{0,8},{8,16},{16,24},{24,32},{32,40},{40,48},{48,56},{56,64},{64,7... | collective-permute-start | bytes 208904 | tf_op jit(solution)/shard_map/ppermute | solution.py:444
  8.9 41.6 %copy-start = (f32[1,2,128,2048]{3,2,1,0:T(8,128)S(1)}, f32[1,2,128,2048]{3,2,1,0:T(8,128)}, u32[]{:S(2)}) copy-start(f32[1,2,128,2048]{3,2,1,0:T(8,128)} %param.6) | copy-start | bytes 6291460
  11.1 6.9 %collective-permute-start.4 = (f32[288,128]{1,0:T(8,128)S(1)}, f32[288,128]{1,0:T(8,128)S(1)}, u32[]{:S(2)}, u32[]{:S(2)}) collective-permute-start(f32[288,128]{1,0:T(8,128)S(1)} %get-tuple-element.44.refs_1_), channel_id=1, source_target_pairs={{0,6},{2,0},{4,2},{6,4},{1,7},{3,1},{5,3},{7,5},{8,14},{10,8},{12,... | collective-permute-start | bytes 442376 | tf_op jit(solution)/shard_map/ppermute | solution.py:456
  13.8 7.3 %collective-permute-start.3 = (f32[288,128]{1,0:T(8,128)S(1)}, f32[288,128]{1,0:T(8,128)S(1)}, u32[]{:S(2)}, u32[]{:S(2)}) collective-permute-start(f32[288,128]{1,0:T(8,128)S(1)} %get-tuple-element.44.refs_1_), channel_id=1, source_target_pairs={{0,4},{2,6},{4,0},{6,2},{1,5},{3,7},{5,1},{7,3},{8,12},{10,14},{12... | collective-permute-start | bytes 442376 | tf_op jit(solution)/shard_map/ppermute | solution.py:456
  14.4 8.8 %collective-permute-start.2 = (f32[288,128]{1,0:T(8,128)S(1)}, f32[288,128]{1,0:T(8,128)S(1)}, u32[]{:S(2)}, u32[]{:S(2)}) collective-permute-start(f32[288,128]{1,0:T(8,128)S(1)} %get-tuple-element.44.refs_1_), channel_id=1, source_target_pairs={{0,2},{2,4},{4,6},{6,0},{1,3},{3,5},{5,7},{7,1},{8,10},{10,12},{12... | collective-permute-start | bytes 442376 | tf_op jit(solution)/shard_map/ppermute | solution.py:456
  15.0 9.9 %collective-permute-start.5 = (f32[288,128]{1,0:T(8,128)S(1)}, f32[288,128]{1,0:T(8,128)S(1)}, u32[]{:S(2)}, u32[]{:S(2)}) collective-permute-start(f32[288,128]{1,0:T(8,128)S(1)} %get-tuple-element.44.refs_1_), channel_id=1, source_target_pairs={{0,1},{1,0},{2,3},{3,2},{4,5},{5,4},{6,7},{7,6},{8,9},{9,8},{10,11... | collective-permute-start | bytes 442376 | tf_op jit(solution)/shard_map/ppermute | solution.py:450
  18.0 6.9 %collective-permute-start.8 = (f32[288,128]{1,0:T(8,128)S(1)}, f32[288,128]{1,0:T(8,128)S(1)}, u32[]{:S(2)}, u32[]{:S(2)}) collective-permute-start(f32[288,128]{1,0:T(8,128)S(1)} %collective-permute-done.4.refs_4_), channel_id=1, source_target_pairs={{0,1},{1,0},{2,3},{3,2},{4,5},{5,4},{6,7},{7,6},{8,9},{9,8},{10,11... | collective-permute-start | bytes 442376 | tf_op jit(solution)/shard_map/ppermute | solution.py:450
  21.1 3.9 %collective-permute-start.7 = (f32[288,128]{1,0:T(8,128)S(1)}, f32[288,128]{1,0:T(8,128)S(1)}, u32[]{:S(2)}, u32[]{:S(2)}) collective-permute-start(f32[288,128]{1,0:T(8,128)S(1)} %collective-permute-done.3.refs_3_), channel_id=1, source_target_pairs={{0,1},{1,0},{2,3},{3,2},{4,5},{5,4},{6,7},{7,6},{8,9},{9,8},{10,11... | collective-permute-start | bytes 442376 | tf_op jit(solution)/shard_map/ppermute | solution.py:450
  23.2 2.6 %collective-permute-start.6 = (f32[288,128]{1,0:T(8,128)S(1)}, f32[288,128]{1,0:T(8,128)S(1)}, u32[]{:S(2)}, u32[]{:S(2)}) collective-permute-start(f32[288,128]{1,0:T(8,128)S(1)} %collective-permute-done.2.refs_2_), channel_id=1, source_target_pairs={{0,1},{1,0},{2,3},{3,2},{4,5},{5,4},{6,7},{7,6},{8,9},{9,8},{10,11... | collective-permute-start | bytes 442376 | tf_op jit(solution)/shard_map/ppermute | solution.py:450
  24.9 5.7 %copy-start.10 = (f32[24,256]{1,0:T(8,128)}, f32[24,256]{1,0:T(8,128)S(1)}, u32[]{:S(2)}) copy-start(f32[24,256]{1,0:T(8,128)S(1)} %maximum_maximum_fusion.refs_14_) | copy-start | bytes 73732
  30.7 36.3 %all-to-all-start = ((f32[32,16,128]{2,1,0:T(8,128)}), f32[32,16,128]{2,1,0:T(8,128)S(1)}, u32[]{:S(2)}, u32[]{:S(2)}) async-start(f32[32,16,128]{2,1,0:T(8,128)} %get-tuple-element.22), calls=%async_computation | async-start | bytes 524288 | tf_op jit(solution)/shard_map/all_to_all | solution.py:461
  45.2 7.1 %collective-permute-start.10 = (f32[152,128]{1,0:T(8,128)S(1)}, f32[152,128]{1,0:T(8,128)S(1)}, u32[]{:S(2)}, u32[]{:S(2)}) collective-permute-start(f32[152,128]{1,0:T(8,128)S(1)} %get-tuple-element.19), channel_id=1, source_target_pairs={{8,0},{16,8},{24,16},{32,24},{40,32},{48,40},{56,48},{64,56},{72,6... | collective-permute-start | bytes 233480 | tf_op jit(solution)/shard_map/ppermute | solution.py:444
  46.5 5.8 %collective-permute-start.9 = (f32[152,128]{1,0:T(8,128)S(1)}, f32[152,128]{1,0:T(8,128)S(1)}, u32[]{:S(2)}, u32[]{:S(2)}) collective-permute-start(f32[152,128]{1,0:T(8,128)S(1)} %get-tuple-element.20), channel_id=1, source_target_pairs={{0,8},{8,16},{16,24},{24,32},{32,40},{40,48},{48,56},{56,64},{64,7... | collective-permute-start | bytes 233480 | tf_op jit(solution)/shard_map/ppermute | solution.py:444
  52.5 14.4 %copy-start.18 = (f32[128,128]{1,0:T(8,128)}, f32[128,128]{1,0:T(8,128)S(1)}, u32[]{:S(2)}) copy-start(f32[128,128]{1,0:T(8,128)S(1)} %fusion) | copy-start | bytes 196612
  53.2 5.2 %collective-permute-start.13 = (f32[400,128]{1,0:T(8,128)S(1)}, f32[400,128]{1,0:T(8,128)S(1)}, u32[]{:S(2)}, u32[]{:S(2)}) collective-permute-start(f32[400,128]{1,0:T(8,128)S(1)} %constant_dynamic-update-slice_fusion.5.refs_1_), channel_id=1, source_target_pairs={{0,6},{2,0},{4,2},{6,4},{1,7},{3,1},{5,3},{7,5},{8,14},{10,8},{12,... | collective-permute-start | bytes 614408 | tf_op jit(solution)/shard_map/ppermute | solution.py:456
  53.5 9.0 %collective-permute-start.12 = (f32[400,128]{1,0:T(8,128)S(1)}, f32[400,128]{1,0:T(8,128)S(1)}, u32[]{:S(2)}, u32[]{:S(2)}) collective-permute-start(f32[400,128]{1,0:T(8,128)S(1)} %constant_dynamic-update-slice_fusion.5.refs_1_), channel_id=1, source_target_pairs={{0,4},{2,6},{4,0},{6,2},{1,5},{3,7},{5,1},{7,3},{8,12},{10,14},{12... | collective-permute-start | bytes 614408 | tf_op jit(solution)/shard_map/ppermute | solution.py:456
  54.0 12.3 %collective-permute-start.11 = (f32[400,128]{1,0:T(8,128)S(1)}, f32[400,128]{1,0:T(8,128)S(1)}, u32[]{:S(2)}, u32[]{:S(2)}) collective-permute-start(f32[400,128]{1,0:T(8,128)S(1)} %constant_dynamic-update-slice_fusion.5.refs_1_), channel_id=1, source_target_pairs={{0,2},{2,4},{4,6},{6,0},{1,3},{3,5},{5,7},{7,1},{8,10},{10,12},{12... | collective-permute-start | bytes 614408 | tf_op jit(solution)/shard_map/ppermute | solution.py:456
  54.7 16.8 %collective-permute-start.14 = (f32[400,128]{1,0:T(8,128)S(1)}, f32[400,128]{1,0:T(8,128)S(1)}, u32[]{:S(2)}, u32[]{:S(2)}) collective-permute-start(f32[400,128]{1,0:T(8,128)S(1)} %constant_dynamic-update-slice_fusion.5.refs_1_), channel_id=1, source_target_pairs={{0,1},{1,0},{2,3},{3,2},{4,5},{5,4},{6,7},{7,6},{8,9},{9,8},{10,11... | collective-permute-start | bytes 614408 | tf_op jit(solution)/shard_map/ppermute | solution.py:450
  58.4 13.0 %collective-permute-start.17 = (f32[400,128]{1,0:T(8,128)S(1)}, f32[400,128]{1,0:T(8,128)}, u32[]{:S(2)}, u32[]{:S(2)}) collective-permute-start(f32[400,128]{1,0:T(8,128)S(1)} %collective-permute-done.13.refs_4_), channel_id=1, source_target_pairs={{0,1},{1,0},{2,3},{3,2},{4,5},{5,4},{6,7},{7,6},{8,9},{9,8},{10,11... | collective-permute-start | bytes 614408 | tf_op jit(solution)/shard_map/ppermute | solution.py:450
  62.5 8.9 %collective-permute-start.16 = (f32[400,128]{1,0:T(8,128)S(1)}, f32[400,128]{1,0:T(8,128)}, u32[]{:S(2)}, u32[]{:S(2)}) collective-permute-start(f32[400,128]{1,0:T(8,128)S(1)} %collective-permute-done.12.refs_3_), channel_id=1, source_target_pairs={{0,1},{1,0},{2,3},{3,2},{4,5},{5,4},{6,7},{7,6},{8,9},{9,8},{10,11... | collective-permute-start | bytes 614408 | tf_op jit(solution)/shard_map/ppermute | solution.py:450
  66.3 5.2 %collective-permute-start.15 = (f32[400,128]{1,0:T(8,128)S(1)}, f32[400,128]{1,0:T(8,128)}, u32[]{:S(2)}, u32[]{:S(2)}) collective-permute-start(f32[400,128]{1,0:T(8,128)S(1)} %collective-permute-done.11.refs_2_), channel_id=1, source_target_pairs={{0,1},{1,0},{2,3},{3,2},{4,5},{5,4},{6,7},{7,6},{8,9},{9,8},{10,11... | collective-permute-start | bytes 614408 | tf_op jit(solution)/shard_map/ppermute | solution.py:450
  71.4 15.3 %copy-start.7 = (f32[40,256]{1,0:T(8,128)}, f32[40,256]{1,0:T(8,128)S(1)}, u32[]{:S(2)}) copy-start(f32[40,256]{1,0:T(8,128)S(1)} %get-tuple-element.24.refs_1_.refs_3_) | copy-start | bytes 122884
  71.4 15.3 %copy-start.16 = (f32[40,128]{1,0:T(8,128)}, f32[40,128]{1,0:T(8,128)S(1)}, u32[]{:S(2)}) copy-start(f32[40,128]{1,0:T(8,128)S(1)} %get-tuple-element.23.refs_9_.refs_10_) | copy-start | bytes 61444
  73.6 24.4 %all-to-all-start.1 = ((f32[32,16,128]{2,1,0:T(8,128)}), f32[32,16,128]{2,1,0:T(8,128)S(1)}, u32[]{:S(2)}, u32[]{:S(2)}) async-start(f32[32,16,128]{2,1,0:T(8,128)} %shard_map.70), calls=%async_computation.1 | async-start | bytes 524288 | tf_op jit(solution)/shard_map/all_to_all | solution.py:461
  101.5 24.5 %copy-start.4 = (f32[256,128]{1,0:T(8,128)S(1)}, f32[256,128]{1,0:T(8,128)}, u32[]{:S(2)}) copy-start(f32[256,128]{1,0:T(8,128)} %copy-done.2) | copy-start | bytes 393220
  102.8 22.8 %all-to-all-start.2 = ((f32[256,2,128]{2,1,0:T(2,128)}), f32[256,2,128]{2,1,0:T(2,128)S(1)}, u32[]{:S(2)}, u32[]{:S(2)}) async-start(f32[256,2,128]{2,1,0:T(2,128)} %get-tuple-element.29), calls=%async_computation.2 | async-start | bytes 524288 | tf_op jit(solution)/shard_map/all_to_all | solution.py:461
  110.3 15.6 %collective-permute-start.18 = (f32[128,128]{1,0:T(8,128)S(1)}, f32[128,128]{1,0:T(8,128)S(1)}, u32[]{:S(2)}, u32[]{:S(2)}) collective-permute-start(f32[128,128]{1,0:T(8,128)S(1)} %get-tuple-element.32), channel_id=1, source_target_pairs={{8,0},{16,8},{24,16},{32,24},{40,32},{48,40},{56,48},{64,56},{72,6... | collective-permute-start | bytes 196616 | tf_op jit(solution)/shard_map/ppermute | solution.py:444
  115.5 3.0 %collective-permute-start.19 = (f32[24,128]{1,0:T(8,128)S(1)}, f32[24,128]{1,0:T(8,128)S(1)}, u32[]{:S(2)}, u32[]{:S(2)}) collective-permute-start(f32[24,128]{1,0:T(8,128)S(1)} %shard_map.73), channel_id=1, source_target_pairs={{0,1},{1,0},{2,3},{3,2},{4,5},{5,4},{6,7},{7,6},{8,9},{9,8},{10,11... | collective-permute-start | bytes 36872 | tf_op jit(solution)/shard_map/ppermute | solution.py:450
  118.6 7.3 %collective-permute-start.22 = (f32[24,128]{1,0:T(8,128)S(1)}, f32[24,128]{1,0:T(8,128)S(1)}, u32[]{:S(2)}, u32[]{:S(2)}) collective-permute-start(f32[24,128]{1,0:T(8,128)S(1)} %add.17.refs_0_), channel_id=1, source_target_pairs={{0,6},{2,0},{4,2},{6,4},{1,7},{3,1},{5,3},{7,5},{8,14},{10,8},{12,... | collective-permute-start | bytes 36872 | tf_op jit(solution)/shard_map/ppermute | solution.py:456
  119.4 6.5 %collective-permute-start.21 = (f32[24,128]{1,0:T(8,128)S(1)}, f32[24,128]{1,0:T(8,128)S(1)}, u32[]{:S(2)}, u32[]{:S(2)}) collective-permute-start(f32[24,128]{1,0:T(8,128)S(1)} %add.17.refs_0_), channel_id=1, source_target_pairs={{0,4},{2,6},{4,0},{6,2},{1,5},{3,7},{5,1},{7,3},{8,12},{10,14},{12... | collective-permute-start | bytes 36872 | tf_op jit(solution)/shard_map/ppermute | solution.py:456
  120.0 6.0 %collective-permute-start.20 = (f32[24,128]{1,0:T(8,128)S(1)}, f32[24,128]{1,0:T(8,128)S(1)}, u32[]{:S(2)}, u32[]{:S(2)}) collective-permute-start(f32[24,128]{1,0:T(8,128)S(1)} %add.17.refs_0_), channel_id=1, source_target_pairs={{0,2},{2,4},{4,6},{6,0},{1,3},{3,5},{5,7},{7,1},{8,10},{10,12},{12... | collective-permute-start | bytes 36872 | tf_op jit(solution)/shard_map/ppermute | solution.py:456
  (16 other events, 12.7 us)
